TPU v7x, 512 devices: a whole 4x8x8 slice. The times are simulated.
512 devices in a mesh: lon: 32 (over x, z_lo, core), lat: 8 (over y), lev: 2 (over z_hi).
Axes of the slice: x: 4, y: 8, z: 8 (z_hi: 2, z_lo: 4; z = z_hi * 4 + z_lo), core: 2. Of those that a mesh axis runs over, the one named last changes fastest.
Arguments:
- adjoint: float32 [4, 16, 256, 8192], P(None, 'lev', 'lat', 'lon'), may hold values from -6 to 6
- courant_lon: bfloat16 [16, 256, 8192], P('lev', 'lat', 'lon'), may hold values from -0.44921875 to 0.44921875
- courant_lat: bfloat16 [16, 256, 8192], P('lev', 'lat', 'lon'), may hold values from -0.44921875 to 0.44921875
- mixing: bfloat16 [16, 256, 8192], P('lev', 'lat', 'lon'), may hold values from 0.5 to 2000
- injection: float32 [4, 16], P(None, 'lev'), may hold values from 0.05 to 1
- prior_flux: bfloat16 [4, 256, 8192], P(None, 'lat', 'lon'), may hold values from 0.0049743652 to 0.049804688
- region_ids: int32 [256, 8192], P('lat', 'lon'), may hold values from 0 to 2047
Outputs:
- adjoint_out: float32 [4, 16, 256, 8192], P(None, 'lev', 'lat', 'lon')
- region_grad: float32 [2048, 24], P(('lon', 'lat', 'lev'))
All inputs are finite; a program needn't handle non-finite values.
Results may differ from a plain program's by a relative error of at most 0.0006.
Values sent between devices are 32-bit elements; how exact they have to be, the bound alone decides.
No kernel may reach another device: no remote copies, remote signals or barrier semaphores. Data moves between devices by JAX's collectives and lax.ppermute only.
A program may use at most 64 MiB of HBM per device.

v0:
```python
import jax
import jax.numpy as jnp
from jax import lax
from jax.sharding import PartitionSpec as P

REGIONS = 2048
STEPS = 6


def shifted(x, axis, by):
    count = lax.axis_size(axis)
    pairs = [(i, i + by) for i in range(count) if 0 <= i + by < count]
    return lax.ppermute(x, axis, pairs)


def extended(cells, sides, width, closed):
    for axis, dim in sides:
        count = lax.axis_size(axis)
        ends = count if closed else count - 1
        head = lax.slice_in_dim(cells, 0, width, axis=dim)
        tail = lax.slice_in_dim(cells, cells.shape[dim] - width, cells.shape[dim], axis=dim)
        cells = jnp.concatenate(
            [
                lax.ppermute(tail, axis, [(i, (i + 1) % count) for i in range(ends)]),
                cells,
                lax.ppermute(head, axis, [((i + 1) % count, i) for i in range(ends)]),
            ],
            axis=dim,
        )
    return cells


def send_upward(planes):
    return shifted(planes, "lev", 1)


def send_downward(planes):
    return shifted(planes, "lev", -1)


def pivot_table(kbelow, kabove, carried):
    inverse_list = []
    cprime_list = []
    for position in range(kabove.shape[0]):
        inverse = 1.0 / (1.0 + kabove[position] + kbelow[position] * (1.0 + carried))
        carried = -kabove[position] * inverse
        inverse_list.append(inverse)
        cprime_list.append(carried)
    return (jnp.stack(inverse_list), jnp.stack(cprime_list))


def eliminate(rhs_field, kbelow, inverse, carried):
    rows_out = []
    for position in range(rhs_field.shape[1]):
        carried = (rhs_field[:, position] + kbelow[position] * carried) * inverse[position]
        rows_out.append(carried)
    return jnp.stack(rows_out, axis=1)


def substitute(reduced, cprime, carried):
    level_count = reduced.shape[1]
    rows_out = [None] * level_count
    for position in reversed(range(level_count)):
        carried = reduced[:, position] - cprime[position] * carried
        rows_out[position] = carried
    return jnp.stack(rows_out, axis=1)


def advect(tracer_field, east_rate, west_rate, north_rate, south_rate):
    lon_ext = extended(tracer_field, (("lon", 3),), 1, True)
    lat_ext = extended(tracer_field, (("lat", 2),), 1, False)
    east_cells = lon_ext[:, :, :, 2:]
    west_cells = lon_ext[:, :, :, :-2]
    north_cells = lat_ext[:, :, 2:, :]
    south_cells = lat_ext[:, :, :-2, :]
    return (
        tracer_field
        + east_rate * (east_cells - tracer_field)
        + west_rate * (west_cells - tracer_field)
        + north_rate * (north_cells - tracer_field)
        + south_rate * (south_cells - tracer_field)
    )


def body(adjoint, courant_lon, courant_lat, mixing, injection, prior_flux, region_ids):
    levels_here = adjoint.shape[1]
    lev_index = lax.axis_index("lev")
    top_flag = lev_index == lax.axis_size("lev") - 1
    level_iota = lax.broadcasted_iota(jnp.int32, (levels_here, 1, 1), 0)
    last_level = level_iota == levels_here - 1
    mixing_f32 = mixing.astype(jnp.float32)
    kabove = jnp.where(last_level & top_flag, 0.0, mixing_f32)
    plane_zero = jnp.zeros_like(kabove[:1])
    tracer_zero = jnp.zeros_like(adjoint[:, 0])
    lon_wind = courant_lon.astype(jnp.float32)
    lat_wind = courant_lat.astype(jnp.float32)
    east_rate = jnp.maximum(lon_wind, 0.0)
    west_rate = jnp.maximum(-lon_wind, 0.0)
    north_rate = jnp.maximum(lat_wind, 0.0)
    south_rate = jnp.maximum(-lat_wind, 0.0)
    flux_weight = prior_flux.astype(jnp.float32)
    kbelow_inner = jnp.concatenate([plane_zero, kabove[:-1]], axis=0)
    inverse, cprime = pivot_table(kbelow_inner, kabove, plane_zero[0])
    received = send_upward(jnp.stack([kabove[-1], cprime[-1]]))
    kbelow = jnp.concatenate([received[:1], kabove[:-1]], axis=0)
    inverse, cprime = pivot_table(kbelow, kabove, received[1])
    current = adjoint
    weight_rows = []
    for step in range(STEPS):
        first_pass = eliminate(current, kbelow, inverse, tracer_zero)
        reduced = eliminate(current, kbelow, inverse, send_upward(first_pass[:, -1]))
        first_back = substitute(reduced, cprime, tracer_zero)
        solved = substitute(reduced, cprime, send_downward(first_back[:, 0]))
        weight_rows.append(
            flux_weight
            * jnp.einsum("tl,tlab->tab", injection, solved, precision=lax.Precision.HIGHEST)
        )
        current = advect(solved, east_rate, west_rate, north_rate, south_rate)
    weights = jnp.concatenate(weight_rows, axis=0).reshape(len(weight_rows) * adjoint.shape[0], -1)
    flat_ids = region_ids.reshape(-1)
    share = REGIONS // (lax.axis_size("lon") * lax.axis_size("lat") * lax.axis_size("lev"))
    block_size = min(256, share * lax.axis_size(("lon", "lat", "lev")))
    block_count = -(-(share * lax.axis_size(("lon", "lat", "lev"))) // block_size)

    def one_block(block_index):
        wanted = block_index * block_size + lax.iota(jnp.int32, block_size)
        onehot = (flat_ids[None, :] == wanted[:, None]).astype(jnp.float32)
        return lax.dot_general(
            onehot,
            weights,
            (((1,), (1,)), ((), ())),
            precision=lax.Precision.HIGH,
            preferred_element_type=jnp.float32,
        )

    blocks = lax.map(one_block, jnp.arange(block_count, dtype=jnp.int32))
    region_grad = lax.psum_scatter(
        blocks.reshape(block_count * block_size, weights.shape[0]),
        ("lon", "lat", "lev"),
        scatter_dimension=0,
        tiled=True,
    )
    return (current, region_grad)


def solution(mesh):
    placed = (
        P(None, "lev", "lat", "lon"),
        P("lev", "lat", "lon"),
        P("lev", "lat", "lon"),
        P("lev", "lat", "lon"),
        P(None, "lev"),
        P(None, "lat", "lon"),
        P("lat", "lon"),
    )
    return jax.shard_map(
        body,
        mesh=mesh,
        in_specs=placed,
        out_specs=(P(None, "lev", "lat", "lon"), P(("lon", "lat", "lev"), None)),
        check_vma=False,
    )
```

profile of v0, /device:TPU:1, one launch (start us, length us, event | category | flops | bytes accessed | tf_op | source)
XLA Modules:
  0.0 570.9 jit_solution(6564354485841182679)
XLA Ops:
  8.5 11.5 %collective-permute-start = (f32[2,32,256]{2,1,0:T(8,128)S(1)}, f32[2,32,256]{2,1,0:T(8,128)S(1)}, u32[]{:S(2)}, u32[]{:S(2)}) collective-permute-start(f32[2,32,256]{2,1,0:T(8,128)S(1)} %pad_maximum_fusion.24), channel_id=1, source_target_pairs={{0,1},{2,3},{4,5},{6,7},{8,9},{10,11},{12,13},{14,15},{16,17},{18,... | collective-permute-start | bytes 196616 | tf_op jit(solution)/shard_map/ppermute | solution.py:13
  21.7 7.7 %collective-permute-start.1 = (f32[4,32,256]{2,1,0:T(8,128)S(1)}, f32[4,32,256]{2,1,0:T(8,128)S(1)}, u32[]{:S(2)}, u32[]{:S(2)}) collective-permute-start(f32[4,32,256]{2,1,0:T(8,128)S(1)} %fusion.120), channel_id=1, source_target_pairs={{0,1},{2,3},{4,5},{6,7},{8,9},{10,11},{12,13},{14,15},{16,17},{18,... | collective-permute-start | bytes 393224 | tf_op jit(solution)/shard_map/ppermute | solution.py:13
  32.8 10.4 %collective-permute-done.2 = f32[4,32,256]{2,1,0:T(8,128)S(1)} collective-permute-done((f32[4,32,256]{2,1,0:T(8,128)S(1)}, f32[4,32,256]{2,1,0:T(8,128)S(1)}, u32[]{:S(2)}, u32[]{:S(2)}) %collective-permute-start.2) | collective-permute-done | bytes 131104 | tf_op jit(solution)/shard_map/ppermute | solution.py:13
  47.7 6.1 %collective-permute-start.4 = (f32[4,8,32,1]{3,2,0,1:T(8,128)S(1)}, f32[4,8,32,1]{3,2,0,1:T(8,128)S(1)}, u32[]{:S(2)}, u32[]{:S(2)}) collective-permute-start(f32[4,8,32,1]{3,2,0,1:T(8,128)S(1)} %get-tuple-element.137), channel_id=1, source_target_pairs={{0,16},{16,32},{32,48},{48,64},{64,80},{80,96},{96,112},{112,128},... | collective-permute-start | bytes 12296 | tf_op jit(solution)/shard_map/ppermute | solution.py:24
  55.0 4.0 collective-permute-start.6
  68.9 8.3 %collective-permute-done.8 = f32[4,32,256]{2,1,0:T(8,128)S(1)} collective-permute-done((f32[4,32,256]{2,1,0:T(8,128)S(1)}, f32[4,32,256]{2,1,0:T(8,128)S(1)}, u32[]{:S(2)}, u32[]{:S(2)}) %collective-permute-start.8) | collective-permute-done | bytes 131104 | tf_op jit(solution)/shard_map/ppermute | solution.py:13
  78.9 4.0 collective-permute-start.12
  83.1 9.9 %collective-permute-start.10 = (f32[4,8,32,1]{3,2,0,1:T(8,128)S(1)}, f32[4,8,32,1]{3,2,0,1:T(8,128)S(1)}, u32[]{:S(2)}, u32[]{:S(2)}) collective-permute-start(f32[4,8,32,1]{3,2,0,1:T(8,128)S(1)} %get-tuple-element.133), channel_id=1, source_target_pairs={{0,16},{16,32},{32,48},{48,64},{64,80},{80,96},{96,112},{112,128},... | collective-permute-start | bytes 12296 | tf_op jit(solution)/shard_map/ppermute | solution.py:24
  94.9 4.2 collective-permute-done.10
  99.1 9.0 %collective-permute-done.9 = f32[4,8,32,1]{3,2,0,1:T(8,128)S(1)} collective-permute-done((f32[4,8,32,1]{3,2,0,1:T(8,128)S(1)}, f32[4,8,32,1]{3,2,0,1:T(8,128)S(1)}, u32[]{:S(2)}, u32[]{:S(2)}) %collective-permute-start.9) | collective-permute-done | bytes 4128 | tf_op jit(solution)/shard_map/ppermute | solution.py:26
  117.8 6.7 %collective-permute-done.14 = f32[4,32,256]{2,1,0:T(8,128)S(1)} collective-permute-done((f32[4,32,256]{2,1,0:T(8,128)S(1)}, f32[4,32,256]{2,1,0:T(8,128)S(1)}, u32[]{:S(2)}, u32[]{:S(2)}) %collective-permute-start.14) | collective-permute-done | bytes 131104 | tf_op jit(solution)/shard_map/ppermute | solution.py:13
  125.2 5.1 collective-permute-start.15
  139.1 5.4 collective-permute-done.15
  150.7 8.3 %collective-permute-done.20 = f32[4,32,256]{2,1,0:T(8,128)S(1)} collective-permute-done((f32[4,32,256]{2,1,0:T(8,128)S(1)}, f32[4,32,256]{2,1,0:T(8,128)S(1)}, u32[]{:S(2)}, u32[]{:S(2)}) %collective-permute-start.20) | collective-permute-done | bytes 131104 | tf_op jit(solution)/shard_map/ppermute | solution.py:13
  159.6 5.6 collective-permute-start.21
  175.3 5.3 collective-permute-done.21
  188.5 6.8 %collective-permute-done.26 = f32[4,32,256]{2,1,0:T(8,128)S(1)} collective-permute-done((f32[4,32,256]{2,1,0:T(8,128)S(1)}, f32[4,32,256]{2,1,0:T(8,128)S(1)}, u32[]{:S(2)}, u32[]{:S(2)}) %collective-permute-start.26) | collective-permute-done | bytes 131104 | tf_op jit(solution)/shard_map/ppermute | solution.py:13
  195.9 4.3 collective-permute-start.27
  200.2 5.9 %collective-permute-start.28 = (f32[4,8,32,1]{3,2,0,1:T(8,128)S(1)}, f32[4,8,32,1]{3,2,0,1:T(8,128)S(1)}, u32[]{:S(2)}, u32[]{:S(2)}) collective-permute-start(f32[4,8,32,1]{3,2,0,1:T(8,128)S(1)} %get-tuple-element.120), channel_id=1, source_target_pairs={{0,16},{16,32},{32,48},{48,64},{64,80},{80,96},{96,112},{112,128},... | collective-permute-start | bytes 12296 | tf_op jit(solution)/shard_map/ppermute | solution.py:24
  211.5 4.8 collective-permute-done.27
  223.7 8.7 %collective-permute-done.32 = f32[4,32,256]{2,1,0:T(8,128)S(1)} collective-permute-done((f32[4,32,256]{2,1,0:T(8,128)S(1)}, f32[4,32,256]{2,1,0:T(8,128)S(1)}, u32[]{:S(2)}, u32[]{:S(2)}) %collective-permute-start.32) | collective-permute-done | bytes 131104 | tf_op jit(solution)/shard_map/ppermute | solution.py:13
  241.4 5.2 collective-permute-start.34
  251.9 38.2 %while.10 = (s32[]{:T(128)}, f32[8,256,24]{1,2,0:T(8,128)S(1)}, s32[32,256]{1,0:T(8,128)S(1)}, s32[8]{0:T(128)S(1)}, f32[24,8192]{1,0:T(8,128)}, /*index=5*/s32[]{:T(128)}, s32[1]{0:T(128)}) while((s32[]{:T(128)}, f32[8,256,24]{1,2,0:T(8,128)S(1)}, s32[32,256]{1,0:T(8,128)S(1)}, s32[8]{0:T(128)S(1)}, f32[24,8192]{1,0:T(8,128)}, ...), condition=%wide.region_1.2_spmd, body=%wide.region_0.1_spmd.sunk | while | flops 304087296 | bytes 911469 | solution.py:136
  294.6 268.2 %all-reduce.3.cloned.1.call-done = f32[2048,24]{1,0:T(8,128)} async-done(((f32[2048,24]{1,0:T(8,128)}), f32[2048,24]{1,0:T(8,128)}) %all-reduce.3.cloned.1.call-update) | async-done | bytes 196624
  (270 shorter events, 134.9 us)
Async XLA Ops:
  7.2 555.7 %all-reduce.3.cloned.1.call-start = ((), (), s32[]{:S(2)}) async-start(), calls=%async_computation | async-start | bytes 2097152
  8.5 12.8 %collective-permute-start = (f32[2,32,256]{2,1,0:T(8,128)S(1)}, f32[2,32,256]{2,1,0:T(8,128)S(1)}, u32[]{:S(2)}, u32[]{:S(2)}) collective-permute-start(f32[2,32,256]{2,1,0:T(8,128)S(1)} %pad_maximum_fusion.24), channel_id=1, source_target_pairs={{0,1},{2,3},{4,5},{6,7},{8,9},{10,11},{12,13},{14,15},{16,17},{18,... | collective-permute-start | bytes 196616 | tf_op jit(solution)/shard_map/ppermute | solution.py:13
  31.5 11.7 %collective-permute-start.2 = (f32[4,32,256]{2,1,0:T(8,128)S(1)}, f32[4,32,256]{2,1,0:T(8,128)S(1)}, u32[]{:S(2)}, u32[]{:S(2)}) collective-permute-start(f32[4,32,256]{2,1,0:T(8,128)S(1)} %get-tuple-element.95), channel_id=1, source_target_pairs={{1,0},{3,2},{5,4},{7,6},{9,8},{11,10},{13,12},{15,14},{17,16},{19,... | collective-permute-start | bytes 393224 | tf_op jit(solution)/shard_map/ppermute | solution.py:13
  43.8 19.2 %collective-permute-start.3 = (f32[4,8,32,1]{3,2,0,1:T(8,128)S(1)}, f32[4,8,32,1]{3,2,0,1:T(8,128)S(1)}, u32[]{:S(2)}, u32[]{:S(2)}) collective-permute-start(f32[4,8,32,1]{3,2,0,1:T(8,128)S(1)} %get-tuple-element.136), channel_id=1, source_target_pairs={{16,0},{32,16},{48,32},{64,48},{80,64},{96,80},{112,96},{128,112},... | collective-permute-start | bytes 12296 | tf_op jit(solution)/shard_map/ppermute | solution.py:26
  47.7 15.4 %collective-permute-start.4 = (f32[4,8,32,1]{3,2,0,1:T(8,128)S(1)}, f32[4,8,32,1]{3,2,0,1:T(8,128)S(1)}, u32[]{:S(2)}, u32[]{:S(2)}) collective-permute-start(f32[4,8,32,1]{3,2,0,1:T(8,128)S(1)} %get-tuple-element.137), channel_id=1, source_target_pairs={{0,16},{16,32},{32,48},{48,64},{64,80},{80,96},{96,112},{112,128},... | collective-permute-start | bytes 12296 | tf_op jit(solution)/shard_map/ppermute | solution.py:24
  77.6 30.5 %collective-permute-start.11 = (f32[4,8,1,256]{3,2,0,1:T(1,128)S(1)}, f32[4,8,1,256]{3,2,0,1:T(1,128)S(1)}, u32[]{:S(2)}, u32[]{:S(2)}) collective-permute-start(f32[4,8,1,256]{3,2,0,1:T(1,128)S(1)} %get-tuple-element.134), channel_id=1, source_target_pairs={{2,0},{4,2},{6,4},{8,6},{10,8},{12,10},{14,12},{3,1},{5,3},{7,5},{... | collective-permute-start | bytes 98312 | tf_op jit(solution)/shard_map/ppermute | solution.py:26
  78.9 29.2 %collective-permute-start.12 = (f32[4,8,1,256]{3,2,0,1:T(1,128)S(1)}, f32[4,8,1,256]{3,2,0,1:T(1,128)S(1)}, u32[]{:S(2)}, u32[]{:S(2)}) collective-permute-start(f32[4,8,1,256]{3,2,0,1:T(1,128)S(1)} %get-tuple-element.135), channel_id=1, source_target_pairs={{0,2},{2,4},{4,6},{6,8},{8,10},{10,12},{12,14},{1,3},{3,5},{5,7},{... | collective-permute-start | bytes 98312 | tf_op jit(solution)/shard_map/ppermute | solution.py:24
  83.1 16.0 %collective-permute-start.10 = (f32[4,8,32,1]{3,2,0,1:T(8,128)S(1)}, f32[4,8,32,1]{3,2,0,1:T(8,128)S(1)}, u32[]{:S(2)}, u32[]{:S(2)}) collective-permute-start(f32[4,8,32,1]{3,2,0,1:T(8,128)S(1)} %get-tuple-element.133), channel_id=1, source_target_pairs={{0,16},{16,32},{32,48},{48,64},{64,80},{80,96},{96,112},{112,128},... | collective-permute-start | bytes 12296 | tf_op jit(solution)/shard_map/ppermute | solution.py:24
  93.0 15.1 %collective-permute-start.9 = (f32[4,8,32,1]{3,2,0,1:T(8,128)S(1)}, f32[4,8,32,1]{3,2,0,1:T(8,128)S(1)}, u32[]{:S(2)}, u32[]{:S(2)}) collective-permute-start(f32[4,8,32,1]{3,2,0,1:T(8,128)S(1)} %get-tuple-element.132), channel_id=1, source_target_pairs={{16,0},{32,16},{48,32},{64,48},{80,64},{96,80},{112,96},{128,112},... | collective-permute-start | bytes 12296 | tf_op jit(solution)/shard_map/ppermute | solution.py:26
  125.2 19.4 %collective-permute-start.15 = (f32[4,8,32,1]{3,2,0,1:T(8,128)S(1)}, f32[4,8,32,1]{3,2,0,1:T(8,128)S(1)}, u32[]{:S(2)}, u32[]{:S(2)}) collective-permute-start(f32[4,8,32,1]{3,2,0,1:T(8,128)S(1)} %get-tuple-element.128), channel_id=1, source_target_pairs={{16,0},{32,16},{48,32},{64,48},{80,64},{96,80},{112,96},{128,112},... | collective-permute-start | bytes 12296 | tf_op jit(solution)/shard_map/ppermute | solution.py:26
  130.2 14.3 %collective-permute-start.16 = (f32[4,8,32,1]{3,2,0,1:T(8,128)S(1)}, f32[4,8,32,1]{3,2,0,1:T(8,128)S(1)}, u32[]{:S(2)}, u32[]{:S(2)}) collective-permute-start(f32[4,8,32,1]{3,2,0,1:T(8,128)S(1)} %get-tuple-element.129), channel_id=1, source_target_pairs={{0,16},{16,32},{32,48},{48,64},{64,80},{80,96},{96,112},{112,128},... | collective-permute-start | bytes 12296 | tf_op jit(solution)/shard_map/ppermute | solution.py:24
  133.7 10.8 %collective-permute-start.17 = (f32[4,8,1,256]{3,2,0,1:T(1,128)S(1)}, f32[4,8,1,256]{3,2,0,1:T(1,128)S(1)}, u32[]{:S(2)}, u32[]{:S(2)}) collective-permute-start(f32[4,8,1,256]{3,2,0,1:T(1,128)S(1)} %get-tuple-element.130), channel_id=1, source_target_pairs={{2,0},{4,2},{6,4},{8,6},{10,8},{12,10},{14,12},{3,1},{5,3},{7,5},{... | collective-permute-start | bytes 98312 | tf_op jit(solution)/shard_map/ppermute | solution.py:26
  159.6 21.1 %collective-permute-start.21 = (f32[4,8,32,1]{3,2,0,1:T(8,128)S(1)}, f32[4,8,32,1]{3,2,0,1:T(8,128)S(1)}, u32[]{:S(2)}, u32[]{:S(2)}) collective-permute-start(f32[4,8,32,1]{3,2,0,1:T(8,128)S(1)} %get-tuple-element.124), channel_id=1, source_target_pairs={{16,0},{32,16},{48,32},{64,48},{80,64},{96,80},{112,96},{128,112},... | collective-permute-start | bytes 12296 | tf_op jit(solution)/shard_map/ppermute | solution.py:26
  165.2 15.5 %collective-permute-start.22 = (f32[4,8,32,1]{3,2,0,1:T(8,128)S(1)}, f32[4,8,32,1]{3,2,0,1:T(8,128)S(1)}, u32[]{:S(2)}, u32[]{:S(2)}) collective-permute-start(f32[4,8,32,1]{3,2,0,1:T(8,128)S(1)} %get-tuple-element.125), channel_id=1, source_target_pairs={{0,16},{16,32},{32,48},{48,64},{64,80},{80,96},{96,112},{112,128},... | collective-permute-start | bytes 12296 | tf_op jit(solution)/shard_map/ppermute | solution.py:24
  168.4 12.2 %collective-permute-start.23 = (f32[4,8,1,256]{3,2,0,1:T(1,128)S(1)}, f32[4,8,1,256]{3,2,0,1:T(1,128)S(1)}, u32[]{:S(2)}, u32[]{:S(2)}) collective-permute-start(f32[4,8,1,256]{3,2,0,1:T(1,128)S(1)} %get-tuple-element.126), channel_id=1, source_target_pairs={{2,0},{4,2},{6,4},{8,6},{10,8},{12,10},{14,12},{3,1},{5,3},{7,5},{... | collective-permute-start | bytes 98312 | tf_op jit(solution)/shard_map/ppermute | solution.py:26
  169.7 10.9 %collective-permute-start.24 = (f32[4,8,1,256]{3,2,0,1:T(1,128)S(1)}, f32[4,8,1,256]{3,2,0,1:T(1,128)S(1)}, u32[]{:S(2)}, u32[]{:S(2)}) collective-permute-start(f32[4,8,1,256]{3,2,0,1:T(1,128)S(1)} %get-tuple-element.127), channel_id=1, source_target_pairs={{0,2},{2,4},{4,6},{6,8},{8,10},{10,12},{12,14},{1,3},{3,5},{5,7},{... | collective-permute-start | bytes 98312 | tf_op jit(solution)/shard_map/ppermute | solution.py:24
  195.9 20.3 %collective-permute-start.27 = (f32[4,8,32,1]{3,2,0,1:T(8,128)S(1)}, f32[4,8,32,1]{3,2,0,1:T(8,128)S(1)}, u32[]{:S(2)}, u32[]{:S(2)}) collective-permute-start(f32[4,8,32,1]{3,2,0,1:T(8,128)S(1)} %get-tuple-element.121), channel_id=1, source_target_pairs={{16,0},{32,16},{48,32},{64,48},{80,64},{96,80},{112,96},{128,112},... | collective-permute-start | bytes 12296 | tf_op jit(solution)/shard_map/ppermute | solution.py:26
  200.2 16.0 %collective-permute-start.28 = (f32[4,8,32,1]{3,2,0,1:T(8,128)S(1)}, f32[4,8,32,1]{3,2,0,1:T(8,128)S(1)}, u32[]{:S(2)}, u32[]{:S(2)}) collective-permute-start(f32[4,8,32,1]{3,2,0,1:T(8,128)S(1)} %get-tuple-element.120), channel_id=1, source_target_pairs={{0,16},{16,32},{32,48},{48,64},{64,80},{80,96},{96,112},{112,128},... | collective-permute-start | bytes 12296 | tf_op jit(solution)/shard_map/ppermute | solution.py:24
  206.2 10.1 %collective-permute-start.29 = (f32[4,8,1,256]{3,2,0,1:T(1,128)S(1)}, f32[4,8,1,256]{3,2,0,1:T(1,128)S(1)}, u32[]{:S(2)}, u32[]{:S(2)}) collective-permute-start(f32[4,8,1,256]{3,2,0,1:T(1,128)S(1)} %get-tuple-element.122), channel_id=1, source_target_pairs={{2,0},{4,2},{6,4},{8,6},{10,8},{12,10},{14,12},{3,1},{5,3},{7,5},{... | collective-permute-start | bytes 98312 | tf_op jit(solution)/shard_map/ppermute | solution.py:26
  222.1 10.2 %collective-permute-start.32 = (f32[4,32,256]{2,1,0:T(8,128)S(1)}, f32[4,32,256]{2,1,0:T(8,128)S(1)}, u32[]{:S(2)}, u32[]{:S(2)}) collective-permute-start(f32[4,32,256]{2,1,0:T(8,128)S(1)} %get-tuple-element.45), channel_id=1, source_target_pairs={{1,0},{3,2},{5,4},{7,6},{9,8},{11,10},{13,12},{15,14},{17,16},{19,... | collective-permute-start | bytes 393224 | tf_op jit(solution)/shard_map/ppermute | solution.py:13
  237.7 53.8 %collective-permute-start.33 = (f32[4,8,32,1]{3,2,0,1:T(8,128)}, f32[4,8,32,1]{3,2,0,1:T(8,128)}, u32[]{:S(2)}, u32[]{:S(2)}) collective-permute-start(f32[4,8,32,1]{3,2,0,1:T(8,128)} %slice.698), channel_id=1, source_target_pairs={{16,0},{32,16},{48,32},{64,48},{80,64},{96,80},{112,96},{128,112},... | collective-permute-start | bytes 12296 | tf_op jit(solution)/shard_map/ppermute | solution.py:26
  241.4 50.2 %collective-permute-start.34 = (f32[4,8,32,1]{3,2,1,0:T(8,128)}, f32[4,8,32,1]{3,2,1,0:T(8,128)}, u32[]{:S(2)}, u32[]{:S(2)}) collective-permute-start(f32[4,8,32,1]{3,2,1,0:T(8,128)} %slice.699), channel_id=1, source_target_pairs={{0,16},{16,32},{32,48},{48,64},{64,80},{80,96},{96,112},{112,128},... | collective-permute-start | bytes 12296 | tf_op jit(solution)/shard_map/ppermute | solution.py:24
  246.6 44.9 %collective-permute-start.35 = (f32[4,8,1,256]{3,2,1,0:T(1,128)S(1)}, f32[4,8,1,256]{3,2,1,0:T(1,128)S(1)}, u32[]{:S(2)}, u32[]{:S(2)}) collective-permute-start(f32[4,8,1,256]{3,2,1,0:T(1,128)S(1)} %get-tuple-element.114), channel_id=1, source_target_pairs={{2,0},{4,2},{6,4},{8,6},{10,8},{12,10},{14,12},{3,1},{5,3},{7,5},{... | collective-permute-start | bytes 98312 | tf_op jit(solution)/shard_map/ppermute | solution.py:26
  247.9 43.7 %collective-permute-start.36 = (f32[4,8,1,256]{3,2,1,0:T(1,128)S(1)}, f32[4,8,1,256]{3,2,1,0:T(1,128)S(1)}, u32[]{:S(2)}, u32[]{:S(2)}) collective-permute-start(f32[4,8,1,256]{3,2,1,0:T(1,128)S(1)} %get-tuple-element.115), channel_id=1, source_target_pairs={{0,2},{2,4},{4,6},{6,8},{8,10},{10,12},{12,14},{1,3},{3,5},{5,7},{... | collective-permute-start | bytes 98312 | tf_op jit(solution)/shard_map/ppermute | solution.py:24
  (51 other events, 1427.7 us)
Sparse Core Ops, SparseCore 0:
  291.6 271.1 all-reduce.2
where the time goes:
time: 573 us; the launch traced here: 571 us
  waiting for transfers between devices  361 us (63%)
  starting transfers between devices  124 us (22%)
  matrix products  37.3 us (7%)
  between operations  15.5 us (3%)
  other arithmetic  14.9 us (3%)
  local copies, waits for them, and re-layouts  13 us (2%)
    unnamed x2, waiting for transfers between devices  268 us
    ppermute x13, waiting for transfers between devices, shifted(): return lax.ppermute(x, axis, pairs)  59.8 us
    ppermute x12, starting transfers between devices, extended(): lax.ppermute(tail, axis, [(i, (i + 1) % count) for i in range(ends)])  57.7 us
    ppermute x13, starting transfers between devices, shifted(): return lax.ppermute(x, axis, pairs)  34.6 us
    ppermute x12, starting transfers between devices, extended(): lax.ppermute(head, axis, [((i + 1) % count, i) for i in range(ends)])  32 us
    ppermute x12, waiting for transfers between devices, extended(): lax.ppermute(head, axis, [((i + 1) % count, i) for i in range(ends)])  28.4 us
    dot_general x8, matrix products, one_block(): lax.dot_general(onehot, weights, (((1,), (1,)), ((), ())), precision=lax....  27.7 us
  transfers between devices with their start and end apart: 38, of which 20 were waited for; matrix products, arithmetic and copies ran while one was open for 8% of the time, Pallas kernels for 0%

commit v1 on v0

v1 whole, which is shorter than its diff:
```python
import jax
import jax.numpy as jnp
from jax import lax
from jax.experimental import pallas as pl
from jax.experimental.pallas import tpu as pltpu
from jax.sharding import PartitionSpec as P

STEPS = 6
TRACERS = 4
FIELDS = TRACERS + 3
HERE = 8
LEVELS = 16
ROWS = 32
HALF = 128
EDGE = 8
TALL = ROWS + 2 * EDGE
WIDE = 2 * HALF
MAIN = FIELDS * HERE
STRIP = 2 * MAIN + 2 * FIELDS
HI = 256
LO = 8
SLOT = 32

VMEM = pl.BlockSpec(memory_space=pltpu.VMEM)
SMEM = pl.BlockSpec(memory_space=pltpu.SMEM)
PARAMS = pltpu.CompilerParams(vmem_limit_bytes=56 * 1024 * 1024)


def call(kernel, out_shape, operands, scalars, scratch=()):
    specs = [SMEM] * scalars + [VMEM] * (len(operands) - scalars)
    many = isinstance(out_shape, (tuple, list))
    return pl.pallas_call(
        kernel,
        out_shape=out_shape,
        in_specs=specs,
        out_specs=tuple(VMEM for _ in out_shape) if many else VMEM,
        scratch_shapes=list(scratch),
        compiler_params=PARAMS,
        name=kernel.__name__,
    )(*operands)


def f32(*shape):
    return jax.ShapeDtypeStruct(shape, jnp.float32)


def half_at(which):
    return pl.ds(pl.multiple_of(which * HALF, HALF), HALF)


def own_plane(refs, field, level, rows, lanes):
    adjoint, lon_wind, lat_wind, mixing = refs
    if field < TRACERS:
        return adjoint[field, level, rows, lanes]
    ref = (lon_wind, lat_wind, mixing)[field - TRACERS]
    return ref[level, rows, lanes].astype(jnp.float32)


def pack(side, injection, adjoint, lon_wind, lat_wind, mixing, to_partner, edge_mine, edge_other):
    refs = (adjoint, lon_wind, lat_wind, mixing)
    k = side[0]
    mine = half_at(k)
    other = half_at(1 - k)
    rows = slice(0, ROWS)
    slot = lax.broadcasted_iota(jnp.int32, (ROWS, HALF), 1) // (2 * EDGE)
    for field in range(FIELDS):
        packed_mine = jnp.zeros((ROWS, HALF), jnp.float32)
        packed_other = jnp.zeros((ROWS, HALF), jnp.float32)
        for level in range(HERE):
            shift = (2 * EDGE * level + EDGE) % HALF
            plane_mine = own_plane(refs, field, level, rows, mine)
            plane_other = own_plane(refs, field, level, rows, other)
            to_partner[field * HERE + level] = plane_other
            packed_mine = jnp.where(slot == level, pltpu.roll(plane_mine, shift, 1), packed_mine)
            packed_other = jnp.where(slot == level, pltpu.roll(plane_other, shift, 1), packed_other)
        to_partner[MAIN + field] = packed_mine
        edge_mine[field] = packed_mine
        edge_other[field] = packed_other
    for tracer in range(TRACERS):
        for level in range(HERE):
            row = tracer * HERE + level
            to_partner[MAIN + FIELDS, row : row + 1, :] = jnp.full((1, HALF), injection[tracer, level], jnp.float32)


def strips(side, adjoint, lon_wind, lat_wind, mixing, partner, edge_other, lon_same, lon_cross, first, last, edges):
    refs = (adjoint, lon_wind, lat_wind, mixing)
    k = side[0]
    mine = half_at(k)
    head = slice(0, EDGE)
    tail = slice(ROWS - EDGE, ROWS)
    for field in range(FIELDS):
        for level in range(HERE):
            at = field * HERE + level
            if field < TRACERS:
                first[at] = adjoint[field, level, head, mine]
                last[at] = adjoint[field, level, tail, mine]
            else:
                plane = own_plane(refs, field, level, slice(0, ROWS), mine)
                first[at] = plane[head]
                last[at] = plane[tail]
    first[MAIN : 2 * MAIN] = partner[0:MAIN, head, :]
    last[MAIN : 2 * MAIN] = partner[0:MAIN, tail, :]
    lane = lax.broadcasted_iota(jnp.int32, (ROWS, HALF), 1)
    inner = ((lane // EDGE) % 2) != k
    for field in range(FIELDS):
        for group, near, far in ((0, edge_other[field], lon_same[field]), (1, partner[MAIN + field], lon_cross[field])):
            merged = jnp.where(inner, near, far)
            at = group * FIELDS + field
            edges[at] = merged
            first[2 * MAIN + at] = merged[head]
            last[2 * MAIN + at] = merged[tail]


def steps(
    side, injection, adjoint, lon_wind, lat_wind, mixing, partner, edges, below, above, prior,
    kept, returned, weights,
    field_ref, lon_ref, lat_ref, kab_ref, inv_ref, cp_ref, red_ref, inj_ref,
):
    refs = (adjoint, lon_wind, lat_wind, mixing)
    k = side[0]
    mine = half_at(k)
    rows = slice(0, ROWS)
    low = slice(0, EDGE)
    mid = slice(EDGE, EDGE + ROWS)
    top = slice(EDGE + ROWS, TALL)
    main = slice(0, HALF)
    wing = slice(HALF, WIDE)

    for group in range(2):
        base = (k if group == 0 else 1 - k) * HERE
        for level in range(HERE):
            shift = (HALF - (2 * EDGE * level + EDGE)) % HALF
            for field in range(FIELDS):
                at = field * HERE + level
                plane_at = group * MAIN + at
                edge_at = group * FIELDS + field
                where = base + level
                if field < TRACERS:
                    target = field_ref.at[field, where]
                else:
                    target = (lon_ref, lat_ref, kab_ref)[field - TRACERS].at[where]
                target[low, main] = below[plane_at]
                target[top, main] = above[plane_at]
                if group == 0:
                    target[mid, main] = own_plane(refs, field, level, rows, mine)
                else:
                    target[mid, main] = partner[at]
                target[low, wing] = pltpu.roll(below[2 * MAIN + edge_at], shift, 1)
                target[mid, wing] = pltpu.roll(edges[edge_at], shift, 1)
                target[top, wing] = pltpu.roll(above[2 * MAIN + edge_at], shift, 1)
    for tracer in range(TRACERS):
        for level in range(HERE):
            row = tracer * HERE + level
            inj_ref[tracer, pl.ds(k * HERE + level, 1)] = jnp.full((1, 8, HALF), injection[tracer, level], jnp.float32)
            inj_ref[tracer, pl.ds((1 - k) * HERE + level, 1)] = jnp.broadcast_to(
                partner[MAIN + FIELDS, row : row + 1, :][None], (1, 8, HALF)
            )
    kab_ref[LEVELS - 1] = jnp.zeros((TALL, WIDE), jnp.float32)

    def pivots(tile, _):
        at = pl.ds(pl.multiple_of(tile * 8, 8), 8)
        carried = jnp.zeros((8, WIDE), jnp.float32)
        kbelow = jnp.zeros((8, WIDE), jnp.float32)
        for level in range(LEVELS):
            kabove = kab_ref[level, at, :]
            inverse = 1.0 / (1.0 + kabove + kbelow * (1.0 + carried))
            carried = -kabove * inverse
            inv_ref[level, at, :] = inverse
            cp_ref[level, at, :] = carried
            kbelow = kabove
        return 0

    lax.fori_loop(0, TALL // 8, pivots, 0)

    def one_step(step, _):
        def solve(tile, _):
            at = pl.ds(pl.multiple_of(tile * 8, 8), 8)
            carried = [jnp.zeros((8, WIDE), jnp.float32) for _ in range(TRACERS)]
            for level in range(LEVELS):
                inverse = inv_ref[level, at, :]
                if level:
                    kbelow = kab_ref[level - 1, at, :]
                for tracer in range(TRACERS):
                    rhs = field_ref[tracer, level, at, :]
                    if level:
                        rhs = rhs + kbelow * carried[tracer]
                    carried[tracer] = rhs * inverse
                    red_ref[tracer, level] = carried[tracer]
            for tracer in range(TRACERS):
                field_ref[tracer, LEVELS - 1, at, :] = carried[tracer]
            for level in reversed(range(LEVELS - 1)):
                cprime = cp_ref[level, at, :]
                for tracer in range(TRACERS):
                    carried[tracer] = red_ref[tracer, level] - cprime * carried[tracer]
                    field_ref[tracer, level, at, :] = carried[tracer]
            return 0

        lax.fori_loop(0, TALL // 8, solve, 0)

        def weigh(tile, _):
            at = pl.ds(pl.multiple_of(tile * 8 + EDGE, 8), 8)
            to = pl.ds(pl.multiple_of(tile * 8, 8), 8)
            for tracer in range(TRACERS):
                total = jnp.zeros((8, HALF), jnp.float32)
                for level in range(LEVELS):
                    total = total + inj_ref[tracer, level] * field_ref[tracer, level, at, main]
                weights[step * TRACERS + tracer, to, :] = total
            return 0

        lax.fori_loop(0, ROWS // 8, weigh, 0)

        def advect(level, _):
            lon = lon_ref[level]
            lat = lat_ref[level]
            east = lon > 0.0
            north = lat > 0.0
            lon = jnp.abs(lon)
            lat = jnp.abs(lat)
            centre = 1.0 - lon - lat
            for tracer in range(TRACERS):
                cells = field_ref[tracer, level]
                along = jnp.where(east, pltpu.roll(cells, WIDE - 1, 1), pltpu.roll(cells, 1, 1))
                across = jnp.where(north, pltpu.roll(cells, TALL - 1, 0), pltpu.roll(cells, 1, 0))
                field_ref[tracer, level] = centre * cells + lon * along + lat * across
            return 0

        lax.fori_loop(0, LEVELS, advect, 0)
        return 0

    lax.fori_loop(0, STEPS, one_step, 0)

    for tracer in range(TRACERS):
        flux = prior[tracer, :, mine].astype(jnp.float32)
        for step in range(STEPS):
            weights[step * TRACERS + tracer] = weights[step * TRACERS + tracer] * flux
        for level in range(HERE):
            kept[tracer, level] = field_ref[tracer, k * HERE + level, mid, main]
            returned[tracer, level] = field_ref[tracer, (1 - k) * HERE + level, mid, main]


def regions(side, weights, ids, sums, onehot, coarse, fine):
    mine = half_at(side[0])
    count = STEPS * TRACERS
    which = lax.broadcasted_iota(jnp.int32, (HI, HALF), 0)
    blank = jnp.zeros((SLOT - count, HALF), jnp.float32)
    nothing = jnp.zeros((SLOT, HALF), jnp.float32)
    for row in range(ROWS):
        at = slice(row * HALF, (row + 1) * HALF)
        region = ids[row : row + 1, mine]
        onehot[:, at] = jnp.where(which == region // LO, 1.0, 0.0).astype(jnp.bfloat16)
        value = jnp.concatenate([weights[:, row, :], blank], axis=0)
        big = value.astype(jnp.bfloat16).astype(jnp.float32)
        small = value - big
        for low in range(LO):
            here = region % LO == low
            to = slice(low * SLOT, (low + 1) * SLOT)
            coarse[to, at] = jnp.where(here, big, nothing).astype(jnp.bfloat16)
            fine[to, at] = jnp.where(here, small, nothing).astype(jnp.bfloat16)
    dims = (((1,), (1,)), ((), ()))
    total = lax.dot_general(onehot[...], coarse[...], dims, preferred_element_type=jnp.float32)
    total = total + lax.dot_general(onehot[...], fine[...], dims, preferred_element_type=jnp.float32)
    sums[0:HI] = total[:, :HALF]
    sums[HI : 2 * HI] = total[:, HALF:]


def join(side, kept, received, out):
    k = side[0]
    for tracer in range(TRACERS):
        for level in range(HERE):
            out[tracer, level, :, half_at(k)] = kept[tracer, level]
            out[tracer, level, :, half_at(1 - k)] = received[tracer, level]


def body(adjoint, courant_lon, courant_lat, mixing, injection, prior_flux, region_ids):
    lon_count = lax.axis_size("lon")
    lat_count = lax.axis_size("lat")
    side = lax.axis_index("lev").astype(jnp.int32).reshape(1)
    own = (adjoint, courant_lon, courant_lat, mixing)

    to_partner, edge_mine, edge_other = call(
        pack,
        (f32(MAIN + FIELDS + 1, ROWS, HALF), f32(FIELDS, ROWS, HALF), f32(FIELDS, ROWS, HALF)),
        (side, injection, *own),
        2,
    )
    partner = lax.ppermute(to_partner, "lev", [(0, 1), (1, 0)])
    same = []
    cross = []
    for i in range(lon_count):
        after = (i + 1) % lon_count
        same += [(2 * i, 2 * after), (2 * after + 1, 2 * i + 1)]
        cross += [(2 * i + 1, 2 * after), (2 * after, 2 * i + 1)]
    lon_same = lax.ppermute(edge_other, ("lon", "lev"), same)
    lon_cross = lax.ppermute(edge_mine, ("lon", "lev"), cross)

    first, last, edges = call(
        strips,
        (f32(STRIP, EDGE, HALF), f32(STRIP, EDGE, HALF), f32(2 * FIELDS, ROWS, HALF)),
        (side, *own, partner, edge_other, lon_same, lon_cross),
        1,
    )
    below = lax.ppermute(last, "lat", [(j, j + 1) for j in range(lat_count - 1)])
    above = lax.ppermute(first, "lat", [(j + 1, j) for j in range(lat_count - 1)])

    block = (LEVELS, TALL, WIDE)
    kept, returned, weights = call(
        steps,
        (
            f32(TRACERS, HERE, ROWS, HALF),
            f32(TRACERS, HERE, ROWS, HALF),
            f32(STEPS * TRACERS, ROWS, HALF),
        ),
        (side, injection, *own, partner, edges, below, above, prior_flux),
        2,
        [
            pltpu.VMEM((TRACERS, *block), jnp.float32),
            pltpu.VMEM(block, jnp.float32),
            pltpu.VMEM(block, jnp.float32),
            pltpu.VMEM(block, jnp.float32),
            pltpu.VMEM(block, jnp.float32),
            pltpu.VMEM(block, jnp.float32),
            pltpu.VMEM((TRACERS, LEVELS, 8, WIDE), jnp.float32),
            pltpu.VMEM((TRACERS, LEVELS, 8, HALF), jnp.float32),
        ],
    )
    received = lax.ppermute(returned, "lev", [(0, 1), (1, 0)])
    sums = call(
        regions,
        f32(2 * HI, HALF),
        (side, weights, region_ids),
        1,
        [pltpu.VMEM((HI, ROWS * HALF), jnp.bfloat16) for _ in range(3)],
    )
    pieces = lax.all_to_all(sums, ("lev", "lon", "lat"), 0, 0, tiled=True)
    region_grad = jnp.sum(pieces, axis=0).reshape(-1, SLOT)[:, : STEPS * TRACERS]
    adjoint_out = call(join, f32(*adjoint.shape), (side, kept, received), 1)
    return (adjoint_out, region_grad)


def solution(mesh):
    placed = (
        P(None, "lev", "lat", "lon"),
        P("lev", "lat", "lon"),
        P("lev", "lat", "lon"),
        P("lev", "lat", "lon"),
        P(None, "lev"),
        P(None, "lat", "lon"),
        P("lat", "lon"),
    )
    return jax.shard_map(
        body,
        mesh=mesh,
        in_specs=placed,
        out_specs=(P(None, "lev", "lat", "lon"), P(("lon", "lat", "lev"), None)),
        check_vma=False,
    )
```

time: 573 us -> 169 us (0.29)
  waiting for transfers between devices: 361 us -> 28.2 us
  starting transfers between devices: 124 us -> 54.8 us
  Pallas kernels: 0 us -> 41.4 us
  blocking collectives: 0 us -> 39 us
  matrix products: 37.3 us -> 0 us
  between operations: 15.5 us -> 0.69 us
  other arithmetic: 14.9 us -> 0.56 us
  local copies, waits for them, and re-layouts: 13 us -> 3.87 us
    unnamed x2 -> x0, waiting for transfers between devices: 268 us -> none
    ppermute x37 -> x6, starting transfers between devices: 124 us -> 54.8 us  [the longest x1 32.2 us: body(): received = lax.ppermute(returned, 'lev', [(0, 1), (1, 0)])]
    ppermute x37 -> x6, waiting for transfers between devices: 92.4 us -> 28.2 us  [the longest x1 18.5 us: body(): lon_cross = lax.ppermute(edge_mine, ('lon', 'lev'), cross)]
    pallas_call x0 -> x5, Pallas kernels: none -> 41.4 us  [call(): pl.pallas_call(kernel, out_shape=out_shape, in_specs=specs, out_specs=tup...]
    all_to_all x0 -> x1, blocking collectives: none -> 39 us  [body(): pieces = lax.all_to_all(sums, ('lev', 'lon', 'lat'), 0, 0, tiled=True)]
    dot_general x14 -> x0, matrix products: 37.3 us -> none  [the longest x8 27.7 us: one_block(): lax.dot_general(onehot, weights, (((1,), (1,)), ((), ())), precision=lax....]
    add x14 -> x0, other arithmetic: 7.34 us -> none  [the longest x6 7.31 us: advect(): tracer_field + east_rate * (east_cells - tracer_field)]
  transfers between devices with their start and end apart: 38 -> 6, of which waited for: 20 -> 4; matrix products, arithmetic and copies ran while one was open for 8% -> 1% of each run, Pallas kernels for 0% -> 2%
where the time goes in v1:
time: 169 us; the launch traced here: 168 us
  starting transfers between devices  54.8 us (32%)
  Pallas kernels  41.4 us (24%)
  blocking collectives  39 us (23%)
  waiting for transfers between devices  28.2 us (17%)
  local copies, waits for them, and re-layouts  3.87 us (2%)
    pallas_call x5, Pallas kernels, call(): pl.pallas_call(kernel, out_shape=out_shape, in_specs=specs, out_specs=tup...  41.4 us
    all_to_all x1, blocking collectives, body(): pieces = lax.all_to_all(sums, ('lev', 'lon', 'lat'), 0, 0, tiled=True)  39 us
    ppermute x1, starting transfers between devices, body(): received = lax.ppermute(returned, 'lev', [(0, 1), (1, 0)])  32.2 us
    ppermute x1, waiting for transfers between devices, body(): lon_cross = lax.ppermute(edge_mine, ('lon', 'lev'), cross)  18.5 us
    ppermute x1, starting transfers between devices, body(): partner = lax.ppermute(to_partner, 'lev', [(0, 1), (1, 0)])  11.5 us
    ppermute x1, waiting for transfers between devices, body(): lax.ppermute(last, 'lat', [(j, j + 1) for j in range(lat_count - 1)])  5 us
    ppermute x1, starting transfers between devices, body(): lon_cross = lax.ppermute(edge_mine, ('lon', 'lev'), cross)  4.77 us
    ppermute x1, waiting for transfers between devices, body(): lax.ppermute(first, 'lat', [(j + 1, j) for j in range(lat_count - 1)])  3.74 us
  transfers between devices with their start and end apart: 6, of which 4 were waited for; matrix products, arithmetic and copies ran while one was open for 1% of the time, Pallas kernels for 2%

profile of v1, /device:TPU:1, one launch (start us, length us, event | category | flops | bytes accessed | tf_op | source)
XLA Modules:
  0.0 168.5 jit_solution(986060835129902241)
XLA Ops:
  0.6 2.8 %pack.1 = (f32[64,32,128]{2,1,0:T(8,128)}, f32[7,32,128]{2,1,0:T(8,128)}, f32[7,32,128]{2,1,0:T(8,128)}) custom-call(s32[1]{0:T(128)} %bitcast.side, f32[4,8]{1,0:T(4,128)} %injection.3, f32[4,8,32,256]{3,2,1,0:T(8,128)} %adjoint.5, bf16[8,32,256]{2,1,0:T(8,128)(2,1)} %lon_wind.5, bf16[8,32,256]{2,1,0:T(8,128)(2,1)} %lat_wind.5, bf16[8,32,256]{2,1,0:T(8,128)(2,1)} %mixing.5), custom_call_target="tpu_custom_call" | custom-call | tf_op jit(solution)/shard_map/pack/pallas_call | solution.py:32
  3.4 11.5 %collective-permute-start = (f32[64,32,128]{2,1,0:T(8,128)}, f32[64,32,128]{2,1,0:T(8,128)S(1)}, u32[]{:S(2)}, u32[]{:S(2)}) collective-permute-start(f32[64,32,128]{2,1,0:T(8,128)} %get-tuple-element.11), channel_id=1, source_target_pairs={{0,1},{1,0},{2,3},{3,2},{4,5},{5,4},{6,7},{7,6},{8,9},{9,8},{10,11... | collective-permute-start | bytes 3145736 | tf_op jit(solution)/shard_map/ppermute | solution.py:286
  14.9 4.8 %collective-permute-start.2 = (f32[7,32,128]{2,1,0:T(8,128)}, f32[7,32,128]{2,1,0:T(8,128)S(1)}, u32[]{:S(2)}, u32[]{:S(2)}) collective-permute-start(f32[7,32,128]{2,1,0:T(8,128)} %get-tuple-element.13), channel_id=1, source_target_pairs={{1,16},{16,1},{17,32},{32,17},{33,48},{48,33},{49,64},{64,49},{65,... | collective-permute-start | bytes 344072 | tf_op jit(solution)/shard_map/ppermute | solution.py:294
  19.7 1.9 %collective-permute-start.1 = (f32[7,32,128]{2,1,0:T(8,128)}, f32[7,32,128]{2,1,0:T(8,128)S(1)}, u32[]{:S(2)}, u32[]{:S(2)}) collective-permute-start(f32[7,32,128]{2,1,0:T(8,128)} %get-tuple-element.12.edge_other), channel_id=1, source_target_pairs={{0,16},{17,1},{16,32},{33,17},{32,48},{49,33},{48,64},{65,49},{64,... | collective-permute-start | bytes 344072 | tf_op jit(solution)/shard_map/ppermute | solution.py:293
  21.6 18.5 %collective-permute-done.2.lon_cross = f32[7,32,128]{2,1,0:T(8,128)S(1)} collective-permute-done((f32[7,32,128]{2,1,0:T(8,128)}, f32[7,32,128]{2,1,0:T(8,128)S(1)}, u32[]{:S(2)}, u32[]{:S(2)}) %collective-permute-start.2) | collective-permute-done | bytes 114720 | tf_op jit(solution)/shard_map/ppermute | solution.py:294
  40.1 0.9 collective-permute-done.1.lon_same
  41.0 0.0 collective-permute-done.partner
  41.0 0.6 copy-done.5
  41.7 1.0 copy-done
  42.6 2.9 %strips.1 = (f32[126,8,128]{2,1,0:T(8,128)}, f32[126,8,128]{2,1,0:T(8,128)}, f32[14,32,128]{2,1,0:T(8,128)}) custom-call(s32[1]{0:T(128)} %bitcast.side, f32[4,8,32,256]{3,2,1,0:T(8,128)} %adjoint.5, bf16[8,32,256]{2,1,0:T(8,128)(2,1)} %lon_wind.5, bf16[8,32,256]{2,1,0:T(8,128)(2,1)} %lat_wind.5, bf16[8,32,256]{2,1,0:T(8,128)(2,1)} %mixing.5, ...), custom_call_target="tpu_custom_call" | custom-call | tf_op jit(solution)/shard_map/strips/pallas_call | solution.py:32
  45.5 3.2 %collective-permute-start.3 = (f32[126,8,128]{2,1,0:T(8,128)}, f32[126,8,128]{2,1,0:T(8,128)S(1)}, u32[]{:S(2)}, u32[]{:S(2)}) collective-permute-start(f32[126,8,128]{2,1,0:T(8,128)} %get-tuple-element.15), channel_id=1, source_target_pairs={{0,2},{2,4},{4,6},{6,8},{8,10},{10,12},{12,14},{1,3},{3,5},{5,7},{... | collective-permute-start | bytes 1548296 | tf_op jit(solution)/shard_map/ppermute | solution.py:302
  48.8 1.3 collective-permute-start.4
  50.1 5.0 %collective-permute-done.3.below = f32[126,8,128]{2,1,0:T(8,128)S(1)} collective-permute-done((f32[126,8,128]{2,1,0:T(8,128)}, f32[126,8,128]{2,1,0:T(8,128)S(1)}, u32[]{:S(2)}, u32[]{:S(2)}) %collective-permute-start.3) | collective-permute-done | bytes 516128 | tf_op jit(solution)/shard_map/ppermute | solution.py:302
  55.1 3.7 %collective-permute-done.4.above = f32[126,8,128]{2,1,0:T(8,128)S(1)} collective-permute-done((f32[126,8,128]{2,1,0:T(8,128)}, f32[126,8,128]{2,1,0:T(8,128)S(1)}, u32[]{:S(2)}, u32[]{:S(2)}) %collective-permute-start.4) | collective-permute-done | bytes 516128 | tf_op jit(solution)/shard_map/ppermute | solution.py:303
  58.8 0.8 copy-done.3
  59.6 29.3 %steps.1 = (f32[4,8,32,128]{3,2,1,0:T(8,128)}, f32[4,8,32,128]{3,2,1,0:T(8,128)}, f32[24,32,128]{2,1,0:T(8,128)}) custom-call(s32[1]{0:T(128)} %bitcast.side, f32[4,8]{1,0:T(4,128)} %injection.3, f32[4,8,32,256]{3,2,1,0:T(8,128)} %adjoint.5, bf16[8,32,256]{2,1,0:T(8,128)(2,1)} %lon_wind.5, bf16[8,32,256]{2,1,0:T(8,128)(2,1)} %lat_wind.5, ...), custom_call_target="tpu_custom_call" | custom-call | tf_op jit(solution)/shard_map/steps/pallas_call | solution.py:32
  89.0 32.2 %collective-permute-start.5 = (f32[4,8,32,128]{3,2,1,0:T(8,128)}, f32[4,8,32,128]{3,2,1,0:T(8,128)S(1)}, u32[]{:S(2)}, u32[]{:S(2)}) collective-permute-start(f32[4,8,32,128]{3,2,1,0:T(8,128)} %get-tuple-element.18), channel_id=1, source_target_pairs={{0,1},{1,0},{2,3},{3,2},{4,5},{5,4},{6,7},{7,6},{8,9},{9,8},{10,11... | collective-permute-start | bytes 1572872 | tf_op jit(solution)/shard_map/ppermute | solution.py:326
  121.1 4.1 %regions.1 = f32[512,128]{1,0:T(8,128)} custom-call(s32[1]{0:T(128)} %bitcast.side, f32[24,32,128]{2,1,0:T(8,128)} %get-tuple-element.19.weights, s32[32,256]{1,0:T(8,128)} %ids.1), custom_call_target="tpu_custom_call" | custom-call | tf_op jit(solution)/shard_map/regions/pallas_call | solution.py:32
  125.3 39.0 %all_to_all.9 = f32[512,1,128]{2,1,0:T(1,128)S(1)} all-to-all(f32[512,1,128]{2,1,0:T(1,128)} %bitcast.5), channel_id=1, replica_groups=mesh['lon'=32,'lat'=8,'lev'=2] {'lev','lon','lat'}, dimensions={0} | all-to-all | bytes 524288 | tf_op jit(solution)/shard_map/all_to_all | solution.py:334
  164.2 0.6 reduce_sum.9
  164.8 0.7 reshape.13
  165.5 0.0 collective-permute-done.5.received
  165.5 0.8 copy-done.1
  166.3 2.2 %join.1 = f32[4,8,32,256]{3,2,1,0:T(8,128)} custom-call(s32[1]{0:T(128)} %bitcast.side, f32[4,8,32,128]{3,2,1,0:T(8,128)} %get-tuple-element.17.kept, f32[4,8,32,128]{3,2,1,0:T(8,128)} %copy-done.1), custom_call_target="tpu_custom_call" | custom-call | tf_op jit(solution)/shard_map/join/pallas_call | solution.py:32
  (8 shorter events, 0.0 us)
Async XLA Ops:
  3.4 37.6 %collective-permute-start = (f32[64,32,128]{2,1,0:T(8,128)}, f32[64,32,128]{2,1,0:T(8,128)S(1)}, u32[]{:S(2)}, u32[]{:S(2)}) collective-permute-start(f32[64,32,128]{2,1,0:T(8,128)} %get-tuple-element.11), channel_id=1, source_target_pairs={{0,1},{1,0},{2,3},{3,2},{4,5},{5,4},{6,7},{7,6},{8,9},{9,8},{10,11... | collective-permute-start | bytes 3145736 | tf_op jit(solution)/shard_map/ppermute | solution.py:286
  14.9 25.2 %collective-permute-start.2 = (f32[7,32,128]{2,1,0:T(8,128)}, f32[7,32,128]{2,1,0:T(8,128)S(1)}, u32[]{:S(2)}, u32[]{:S(2)}) collective-permute-start(f32[7,32,128]{2,1,0:T(8,128)} %get-tuple-element.13), channel_id=1, source_target_pairs={{1,16},{16,1},{17,32},{32,17},{33,48},{48,33},{49,64},{64,49},{65,... | collective-permute-start | bytes 344072 | tf_op jit(solution)/shard_map/ppermute | solution.py:294
  19.7 21.3 %collective-permute-start.1 = (f32[7,32,128]{2,1,0:T(8,128)}, f32[7,32,128]{2,1,0:T(8,128)S(1)}, u32[]{:S(2)}, u32[]{:S(2)}) collective-permute-start(f32[7,32,128]{2,1,0:T(8,128)} %get-tuple-element.12.edge_other), channel_id=1, source_target_pairs={{0,16},{17,1},{16,32},{33,17},{32,48},{49,33},{48,64},{65,49},{64,... | collective-permute-start | bytes 344072 | tf_op jit(solution)/shard_map/ppermute | solution.py:293
  40.1 0.9 copy-start.4
  41.0 0.7 copy-start.5
  41.7 1.0 copy-start
  45.5 9.5 %collective-permute-start.3 = (f32[126,8,128]{2,1,0:T(8,128)}, f32[126,8,128]{2,1,0:T(8,128)S(1)}, u32[]{:S(2)}, u32[]{:S(2)}) collective-permute-start(f32[126,8,128]{2,1,0:T(8,128)} %get-tuple-element.15), channel_id=1, source_target_pairs={{0,2},{2,4},{4,6},{6,8},{8,10},{10,12},{12,14},{1,3},{3,5},{5,7},{... | collective-permute-start | bytes 1548296 | tf_op jit(solution)/shard_map/ppermute | solution.py:302
  48.8 10.0 %collective-permute-start.4 = (f32[126,8,128]{2,1,0:T(8,128)}, f32[126,8,128]{2,1,0:T(8,128)S(1)}, u32[]{:S(2)}, u32[]{:S(2)}) collective-permute-start(f32[126,8,128]{2,1,0:T(8,128)} %get-tuple-element.16), channel_id=1, source_target_pairs={{2,0},{4,2},{6,4},{8,6},{10,8},{12,10},{14,12},{3,1},{5,3},{7,5},{... | collective-permute-start | bytes 1548296 | tf_op jit(solution)/shard_map/ppermute | solution.py:303
  55.1 3.7 %copy-start.2 = (f32[126,8,128]{2,1,0:T(8,128)}, f32[126,8,128]{2,1,0:T(8,128)S(1)}, u32[]{:S(2)}) copy-start(f32[126,8,128]{2,1,0:T(8,128)S(1)} %collective-permute-done.3.below) | copy-start | bytes 1548292
  58.8 0.8 copy-start.3
  89.0 76.5 %collective-permute-start.5 = (f32[4,8,32,128]{3,2,1,0:T(8,128)}, f32[4,8,32,128]{3,2,1,0:T(8,128)S(1)}, u32[]{:S(2)}, u32[]{:S(2)}) collective-permute-start(f32[4,8,32,128]{3,2,1,0:T(8,128)} %get-tuple-element.18), channel_id=1, source_target_pairs={{0,1},{1,0},{2,3},{3,2},{4,5},{5,4},{6,7},{7,6},{8,9},{9,8},{10,11... | collective-permute-start | bytes 1572872 | tf_op jit(solution)/shard_map/ppermute | solution.py:326
  165.5 0.8 copy-start.1

commit v2 on v1

--- a/solution.py
+++ b/solution.py
@@ -23,10 +23,10 @@
 
 VMEM = pl.BlockSpec(memory_space=pltpu.VMEM)
 SMEM = pl.BlockSpec(memory_space=pltpu.SMEM)
-PARAMS = pltpu.CompilerParams(vmem_limit_bytes=56 * 1024 * 1024)
-
-
-def call(kernel, out_shape, operands, scalars, scratch=()):
+MIB = 1024 * 1024
+
+
+def call(kernel, out_shape, operands, scalars, scratch=(), limit=8):
     specs = [SMEM] * scalars + [VMEM] * (len(operands) - scalars)
     many = isinstance(out_shape, (tuple, list))
     return pl.pallas_call(
@@ -35,13 +35,25 @@
         in_specs=specs,
         out_specs=tuple(VMEM for _ in out_shape) if many else VMEM,
         scratch_shapes=list(scratch),
-        compiler_params=PARAMS,
+        compiler_params=pltpu.CompilerParams(vmem_limit_bytes=limit * MIB),
         name=kernel.__name__,
     )(*operands)
 
 
 def f32(*shape):
     return jax.ShapeDtypeStruct(shape, jnp.float32)
+
+
+def near(*shape):
+    return pltpu.VMEM(shape, jnp.float32)
+
+
+def hold(x):
+    return pltpu.with_memory_space_constraint(x, pltpu.VMEM)
+
+
+def permute(x, axes, pairs):
+    return hold(lax.ppermute(x, axes, pairs))
 
 
 def half_at(which):
@@ -259,8 +271,8 @@
     dims = (((1,), (1,)), ((), ()))
     total = lax.dot_general(onehot[...], coarse[...], dims, preferred_element_type=jnp.float32)
     total = total + lax.dot_general(onehot[...], fine[...], dims, preferred_element_type=jnp.float32)
-    sums[0:HI] = total[:, :HALF]
-    sums[HI : 2 * HI] = total[:, HALF:]
+    sums[pl.ds(0, HI, stride=2)] = total[:, :HALF]
+    sums[pl.ds(1, HI, stride=2)] = total[:, HALF:]
 
 
 def join(side, kept, received, out):
@@ -279,36 +291,37 @@
 
     to_partner, edge_mine, edge_other = call(
         pack,
-        (f32(MAIN + FIELDS + 1, ROWS, HALF), f32(FIELDS, ROWS, HALF), f32(FIELDS, ROWS, HALF)),
+        (near(MAIN + FIELDS + 1, ROWS, HALF), near(FIELDS, ROWS, HALF), near(FIELDS, ROWS, HALF)),
         (side, injection, *own),
         2,
     )
-    partner = lax.ppermute(to_partner, "lev", [(0, 1), (1, 0)])
     same = []
     cross = []
     for i in range(lon_count):
         after = (i + 1) % lon_count
         same += [(2 * i, 2 * after), (2 * after + 1, 2 * i + 1)]
         cross += [(2 * i + 1, 2 * after), (2 * after, 2 * i + 1)]
-    lon_same = lax.ppermute(edge_other, ("lon", "lev"), same)
-    lon_cross = lax.ppermute(edge_mine, ("lon", "lev"), cross)
+    lon_same = permute(edge_other, ("lon", "lev"), same)
+    lon_cross = permute(edge_mine, ("lon", "lev"), cross)
+
+    partner = permute(to_partner, "lev", [(0, 1), (1, 0)])
 
     first, last, edges = call(
         strips,
-        (f32(STRIP, EDGE, HALF), f32(STRIP, EDGE, HALF), f32(2 * FIELDS, ROWS, HALF)),
+        (near(STRIP, EDGE, HALF), near(STRIP, EDGE, HALF), near(2 * FIELDS, ROWS, HALF)),
         (side, *own, partner, edge_other, lon_same, lon_cross),
         1,
     )
-    below = lax.ppermute(last, "lat", [(j, j + 1) for j in range(lat_count - 1)])
-    above = lax.ppermute(first, "lat", [(j + 1, j) for j in range(lat_count - 1)])
+    below = permute(last, "lat", [(j, j + 1) for j in range(lat_count - 1)])
+    above = permute(first, "lat", [(j + 1, j) for j in range(lat_count - 1)])
 
     block = (LEVELS, TALL, WIDE)
     kept, returned, weights = call(
         steps,
         (
-            f32(TRACERS, HERE, ROWS, HALF),
-            f32(TRACERS, HERE, ROWS, HALF),
-            f32(STEPS * TRACERS, ROWS, HALF),
+            near(TRACERS, HERE, ROWS, HALF),
+            near(TRACERS, HERE, ROWS, HALF),
+            near(STEPS * TRACERS, ROWS, HALF),
         ),
         (side, injection, *own, partner, edges, below, above, prior_flux),
         2,
@@ -322,16 +335,18 @@
             pltpu.VMEM((TRACERS, LEVELS, 8, WIDE), jnp.float32),
             pltpu.VMEM((TRACERS, LEVELS, 8, HALF), jnp.float32),
         ],
-    )
-    received = lax.ppermute(returned, "lev", [(0, 1), (1, 0)])
+        24,
+    )
+    received = permute(returned, "lev", [(0, 1), (1, 0)])
     sums = call(
         regions,
-        f32(2 * HI, HALF),
+        near(2 * HI, HALF),
         (side, weights, region_ids),
         1,
         [pltpu.VMEM((HI, ROWS * HALF), jnp.bfloat16) for _ in range(3)],
-    )
-    pieces = lax.all_to_all(sums, ("lev", "lon", "lat"), 0, 0, tiled=True)
+        12,
+    )
+    pieces = lax.all_to_all(sums, ("lon", "lat", "lev"), 0, 0, tiled=True)
     region_grad = jnp.sum(pieces, axis=0).reshape(-1, SLOT)[:, : STEPS * TRACERS]
     adjoint_out = call(join, f32(*adjoint.shape), (side, kept, received), 1)
     return (adjoint_out, region_grad)

time: 169 us -> 159 us (0.941)
  Pallas kernels: 41.4 us -> 31.3 us
    pallas_call x5, Pallas kernels: 41.4 us -> 31.3 us  [call(): pl.pallas_call(kernel, out_shape=out_shape, in_specs=specs, out_specs=tup...]
    unnamed x12 -> x22, local copies, waits for them, and re-layouts: 3.2 us -> 4.63 us
where the time goes in v2:
time: 159 us
  starting transfers between devices  55.1 us (35%)
  blocking collectives  38.3 us (24%)
  Pallas kernels  31.3 us (20%)
  waiting for transfers between devices  27.5 us (17%)
  local copies, waits for them, and re-layouts  5.3 us (3%)
    ppermute x6, starting transfers between devices, permute(): return hold(lax.ppermute(x, axes, pairs))  55.1 us
    all_to_all x1, blocking collectives, body(): pieces = lax.all_to_all(sums, ('lon', 'lat', 'lev'), 0, 0, tiled=True)  38.3 us
    pallas_call x5, Pallas kernels, call(): pl.pallas_call(kernel, out_shape=out_shape, in_specs=specs, out_specs=tup...  31.3 us
    ppermute x6, waiting for transfers between devices, permute(): return hold(lax.ppermute(x, axes, pairs))  27.5 us
    unnamed x22, local copies, waits for them, and re-layouts  4.63 us
  transfers between devices with their start and end apart: 6, of which 4 were waited for; matrix products, arithmetic and copies ran while one was open for 1% of the time, Pallas kernels for 2%

profile of v2, /device:TPU:1, one launch (start us, length us, event | category | flops | bytes accessed | tf_op | source)
XLA Modules:
  0.0 158.7 jit_solution(15962467583148341250)
XLA Ops:
  0.6 0.7 copy-done.10
  1.3 1.2 copy-done
  2.5 0.9 copy-done.2
  3.5 0.9 copy-done.4
  4.4 0.9 copy-done.6
  5.3 1.0 pack.1
  6.3 11.5 %collective-permute-start = (f32[64,32,128]{2,1,0:T(8,128)S(1)}, f32[64,32,128]{2,1,0:T(8,128)S(1)}, u32[]{:S(2)}, u32[]{:S(2)}) collective-permute-start(f32[64,32,128]{2,1,0:T(8,128)S(1)} %get-tuple-element.11), channel_id=1, source_target_pairs={{0,1},{1,0},{2,3},{3,2},{4,5},{5,4},{6,7},{7,6},{8,9},{9,8},{10,11... | collective-permute-start | bytes 3145736 | tf_op jit(solution)/shard_map/ppermute | solution.py:56
  17.8 4.8 %collective-permute-start.2 = (f32[7,32,128]{2,1,0:T(8,128)S(1)}, f32[7,32,128]{2,1,0:T(8,128)S(1)}, u32[]{:S(2)}, u32[]{:S(2)}) collective-permute-start(f32[7,32,128]{2,1,0:T(8,128)S(1)} %get-tuple-element.13), channel_id=1, source_target_pairs={{1,16},{16,1},{17,32},{32,17},{33,48},{48,33},{49,64},{64,49},{65,... | collective-permute-start | bytes 344072 | tf_op jit(solution)/shard_map/ppermute | solution.py:56
  22.5 0.0 copy-start.8
  22.6 2.1 %collective-permute-start.1 = (f32[7,32,128]{2,1,0:T(8,128)S(1)}, f32[7,32,128]{2,1,0:T(8,128)S(1)}, u32[]{:S(2)}, u32[]{:S(2)}) collective-permute-start(f32[7,32,128]{2,1,0:T(8,128)S(1)} %get-tuple-element.12.edge_other), channel_id=1, source_target_pairs={{0,16},{17,1},{16,32},{33,17},{32,48},{49,33},{48,64},{65,49},{64,... | collective-permute-start | bytes 344072 | tf_op jit(solution)/shard_map/ppermute | solution.py:56
  24.6 18.2 %collective-permute-done.2.lon_cross = f32[7,32,128]{2,1,0:T(8,128)S(1)} collective-permute-done((f32[7,32,128]{2,1,0:T(8,128)S(1)}, f32[7,32,128]{2,1,0:T(8,128)S(1)}, u32[]{:S(2)}, u32[]{:S(2)}) %collective-permute-start.2) | collective-permute-done | bytes 114720 | tf_op jit(solution)/shard_map/ppermute | solution.py:56
  42.8 0.7 collective-permute-done.1.lon_same
  43.6 0.1 strips.1
  43.7 3.2 %collective-permute-start.3 = (f32[126,8,128]{2,1,0:T(8,128)S(1)}, f32[126,8,128]{2,1,0:T(8,128)S(1)}, u32[]{:S(2)}, u32[]{:S(2)}) collective-permute-start(f32[126,8,128]{2,1,0:T(8,128)S(1)} %get-tuple-element.15), channel_id=1, source_target_pairs={{0,2},{2,4},{4,6},{6,8},{8,10},{10,12},{12,14},{1,3},{3,5},{5,7},{... | collective-permute-start | bytes 1548296 | tf_op jit(solution)/shard_map/ppermute | solution.py:56
  46.9 1.3 collective-permute-start.4
  48.2 4.7 %collective-permute-done.3.below = f32[126,8,128]{2,1,0:T(8,128)S(1)} collective-permute-done((f32[126,8,128]{2,1,0:T(8,128)S(1)}, f32[126,8,128]{2,1,0:T(8,128)S(1)}, u32[]{:S(2)}, u32[]{:S(2)}) %collective-permute-start.3) | collective-permute-done | bytes 516128 | tf_op jit(solution)/shard_map/ppermute | solution.py:56
  52.9 3.8 %collective-permute-done.4.above = f32[126,8,128]{2,1,0:T(8,128)S(1)} collective-permute-done((f32[126,8,128]{2,1,0:T(8,128)S(1)}, f32[126,8,128]{2,1,0:T(8,128)S(1)}, u32[]{:S(2)}, u32[]{:S(2)}) %collective-permute-start.4) | collective-permute-done | bytes 516128 | tf_op jit(solution)/shard_map/ppermute | solution.py:56
  56.7 26.7 %steps.1 = (f32[4,8,32,128]{3,2,1,0:T(8,128)S(1)}, f32[4,8,32,128]{3,2,1,0:T(8,128)S(1)}, f32[24,32,128]{2,1,0:T(8,128)S(1)}) custom-call(s32[1]{0:T(128)} %bitcast.side, f32[4,8]{1,0:T(4,128)S(1)} %copy-done.10, f32[4,8,32,256]{3,2,1,0:T(8,128)S(1)} %copy-done.1, bf16[8,32,256]{2,1,0:T(8,128)(2,1)S(1)} %copy-done.3, bf16[8,32,256]{2,1,0:T(8,128)(2,1)S(1)} %copy-done.5, ...), custom_call_target="tpu_custom_call" | custom-call | tf_op jit(solution)/shard_map/steps/pallas_call | solution.py:32
  83.5 32.3 %collective-permute-start.5 = (f32[4,8,32,128]{3,2,1,0:T(8,128)S(1)}, f32[4,8,32,128]{3,2,1,0:T(8,128)S(1)}, u32[]{:S(2)}, u32[]{:S(2)}) collective-permute-start(f32[4,8,32,128]{3,2,1,0:T(8,128)S(1)} %get-tuple-element.18), channel_id=1, source_target_pairs={{0,1},{1,0},{2,3},{3,2},{4,5},{5,4},{6,7},{7,6},{8,9},{9,8},{10,11... | collective-permute-start | bytes 1572872 | tf_op jit(solution)/shard_map/ppermute | solution.py:56
  115.8 2.4 %regions.1 = f32[512,128]{1,0:T(8,128)S(1)} custom-call(s32[1]{0:T(128)} %bitcast.side, f32[24,32,128]{2,1,0:T(8,128)S(1)} %get-tuple-element.19.weights, s32[32,256]{1,0:T(8,128)S(1)} %copy-done.9), custom_call_target="tpu_custom_call" | custom-call | tf_op jit(solution)/shard_map/regions/pallas_call | solution.py:32
  118.2 38.3 %all_to_all.9 = f32[512,1,128]{2,1,0:T(1,128)S(1)} all-to-all(f32[512,1,128]{2,1,0:T(1,128)S(1)} %bitcast.5), channel_id=1, replica_groups=mesh['lon'=32,'lat'=8,'lev'=2] {'lon','lat','lev'}, dimensions={0} | all-to-all | bytes 524288 | tf_op jit(solution)/shard_map/all_to_all | solution.py:349
  156.5 0.6 reduce_sum.9
  157.0 0.7 reshape.13
  157.7 1.0 join.1
  (18 shorter events, 0.0 us)
Async XLA Ops:
  0.6 0.7 copy-start.10
  1.3 1.2 copy-start
  2.5 0.9 copy-start.2
  3.4 0.9 copy-start.4
  4.4 0.9 copy-start.6
  5.3 38.3 %copy-start.1 = (f32[4,8,32,256]{3,2,1,0:T(8,128)S(1)}, f32[4,8,32,256]{3,2,1,0:T(8,128)}, u32[]{:S(2)}) copy-start(f32[4,8,32,256]{3,2,1,0:T(8,128)} %adjoint.5) | copy-start | bytes 3145732
  5.3 38.3 %copy-start.3 = (bf16[8,32,256]{2,1,0:T(8,128)(2,1)S(1)}, bf16[8,32,256]{2,1,0:T(8,128)(2,1)}, u32[]{:S(2)}) copy-start(bf16[8,32,256]{2,1,0:T(8,128)(2,1)} %lon_wind.5) | copy-start | bytes 393220
  5.3 38.3 %copy-start.5 = (bf16[8,32,256]{2,1,0:T(8,128)(2,1)S(1)}, bf16[8,32,256]{2,1,0:T(8,128)(2,1)}, u32[]{:S(2)}) copy-start(bf16[8,32,256]{2,1,0:T(8,128)(2,1)} %lat_wind.5) | copy-start | bytes 393220
  5.3 38.3 %copy-start.7 = (bf16[8,32,256]{2,1,0:T(8,128)(2,1)S(1)}, bf16[8,32,256]{2,1,0:T(8,128)(2,1)}, u32[]{:S(2)}) copy-start(bf16[8,32,256]{2,1,0:T(8,128)(2,1)} %mixing.5) | copy-start | bytes 393220
  6.3 37.2 %collective-permute-start = (f32[64,32,128]{2,1,0:T(8,128)S(1)}, f32[64,32,128]{2,1,0:T(8,128)S(1)}, u32[]{:S(2)}, u32[]{:S(2)}) collective-permute-start(f32[64,32,128]{2,1,0:T(8,128)S(1)} %get-tuple-element.11), channel_id=1, source_target_pairs={{0,1},{1,0},{2,3},{3,2},{4,5},{5,4},{6,7},{7,6},{8,9},{9,8},{10,11... | collective-permute-start | bytes 3145736 | tf_op jit(solution)/shard_map/ppermute | solution.py:56
  17.8 25.0 %collective-permute-start.2 = (f32[7,32,128]{2,1,0:T(8,128)S(1)}, f32[7,32,128]{2,1,0:T(8,128)S(1)}, u32[]{:S(2)}, u32[]{:S(2)}) collective-permute-start(f32[7,32,128]{2,1,0:T(8,128)S(1)} %get-tuple-element.13), channel_id=1, source_target_pairs={{1,16},{16,1},{17,32},{32,17},{33,48},{48,33},{49,64},{64,49},{65,... | collective-permute-start | bytes 344072 | tf_op jit(solution)/shard_map/ppermute | solution.py:56
  22.5 34.2 %copy-start.8 = (bf16[4,32,256]{2,1,0:T(8,128)(2,1)S(1)}, bf16[4,32,256]{2,1,0:T(8,128)(2,1)}, u32[]{:S(2)}) copy-start(bf16[4,32,256]{2,1,0:T(8,128)(2,1)} %prior.1) | copy-start | bytes 196612
  22.6 21.0 %collective-permute-start.1 = (f32[7,32,128]{2,1,0:T(8,128)S(1)}, f32[7,32,128]{2,1,0:T(8,128)S(1)}, u32[]{:S(2)}, u32[]{:S(2)}) collective-permute-start(f32[7,32,128]{2,1,0:T(8,128)S(1)} %get-tuple-element.12.edge_other), channel_id=1, source_target_pairs={{0,16},{17,1},{16,32},{33,17},{32,48},{49,33},{48,64},{65,49},{64,... | collective-permute-start | bytes 344072 | tf_op jit(solution)/shard_map/ppermute | solution.py:56
  43.7 9.2 %collective-permute-start.3 = (f32[126,8,128]{2,1,0:T(8,128)S(1)}, f32[126,8,128]{2,1,0:T(8,128)S(1)}, u32[]{:S(2)}, u32[]{:S(2)}) collective-permute-start(f32[126,8,128]{2,1,0:T(8,128)S(1)} %get-tuple-element.15), channel_id=1, source_target_pairs={{0,2},{2,4},{4,6},{6,8},{8,10},{10,12},{12,14},{1,3},{3,5},{5,7},{... | collective-permute-start | bytes 1548296 | tf_op jit(solution)/shard_map/ppermute | solution.py:56
  46.9 9.8 %collective-permute-start.4 = (f32[126,8,128]{2,1,0:T(8,128)S(1)}, f32[126,8,128]{2,1,0:T(8,128)S(1)}, u32[]{:S(2)}, u32[]{:S(2)}) collective-permute-start(f32[126,8,128]{2,1,0:T(8,128)S(1)} %get-tuple-element.16), channel_id=1, source_target_pairs={{2,0},{4,2},{6,4},{8,6},{10,8},{12,10},{14,12},{3,1},{5,3},{7,5},{... | collective-permute-start | bytes 1548296 | tf_op jit(solution)/shard_map/ppermute | solution.py:56
  56.7 59.0 %copy-start.9 = (s32[32,256]{1,0:T(8,128)S(1)}, s32[32,256]{1,0:T(8,128)}, u32[]{:S(2)}) copy-start(s32[32,256]{1,0:T(8,128)} %ids.1) | copy-start | bytes 98308
  83.5 74.2 %collective-permute-start.5 = (f32[4,8,32,128]{3,2,1,0:T(8,128)S(1)}, f32[4,8,32,128]{3,2,1,0:T(8,128)S(1)}, u32[]{:S(2)}, u32[]{:S(2)}) collective-permute-start(f32[4,8,32,128]{3,2,1,0:T(8,128)S(1)} %get-tuple-element.18), channel_id=1, source_target_pairs={{0,1},{1,0},{2,3},{3,2},{4,5},{5,4},{6,7},{7,6},{8,9},{9,8},{10,11... | collective-permute-start | bytes 1572872 | tf_op jit(solution)/shard_map/ppermute | solution.py:56

commit v3 on v2

v3 whole, which is shorter than its diff:
```python
import jax
import jax.numpy as jnp
from jax import lax
from jax.experimental import pallas as pl
from jax.experimental.pallas import tpu as pltpu
from jax.sharding import PartitionSpec as P

STEPS = 6
TRACERS = 4
WINDS = 3
FIELDS = WINDS + TRACERS
FIRST = WINDS + 2
HERE = 8
LEVELS = 16
ROWS = 32
HALF = 128
EDGE = 8
TALL = ROWS + 2 * EDGE
WIDE = 2 * HALF
CHUNK = 16
HI = 256
LO = 8
SLOT = 32

VMEM = pl.BlockSpec(memory_space=pltpu.VMEM)
SMEM = pl.BlockSpec(memory_space=pltpu.SMEM)
MIB = 1024 * 1024


def call(kernel, out_shape, operands, scalars, scratch=(), limit=8):
    specs = [SMEM] * scalars + [VMEM] * (len(operands) - scalars)
    many = isinstance(out_shape, (tuple, list))
    return pl.pallas_call(
        kernel,
        out_shape=out_shape,
        in_specs=specs,
        out_specs=tuple(VMEM for _ in out_shape) if many else VMEM,
        scratch_shapes=list(scratch),
        compiler_params=pltpu.CompilerParams(vmem_limit_bytes=limit * MIB),
        name=kernel.__name__,
    )(*operands)


def f32(*shape):
    return jax.ShapeDtypeStruct(shape, jnp.float32)


def near(*shape):
    return pltpu.VMEM(shape, jnp.float32)


def hold(x):
    return pltpu.with_memory_space_constraint(x, pltpu.VMEM)


def permute(x, axes, pairs):
    return hold(lax.ppermute(x, axes, pairs))


def half_at(which):
    return pl.ds(pl.multiple_of(which * HALF, HALF), HALF)


def own_plane(refs, field, level, rows, lanes):
    if field >= WINDS:
        return refs[WINDS][field - WINDS, level, rows, lanes]
    return refs[field][level, rows, lanes].astype(jnp.float32)


def pack(side, injection, lon_wind, lat_wind, mixing, adjoint, first_part, second_part, edge_mine, edge_other):
    refs = (lon_wind, lat_wind, mixing, adjoint)
    k = side[0]
    mine = half_at(k)
    other = half_at(1 - k)
    rows = slice(0, ROWS)
    slot = lax.broadcasted_iota(jnp.int32, (ROWS, HALF), 1) // (2 * EDGE)
    for field in range(FIELDS):
        part, begin, count = (first_part, 0, FIRST) if field < FIRST else (second_part, FIRST, FIELDS - FIRST)
        packed_mine = jnp.zeros((ROWS, HALF), jnp.float32)
        packed_other = jnp.zeros((ROWS, HALF), jnp.float32)
        for level in range(HERE):
            shift = (2 * EDGE * level + EDGE) % HALF
            plane_mine = own_plane(refs, field, level, rows, mine)
            plane_other = own_plane(refs, field, level, rows, other)
            part[(field - begin) * HERE + level] = plane_other
            packed_mine = jnp.where(slot == level, pltpu.roll(plane_mine, shift, 1), packed_mine)
            packed_other = jnp.where(slot == level, pltpu.roll(plane_other, shift, 1), packed_other)
        part[count * HERE + field - begin] = packed_mine
        edge_mine[field] = packed_mine
        edge_other[field] = packed_other
    for tracer in range(TRACERS):
        for level in range(HERE):
            row = tracer * HERE + level
            first_part[FIRST * HERE + FIRST, row : row + 1, :] = jnp.full(
                (1, HALF), injection[tracer, level], jnp.float32
            )


def inner_lanes(side):
    lane = lax.broadcasted_iota(jnp.int32, (ROWS, HALF), 1)
    return ((lane // EDGE) % 2) != side[0]


def own_strips(side, lon_wind, lat_wind, mixing, adjoint, edge_other, lon_same, first, last, edges):
    refs = (lon_wind, lat_wind, mixing, adjoint)
    mine = half_at(side[0])
    head = slice(0, EDGE)
    tail = slice(ROWS - EDGE, ROWS)
    inner = inner_lanes(side)
    for field in range(FIELDS):
        for level in range(HERE):
            at = field * HERE + level
            if field < WINDS:
                plane = own_plane(refs, field, level, slice(0, ROWS), mine)
                first[at] = plane[head]
                last[at] = plane[tail]
            else:
                first[at] = own_plane(refs, field, level, head, mine)
                last[at] = own_plane(refs, field, level, tail, mine)
        merged = jnp.where(inner, edge_other[field], lon_same[field])
        edges[field] = merged
        first[FIELDS * HERE + field] = merged[head]
        last[FIELDS * HERE + field] = merged[tail]


def part_strips(begin):
    def strips(side, partner, lon_cross, first, last, edges):
        head = slice(0, EDGE)
        tail = slice(ROWS - EDGE, ROWS)
        count = edges.shape[0]
        planes = count * HERE
        inner = inner_lanes(side)
        first[0:planes] = partner[0:planes, head, :]
        last[0:planes] = partner[0:planes, tail, :]
        for field in range(count):
            merged = jnp.where(inner, partner[planes + field], lon_cross[begin + field])
            edges[field] = merged
            first[planes + field] = merged[head]
            last[planes + field] = merged[tail]

    return strips


CORE = slice(0, HALF)
WING = slice(HALF, WIDE)


def place(target, main, edge, shift):
    for rows, source, rim in zip(((0, EDGE), (EDGE, EDGE + ROWS), (EDGE + ROWS, TALL)), main, edge):
        at = slice(*rows)
        target[at, CORE] = source
        target[at, WING] = pltpu.roll(rim, shift, 1)


def gather(k, refs, begin, count, target_of, partner, own_edges, edges, own_below, own_above, below, above):
    mine = half_at(k)
    for group in range(2):
        base = (k if group == 0 else 1 - k) * HERE
        for level in range(HERE):
            shift = (HALF - (2 * EDGE * level + EDGE)) % HALF
            for field in range(begin, begin + count):
                if group == 0:
                    at = field * HERE + level
                    rim = FIELDS * HERE + field
                    middle = own_plane(refs, field, level, slice(0, ROWS), mine)
                    main = (own_below[at], middle, own_above[at])
                    edge = (own_below[rim], own_edges[field], own_above[rim])
                else:
                    at = (field - begin) * HERE + level
                    rim = count * HERE + field - begin
                    main = (below[at], partner[at], above[at])
                    edge = (below[rim], edges[field - begin], above[rim])
                place(target_of(field, base + level), main, edge, shift)


def integrate(k, count, prior, first_tracer, kept, returned, weights, field_ref, solved_ref, lon_ref, lat_ref, kab_ref, inv_ref, cp_ref, red_ref, inj_ref):
    def one_step(step, _):
        def solve(tile, _):
            at = pl.ds(pl.multiple_of(tile * 8, 8), 8)
            to = pl.ds(pl.multiple_of(tile * 8 + EDGE, 8), 8)
            carried = [None] * count
            for level in range(LEVELS):
                inverse = inv_ref[level, at, :]
                if level:
                    kbelow = kab_ref[level - 1, at, :]
                for tracer in range(count):
                    rhs = field_ref[tracer, level, at, :]
                    if level:
                        rhs = rhs + kbelow * carried[tracer]
                    carried[tracer] = rhs * inverse
                    red_ref[tracer, level] = carried[tracer]
            for tracer in range(count):
                solved_ref[tracer, LEVELS - 1, to, :] = carried[tracer]
            for level in reversed(range(LEVELS - 1)):
                cprime = cp_ref[level, at, :]
                for tracer in range(count):
                    carried[tracer] = red_ref[tracer, level] - cprime * carried[tracer]
                    solved_ref[tracer, level, to, :] = carried[tracer]
            return 0

        lax.fori_loop(0, TALL // 8, solve, 0)

        def weigh(tile, _):
            at = pl.ds(pl.multiple_of(tile * 8 + 2 * EDGE, 8), 8)
            to = pl.ds(pl.multiple_of(tile * 8, 8), 8)
            for tracer in range(count):
                total = jnp.zeros((8, HALF), jnp.float32)
                for level in range(LEVELS):
                    total = total + inj_ref[first_tracer + tracer, level] * solved_ref[tracer, level, at, CORE]
                weights[step * count + tracer, to, :] = total
            return 0

        lax.fori_loop(0, ROWS // 8, weigh, 0)

        lane = lax.broadcasted_iota(jnp.int32, (CHUNK, HALF), 1)
        left = lane == 0
        right = lane == HALF - 1

        def advect(level, _):
            for start in range(0, TALL, CHUNK):
                rows = slice(start, start + CHUNK)
                centre = slice(EDGE + start, EDGE + start + CHUNK)
                north_rows = slice(EDGE + start + 1, EDGE + start + CHUNK + 1)
                south_rows = slice(EDGE + start - 1, EDGE + start + CHUNK - 1)
                rates = []
                for side in (CORE, WING):
                    lon = lon_ref[level, rows, side]
                    lat = lat_ref[level, rows, side]
                    rates.append((lon > 0.0, lat > 0.0, jnp.abs(lon), jnp.abs(lat)))
                for tracer in range(count):
                    cells = [solved_ref[tracer, level, centre, side] for side in (CORE, WING)]
                    ahead = [pltpu.roll(c, HALF - 1, 1) for c in cells]
                    behind = [pltpu.roll(c, 1, 1) for c in cells]
                    for i, side in enumerate((CORE, WING)):
                        east, north, lon, lat = rates[i]
                        along = jnp.where(
                            east,
                            jnp.where(right, ahead[1 - i], ahead[i]),
                            jnp.where(left, behind[1 - i], behind[i]),
                        )
                        across = jnp.where(
                            north,
                            solved_ref[tracer, level, north_rows, side],
                            solved_ref[tracer, level, south_rows, side],
                        )
                        field_ref[tracer, level, rows, side] = (
                            cells[i] + lon * (along - cells[i]) + lat * (across - cells[i])
                        )
            return 0

        lax.fori_loop(0, LEVELS, advect, 0)
        return 0

    solved_ref[:, :, 0:EDGE, :] = jnp.zeros((count, LEVELS, EDGE, WIDE), jnp.float32)
    solved_ref[:, :, EDGE + TALL :, :] = jnp.zeros((count, LEVELS, EDGE, WIDE), jnp.float32)
    lax.fori_loop(0, STEPS, one_step, 0)

    mine = half_at(k)
    inside = slice(EDGE, EDGE + ROWS)
    for tracer in range(count):
        flux = prior[first_tracer + tracer, :, mine].astype(jnp.float32)
        for step in range(STEPS):
            weights[step * count + tracer] = weights[step * count + tracer] * flux
        for level in range(HERE):
            kept[tracer, level] = field_ref[tracer, k * HERE + level, inside, CORE]
            returned[tracer, level] = field_ref[tracer, (1 - k) * HERE + level, inside, CORE]


def first_steps(
    side, injection, lon_wind, lat_wind, mixing, adjoint, partner, own_edges, edges,
    own_below, own_above, below, above, prior,
    kept, returned, weights, lon_ref, lat_ref, kab_ref, inv_ref, cp_ref, inj_ref,
    field_ref, solved_ref, red_ref,
):
    k = side[0]
    refs = (lon_wind, lat_wind, mixing, adjoint)

    def target_of(field, level):
        if field >= WINDS:
            return field_ref.at[field - WINDS, level]
        return (lon_ref, lat_ref, kab_ref)[field].at[level]

    gather(k, refs, 0, FIRST, target_of, partner, own_edges, edges, own_below, own_above, below, above)
    for tracer in range(TRACERS):
        for level in range(HERE):
            row = tracer * HERE + level
            inj_ref[tracer, pl.ds(k * HERE + level, 1)] = jnp.full((1, 8, HALF), injection[tracer, level], jnp.float32)
            inj_ref[tracer, pl.ds((1 - k) * HERE + level, 1)] = jnp.broadcast_to(
                partner[FIRST * HERE + FIRST, row : row + 1, :][None], (1, 8, HALF)
            )
    kab_ref[LEVELS - 1] = jnp.zeros((TALL, WIDE), jnp.float32)

    def pivots(tile, _):
        at = pl.ds(pl.multiple_of(tile * 8, 8), 8)
        carried = jnp.zeros((8, WIDE), jnp.float32)
        kbelow = jnp.zeros((8, WIDE), jnp.float32)
        for level in range(LEVELS):
            kabove = kab_ref[level, at, :]
            inverse = 1.0 / (1.0 + kabove + kbelow * (1.0 + carried))
            carried = -kabove * inverse
            inv_ref[level, at, :] = inverse
            cp_ref[level, at, :] = carried
            kbelow = kabove
        return 0

    lax.fori_loop(0, TALL // 8, pivots, 0)
    integrate(
        k, FIRST - WINDS, prior, 0, kept, returned, weights,
        field_ref, solved_ref, lon_ref, lat_ref, kab_ref, inv_ref, cp_ref, red_ref, inj_ref,
    )


def second_steps(
    side, adjoint, partner, own_edges, edges, own_below, own_above, below, above, prior,
    lon_ref, lat_ref, kab_ref, inv_ref, cp_ref, inj_ref,
    kept, returned, weights, field_ref, solved_ref, red_ref,
):
    k = side[0]
    refs = (None, None, None, adjoint)
    gather(
        k, refs, FIRST, FIELDS - FIRST, lambda field, level: field_ref.at[field - FIRST, level],
        partner, own_edges, edges, own_below, own_above, below, above,
    )
    integrate(
        k, FIELDS - FIRST, prior, FIRST - WINDS, kept, returned, weights,
        field_ref, solved_ref, lon_ref, lat_ref, kab_ref, inv_ref, cp_ref, red_ref, inj_ref,
    )


def regions(side, first_weights, second_weights, ids, sums, onehot, coarse, fine, ordered):
    mine = half_at(side[0])
    count = STEPS * TRACERS
    which = lax.broadcasted_iota(jnp.int32, (HI, HALF), 0)
    blank = jnp.zeros((SLOT - count, HALF), jnp.float32)
    nothing = jnp.zeros((SLOT, HALF), jnp.float32)
    pair = TRACERS // 2
    for step in range(STEPS):
        ordered[step * TRACERS : step * TRACERS + pair] = first_weights[step * pair : (step + 1) * pair]
        ordered[step * TRACERS + pair : (step + 1) * TRACERS] = second_weights[step * pair : (step + 1) * pair]
    for row in range(ROWS):
        at = slice(row * HALF, (row + 1) * HALF)
        region = ids[row : row + 1, mine]
        onehot[:, at] = jnp.where(which == region // LO, 1.0, 0.0).astype(jnp.bfloat16)
        value = jnp.concatenate([ordered[:, row, :], blank], axis=0)
        big = value.astype(jnp.bfloat16).astype(jnp.float32)
        small = value - big
        for low in range(LO):
            here = region % LO == low
            to = slice(low * SLOT, (low + 1) * SLOT)
            coarse[to, at] = jnp.where(here, big, nothing).astype(jnp.bfloat16)
            fine[to, at] = jnp.where(here, small, nothing).astype(jnp.bfloat16)
    dims = (((1,), (1,)), ((), ()))
    total = lax.dot_general(onehot[...], coarse[...], dims, preferred_element_type=jnp.float32)
    total = total + lax.dot_general(onehot[...], fine[...], dims, preferred_element_type=jnp.float32)
    sums[pl.ds(0, HI, stride=2)] = total[:, :HALF]
    sums[pl.ds(1, HI, stride=2)] = total[:, HALF:]


def join(side, kept0, kept1, received0, received1, out):
    k = side[0]
    for tracer in range(TRACERS):
        kept, received, at = (kept0, received0, tracer) if tracer < 2 else (kept1, received1, tracer - 2)
        for level in range(HERE):
            out[tracer, level, :, half_at(k)] = kept[at, level]
            out[tracer, level, :, half_at(1 - k)] = received[at, level]


def body(adjoint, courant_lon, courant_lat, mixing, injection, prior_flux, region_ids):
    lon_count = lax.axis_size("lon")
    lat_count = lax.axis_size("lat")
    side = lax.axis_index("lev").astype(jnp.int32).reshape(1)
    own = tuple(hold(x) for x in (courant_lon, courant_lat, mixing, adjoint))
    adjoint = own[3]
    prior_flux = hold(prior_flux)

    same = []
    cross = []
    for i in range(lon_count):
        after = (i + 1) % lon_count
        same += [(2 * i, 2 * after), (2 * after + 1, 2 * i + 1)]
        cross += [(2 * i + 1, 2 * after), (2 * after, 2 * i + 1)]
    swap = [(0, 1), (1, 0)]
    north = [(j, j + 1) for j in range(lat_count - 1)]
    south = [(j + 1, j) for j in range(lat_count - 1)]

    counts = (FIRST, FIELDS - FIRST)
    parts = call(
        pack,
        (
            near(FIRST * HERE + FIRST + 1, ROWS, HALF),
            near(counts[1] * HERE + counts[1], ROWS, HALF),
            near(FIELDS, ROWS, HALF),
            near(FIELDS, ROWS, HALF),
        ),
        (side, injection, *own),
        2,
    )
    edge_mine, edge_other = parts[2:]
    lon_same = permute(edge_other, ("lon", "lev"), same)
    lon_cross = permute(edge_mine, ("lon", "lev"), cross)
    partners = [permute(part, "lev", swap) for part in parts[:2]]

    strip = FIELDS * HERE + FIELDS
    first, last, own_edges = call(
        own_strips,
        (near(strip, EDGE, HALF), near(strip, EDGE, HALF), near(FIELDS, ROWS, HALF)),
        (side, *own, edge_other, lon_same),
        1,
    )
    own_below = permute(last, "lat", north)
    own_above = permute(first, "lat", south)

    halos = []
    for group in range(2):
        count = counts[group]
        strip = count * HERE + count
        first, last, edges = call(
            part_strips(group * FIRST),
            (near(strip, EDGE, HALF), near(strip, EDGE, HALF), near(count, ROWS, HALF)),
            (side, partners[group], lon_cross),
            1,
        )
        halos.append((partners[group], own_edges, edges, own_below, own_above, permute(last, "lat", north), permute(first, "lat", south)))

    def results(group):
        tracers = TRACERS // 2
        return (near(tracers, HERE, ROWS, HALF), near(tracers, HERE, ROWS, HALF), near(STEPS * tracers, ROWS, HALF))

    block = (LEVELS, TALL, WIDE)
    scratch = [
        pltpu.VMEM((TRACERS // 2, LEVELS, TALL, WIDE), jnp.float32),
        pltpu.VMEM((TRACERS // 2, LEVELS, TALL + 2 * EDGE, WIDE), jnp.float32),
        pltpu.VMEM((TRACERS // 2, LEVELS, 8, WIDE), jnp.float32),
    ]
    outs = call(
        first_steps,
        (*results(0), *(near(*block) for _ in range(5)), near(TRACERS, LEVELS, 8, HALF)),
        (side, injection, *own, *halos[0], prior_flux),
        2,
        scratch,
        12,
    )
    kept0, returned0, weights0 = outs[:3]
    received0 = permute(returned0, "lev", swap)
    kept1, returned1, weights1 = call(
        second_steps,
        results(1),
        (side, adjoint, *halos[1], prior_flux, *outs[3:]),
        1,
        scratch,
        12,
    )
    received1 = permute(returned1, "lev", swap)
    sums = call(
        regions,
        near(2 * HI, HALF),
        (side, weights0, weights1, region_ids),
        1,
        [pltpu.VMEM((HI, ROWS * HALF), jnp.bfloat16) for _ in range(3)]
        + [pltpu.VMEM((STEPS * TRACERS, ROWS, HALF), jnp.float32)],
        12,
    )
    pieces = lax.all_to_all(sums, ("lon", "lat", "lev"), 0, 0, tiled=True)
    region_grad = jnp.sum(pieces, axis=0).reshape(-1, SLOT)[:, : STEPS * TRACERS]
    adjoint_out = call(join, f32(*adjoint.shape), (side, kept0, kept1, received0, received1), 1)
    return (adjoint_out, region_grad)


def solution(mesh):
    placed = (
        P(None, "lev", "lat", "lon"),
        P("lev", "lat", "lon"),
        P("lev", "lat", "lon"),
        P("lev", "lat", "lon"),
        P(None, "lev"),
        P(None, "lat", "lon"),
        P("lat", "lon"),
    )
    return jax.shard_map(
        body,
        mesh=mesh,
        in_specs=placed,
        out_specs=(P(None, "lev", "lat", "lon"), P(("lon", "lat", "lev"), None)),
        check_vma=False,
    )
```

time: 159 us -> 178 us (1.12)
  the two profiles are of different devices: /device:TPU:1 before, /device:TPU:65 now
where the time goes in v3:
time: 178 us
  starting transfers between devices  88 us (49%)
  waiting for transfers between devices  41.6 us (23%)
  Pallas kernels  41.1 us (23%)
  local copies, waits for them, and re-layouts  5.3 us (3%)
    ppermute x12, starting transfers between devices, permute(): return hold(lax.ppermute(x, axes, pairs))  63.6 us
    ppermute x12, waiting for transfers between devices, permute(): return hold(lax.ppermute(x, axes, pairs))  41.6 us
    pallas_call x8, Pallas kernels, call(): pl.pallas_call(kernel, out_shape=out_shape, in_specs=specs, out_specs=tup...  41.1 us
    all_to_all x1, starting transfers between devices, body(): pieces = lax.all_to_all(sums, ('lon', 'lat', 'lev'), 0, 0, tiled=True)  24.3 us
    unnamed x22, local copies, waits for them, and re-layouts  4.64 us
  transfers between devices with their start and end apart: 13, of which 4 were waited for; matrix products, arithmetic and copies ran while one was open for 0% of the time, Pallas kernels for 11%

profile of v3, /device:TPU:65, one launch (start us, length us, event | category | flops | bytes accessed | tf_op | source)
XLA Modules:
  0.0 177.5 jit_solution(14748480115694932587)
XLA Ops:
  1.3 1.2 copy-done
  2.5 0.9 copy-done.2
  5.3 1.0 pack.1
  6.3 9.7 %collective-permute-start = (f32[46,32,128]{2,1,0:T(8,128)S(1)}, f32[46,32,128]{2,1,0:T(8,128)S(1)}, u32[]{:S(2)}, u32[]{:S(2)}) collective-permute-start(f32[46,32,128]{2,1,0:T(8,128)S(1)} %get-tuple-element.27), channel_id=1, source_target_pairs={{0,1},{1,0},{2,3},{3,2},{4,5},{5,4},{6,7},{7,6},{8,9},{9,8},{10,11... | collective-permute-start | bytes 2261000 | tf_op jit(solution)/shard_map/ppermute | solution.py:57
  16.0 3.9 %collective-permute-start.1 = (f32[7,32,128]{2,1,0:T(8,128)S(1)}, f32[7,32,128]{2,1,0:T(8,128)S(1)}, u32[]{:S(2)}, u32[]{:S(2)}) collective-permute-start(f32[7,32,128]{2,1,0:T(8,128)S(1)} %get-tuple-element.28.edge_other), channel_id=1, source_target_pairs={{0,16},{17,1},{16,32},{33,17},{32,48},{49,33},{48,64},{65,49},{64,... | collective-permute-start | bytes 344072 | tf_op jit(solution)/shard_map/ppermute | solution.py:57
  20.0 1.9 %collective-permute-start.7 = (f32[18,32,128]{2,1,0:T(8,128)S(1)}, f32[18,32,128]{2,1,0:T(8,128)S(1)}, u32[]{:S(2)}, u32[]{:S(2)}) collective-permute-start(f32[18,32,128]{2,1,0:T(8,128)S(1)} %get-tuple-element.37), channel_id=1, source_target_pairs={{0,1},{1,0},{2,3},{3,2},{4,5},{5,4},{6,7},{7,6},{8,9},{9,8},{10,11... | collective-permute-start | bytes 884744 | tf_op jit(solution)/shard_map/ppermute | solution.py:57
  21.9 12.3 %collective-permute-done.1.lon_same = f32[7,32,128]{2,1,0:T(8,128)S(1)} collective-permute-done((f32[7,32,128]{2,1,0:T(8,128)S(1)}, f32[7,32,128]{2,1,0:T(8,128)S(1)}, u32[]{:S(2)}, u32[]{:S(2)}) %collective-permute-start.1) | collective-permute-done | bytes 114720 | tf_op jit(solution)/shard_map/ppermute | solution.py:57
  34.3 3.2 %collective-permute-start.3 = (f32[63,8,128]{2,1,0:T(8,128)S(1)}, f32[63,8,128]{2,1,0:T(8,128)S(1)}, u32[]{:S(2)}, u32[]{:S(2)}) collective-permute-start(f32[63,8,128]{2,1,0:T(8,128)S(1)} %get-tuple-element.32), channel_id=1, source_target_pairs={{0,2},{2,4},{4,6},{6,8},{8,10},{10,12},{12,14},{1,3},{3,5},{5,7},{... | collective-permute-start | bytes 774152 | tf_op jit(solution)/shard_map/ppermute | solution.py:57
  37.5 23.4 %collective-permute-start.2 = (f32[7,32,128]{2,1,0:T(8,128)S(1)}, f32[7,32,128]{2,1,0:T(8,128)S(1)}, u32[]{:S(2)}, u32[]{:S(2)}) collective-permute-start(f32[7,32,128]{2,1,0:T(8,128)S(1)} %get-tuple-element.30), channel_id=1, source_target_pairs={{1,16},{16,1},{17,32},{32,17},{33,48},{48,33},{49,64},{64,49},{65,... | collective-permute-start | bytes 344072 | tf_op jit(solution)/shard_map/ppermute | solution.py:57
  60.9 1.3 collective-permute-start.4
  62.2 4.8 %collective-permute-done.2.lon_cross = f32[7,32,128]{2,1,0:T(8,128)S(1)} collective-permute-done((f32[7,32,128]{2,1,0:T(8,128)S(1)}, f32[7,32,128]{2,1,0:T(8,128)S(1)}, u32[]{:S(2)}, u32[]{:S(2)}) %collective-permute-start.2) | collective-permute-done | bytes 114720 | tf_op jit(solution)/shard_map/ppermute | solution.py:57
  67.1 3.2 %collective-permute-start.5 = (f32[45,8,128]{2,1,0:T(8,128)S(1)}, f32[45,8,128]{2,1,0:T(8,128)S(1)}, u32[]{:S(2)}, u32[]{:S(2)}) collective-permute-start(f32[45,8,128]{2,1,0:T(8,128)S(1)} %get-tuple-element.34), channel_id=1, source_target_pairs={{0,2},{2,4},{4,6},{6,8},{8,10},{10,12},{12,14},{1,3},{3,5},{5,7},{... | collective-permute-start | bytes 552968 | tf_op jit(solution)/shard_map/ppermute | solution.py:57
  70.3 1.4 collective-permute-start.6
  71.8 4.0 %collective-permute-start.8 = (f32[18,8,128]{2,1,0:T(8,128)S(1)}, f32[18,8,128]{2,1,0:T(8,128)S(1)}, u32[]{:S(2)}, u32[]{:S(2)}) collective-permute-start(f32[18,8,128]{2,1,0:T(8,128)S(1)} %get-tuple-element.39), channel_id=1, source_target_pairs={{0,2},{2,4},{4,6},{6,8},{8,10},{10,12},{12,14},{1,3},{3,5},{5,7},{... | collective-permute-start | bytes 221192 | tf_op jit(solution)/shard_map/ppermute | solution.py:57
  75.8 1.3 collective-permute-start.9
  77.2 18.9 %first_steps.1 = (f32[2,8,32,128]{3,2,1,0:T(8,128)S(1)}, f32[2,8,32,128]{3,2,1,0:T(8,128)S(1)}, f32[12,32,128]{2,1,0:T(8,128)S(1)}, f32[16,48,256]{2,1,0:T(8,128...) custom-call(s32[1]{0:T(128)} %bitcast.side, ...), custom_call_target="tpu_custom_call" | custom-call | tf_op jit(solution)/shard_map/first_steps/pallas_call | solution.py:33
  96.1 17.0 %second_steps.1 = (f32[2,8,32,128]{3,2,1,0:T(8,128)S(1)}, f32[2,8,32,128]{3,2,1,0:T(8,128)S(1)}, f32[12,32,128]{2,1,0:T(8,128)S(1)}) custom-call(s32[1]{0:T(128)} %bitcast.side, f32[4,8,32,256]{3,2,1,0:T(8,128)S(1)} %copy-done.1, f32[18,32,128]{2,1,0:T(8,128)S(1)} %collective-permute-done.7.partner, f32[7,32,128]{2,1,0:T(8,128)S(1)} %get-tuple-element.29.own_edges, ...), custom_call_target="tpu_custom_call" | custom-call | tf_op jit(solution)/shard_map/second_steps/pallas_call | solution.py:33
  113.1 3.2 %regions.1 = f32[512,128]{1,0:T(8,128)} custom-call(s32[1]{0:T(128)} %bitcast.side, f32[12,32,128]{2,1,0:T(8,128)S(1)} %get-tuple-element.50.first_weights, f32[12,32,128]{2,1,0:T(8,128)S(1)} %get-tuple-element.51.second_weights, s32[32,256]{1,0:T(8,128)S(1)} %copy-done.9), custom_call_target="tpu_custom_call" | custom-call | tf_op jit(solution)/shard_map/regions/pallas_call | solution.py:33
  116.2 24.3 %all-to-all-start = ((f32[512,1,128]{2,1,0:T(1,128)}), f32[512,1,128]{2,1,0:T(1,128)S(1)}, u32[]{:S(2)}, u32[]{:S(2)}) async-start(f32[512,1,128]{2,1,0:T(1,128)} %bitcast.2), calls=%async_computation | async-start | bytes 524288 | tf_op jit(solution)/shard_map/all_to_all | solution.py:463
  140.6 8.3 %collective-permute-start.11 = (f32[2,8,32,128]{3,2,1,0:T(8,128)S(1)}, f32[2,8,32,128]{3,2,1,0:T(8,128)S(1)}, u32[]{:S(2)}, u32[]{:S(2)}) collective-permute-start(f32[2,8,32,128]{3,2,1,0:T(8,128)S(1)} %get-tuple-element.49), channel_id=1, source_target_pairs={{0,1},{1,0},{2,3},{3,2},{4,5},{5,4},{6,7},{7,6},{8,9},{9,8},{10,11... | collective-permute-start | bytes 786440 | tf_op jit(solution)/shard_map/ppermute | solution.py:57
  148.8 1.9 %collective-permute-start.10 = (f32[2,8,32,128]{3,2,1,0:T(8,128)S(1)}, f32[2,8,32,128]{3,2,1,0:T(8,128)S(1)}, u32[]{:S(2)}, u32[]{:S(2)}) collective-permute-start(f32[2,8,32,128]{3,2,1,0:T(8,128)S(1)} %get-tuple-element.48), channel_id=1, source_target_pairs={{0,1},{1,0},{2,3},{3,2},{4,5},{5,4},{6,7},{7,6},{8,9},{9,8},{10,11... | collective-permute-start | bytes 786440 | tf_op jit(solution)/shard_map/ppermute | solution.py:57
  150.8 18.9 %collective-permute-done.11.received1 = f32[2,8,32,128]{3,2,1,0:T(8,128)S(1)} collective-permute-done((f32[2,8,32,128]{3,2,1,0:T(8,128)S(1)}, f32[2,8,32,128]{3,2,1,0:T(8,128)S(1)}, u32[]{:S(2)}, u32[]{:S(2)}) %collective-permute-start.11) | collective-permute-done | bytes 262176 | tf_op jit(solution)/shard_map/ppermute | solution.py:57
  169.6 5.6 %collective-permute-done.10.received0 = f32[2,8,32,128]{3,2,1,0:T(8,128)S(1)} collective-permute-done((f32[2,8,32,128]{3,2,1,0:T(8,128)S(1)}, f32[2,8,32,128]{3,2,1,0:T(8,128)S(1)}, u32[]{:S(2)}, u32[]{:S(2)}) %collective-permute-start.10) | collective-permute-done | bytes 262176 | tf_op jit(solution)/shard_map/ppermute | solution.py:57
  175.3 1.0 join.1
  (34 shorter events, 3.9 us)
Async XLA Ops:
  0.6 0.7 copy-start.10
  1.3 1.2 copy-start
  2.5 0.9 copy-start.2
  3.4 0.9 copy-start.4
  4.4 0.9 copy-start.6
  5.3 29.0 %copy-start.1 = (f32[4,8,32,256]{3,2,1,0:T(8,128)S(1)}, f32[4,8,32,256]{3,2,1,0:T(8,128)}, u32[]{:S(2)}) copy-start(f32[4,8,32,256]{3,2,1,0:T(8,128)} %adjoint.7) | copy-start | bytes 3145732
  5.3 29.0 %copy-start.3 = (bf16[8,32,256]{2,1,0:T(8,128)(2,1)S(1)}, bf16[8,32,256]{2,1,0:T(8,128)(2,1)}, u32[]{:S(2)}) copy-start(bf16[8,32,256]{2,1,0:T(8,128)(2,1)} %lon_wind.5) | copy-start | bytes 393220
  5.3 29.0 %copy-start.5 = (bf16[8,32,256]{2,1,0:T(8,128)(2,1)S(1)}, bf16[8,32,256]{2,1,0:T(8,128)(2,1)}, u32[]{:S(2)}) copy-start(bf16[8,32,256]{2,1,0:T(8,128)(2,1)} %lat_wind.5) | copy-start | bytes 393220
  6.3 60.8 %collective-permute-start = (f32[46,32,128]{2,1,0:T(8,128)S(1)}, f32[46,32,128]{2,1,0:T(8,128)S(1)}, u32[]{:S(2)}, u32[]{:S(2)}) collective-permute-start(f32[46,32,128]{2,1,0:T(8,128)S(1)} %get-tuple-element.27), channel_id=1, source_target_pairs={{0,1},{1,0},{2,3},{3,2},{4,5},{5,4},{6,7},{7,6},{8,9},{9,8},{10,11... | collective-permute-start | bytes 2261000 | tf_op jit(solution)/shard_map/ppermute | solution.py:57
  16.0 18.2 %collective-permute-start.1 = (f32[7,32,128]{2,1,0:T(8,128)S(1)}, f32[7,32,128]{2,1,0:T(8,128)S(1)}, u32[]{:S(2)}, u32[]{:S(2)}) collective-permute-start(f32[7,32,128]{2,1,0:T(8,128)S(1)} %get-tuple-element.28.edge_other), channel_id=1, source_target_pairs={{0,16},{17,1},{16,32},{33,17},{32,48},{49,33},{48,64},{65,49},{64,... | collective-permute-start | bytes 344072 | tf_op jit(solution)/shard_map/ppermute | solution.py:57
  20.0 51.8 %collective-permute-start.7 = (f32[18,32,128]{2,1,0:T(8,128)S(1)}, f32[18,32,128]{2,1,0:T(8,128)S(1)}, u32[]{:S(2)}, u32[]{:S(2)}) collective-permute-start(f32[18,32,128]{2,1,0:T(8,128)S(1)} %get-tuple-element.37), channel_id=1, source_target_pairs={{0,1},{1,0},{2,3},{3,2},{4,5},{5,4},{6,7},{7,6},{8,9},{9,8},{10,11... | collective-permute-start | bytes 884744 | tf_op jit(solution)/shard_map/ppermute | solution.py:57
  34.3 41.5 %collective-permute-start.3 = (f32[63,8,128]{2,1,0:T(8,128)S(1)}, f32[63,8,128]{2,1,0:T(8,128)S(1)}, u32[]{:S(2)}, u32[]{:S(2)}) collective-permute-start(f32[63,8,128]{2,1,0:T(8,128)S(1)} %get-tuple-element.32), channel_id=1, source_target_pairs={{0,2},{2,4},{4,6},{6,8},{8,10},{10,12},{12,14},{1,3},{3,5},{5,7},{... | collective-permute-start | bytes 774152 | tf_op jit(solution)/shard_map/ppermute | solution.py:57
  37.5 29.6 %collective-permute-start.2 = (f32[7,32,128]{2,1,0:T(8,128)S(1)}, f32[7,32,128]{2,1,0:T(8,128)S(1)}, u32[]{:S(2)}, u32[]{:S(2)}) collective-permute-start(f32[7,32,128]{2,1,0:T(8,128)S(1)} %get-tuple-element.30), channel_id=1, source_target_pairs={{1,16},{16,1},{17,32},{32,17},{33,48},{48,33},{49,64},{64,49},{65,... | collective-permute-start | bytes 344072 | tf_op jit(solution)/shard_map/ppermute | solution.py:57
  60.9 16.2 %collective-permute-start.4 = (f32[63,8,128]{2,1,0:T(8,128)S(1)}, f32[63,8,128]{2,1,0:T(8,128)S(1)}, u32[]{:S(2)}, u32[]{:S(2)}) collective-permute-start(f32[63,8,128]{2,1,0:T(8,128)S(1)} %get-tuple-element.33), channel_id=1, source_target_pairs={{2,0},{4,2},{6,4},{8,6},{10,8},{12,10},{14,12},{3,1},{5,3},{7,5},{... | collective-permute-start | bytes 774152 | tf_op jit(solution)/shard_map/ppermute | solution.py:57
  67.1 10.0 %collective-permute-start.5 = (f32[45,8,128]{2,1,0:T(8,128)S(1)}, f32[45,8,128]{2,1,0:T(8,128)S(1)}, u32[]{:S(2)}, u32[]{:S(2)}) collective-permute-start(f32[45,8,128]{2,1,0:T(8,128)S(1)} %get-tuple-element.34), channel_id=1, source_target_pairs={{0,2},{2,4},{4,6},{6,8},{8,10},{10,12},{12,14},{1,3},{3,5},{5,7},{... | collective-permute-start | bytes 552968 | tf_op jit(solution)/shard_map/ppermute | solution.py:57
  70.3 6.8 %copy-start.7 = (bf16[8,32,256]{2,1,0:T(8,128)(2,1)S(1)}, bf16[8,32,256]{2,1,0:T(8,128)(2,1)}, u32[]{:S(2)}) copy-start(bf16[8,32,256]{2,1,0:T(8,128)(2,1)} %mixing.5) | copy-start | bytes 393220
  70.3 6.8 %copy-start.8 = (bf16[4,32,256]{2,1,0:T(8,128)(2,1)S(1)}, bf16[4,32,256]{2,1,0:T(8,128)(2,1)}, u32[]{:S(2)}) copy-start(bf16[4,32,256]{2,1,0:T(8,128)(2,1)} %prior.3) | copy-start | bytes 196612
  70.3 6.8 %collective-permute-start.6 = (f32[45,8,128]{2,1,0:T(8,128)S(1)}, f32[45,8,128]{2,1,0:T(8,128)S(1)}, u32[]{:S(2)}, u32[]{:S(2)}) collective-permute-start(f32[45,8,128]{2,1,0:T(8,128)S(1)} %get-tuple-element.35), channel_id=1, source_target_pairs={{2,0},{4,2},{6,4},{8,6},{10,8},{12,10},{14,12},{3,1},{5,3},{7,5},{... | collective-permute-start | bytes 552968 | tf_op jit(solution)/shard_map/ppermute | solution.py:57
  71.8 24.3 %collective-permute-start.8 = (f32[18,8,128]{2,1,0:T(8,128)S(1)}, f32[18,8,128]{2,1,0:T(8,128)S(1)}, u32[]{:S(2)}, u32[]{:S(2)}) collective-permute-start(f32[18,8,128]{2,1,0:T(8,128)S(1)} %get-tuple-element.39), channel_id=1, source_target_pairs={{0,2},{2,4},{4,6},{6,8},{8,10},{10,12},{12,14},{1,3},{3,5},{5,7},{... | collective-permute-start | bytes 221192 | tf_op jit(solution)/shard_map/ppermute | solution.py:57
  75.8 20.3 %collective-permute-start.9 = (f32[18,8,128]{2,1,0:T(8,128)S(1)}, f32[18,8,128]{2,1,0:T(8,128)S(1)}, u32[]{:S(2)}, u32[]{:S(2)}) collective-permute-start(f32[18,8,128]{2,1,0:T(8,128)S(1)} %get-tuple-element.40), channel_id=1, source_target_pairs={{2,0},{4,2},{6,4},{8,6},{10,8},{12,10},{14,12},{3,1},{5,3},{7,5},{... | collective-permute-start | bytes 221192 | tf_op jit(solution)/shard_map/ppermute | solution.py:57
  96.1 17.0 %copy-start.9 = (s32[32,256]{1,0:T(8,128)S(1)}, s32[32,256]{1,0:T(8,128)}, u32[]{:S(2)}) copy-start(s32[32,256]{1,0:T(8,128)} %ids.1) | copy-start | bytes 98308
  116.2 60.1 %all-to-all-start = ((f32[512,1,128]{2,1,0:T(1,128)}), f32[512,1,128]{2,1,0:T(1,128)S(1)}, u32[]{:S(2)}, u32[]{:S(2)}) async-start(f32[512,1,128]{2,1,0:T(1,128)} %bitcast.2), calls=%async_computation | async-start | bytes 524288 | tf_op jit(solution)/shard_map/all_to_all | solution.py:463
  140.6 29.1 %collective-permute-start.11 = (f32[2,8,32,128]{3,2,1,0:T(8,128)S(1)}, f32[2,8,32,128]{3,2,1,0:T(8,128)S(1)}, u32[]{:S(2)}, u32[]{:S(2)}) collective-permute-start(f32[2,8,32,128]{3,2,1,0:T(8,128)S(1)} %get-tuple-element.49), channel_id=1, source_target_pairs={{0,1},{1,0},{2,3},{3,2},{4,5},{5,4},{6,7},{7,6},{8,9},{9,8},{10,11... | collective-permute-start | bytes 786440 | tf_op jit(solution)/shard_map/ppermute | solution.py:57
  148.8 26.4 %collective-permute-start.10 = (f32[2,8,32,128]{3,2,1,0:T(8,128)S(1)}, f32[2,8,32,128]{3,2,1,0:T(8,128)S(1)}, u32[]{:S(2)}, u32[]{:S(2)}) collective-permute-start(f32[2,8,32,128]{3,2,1,0:T(8,128)S(1)} %get-tuple-element.48), channel_id=1, source_target_pairs={{0,1},{1,0},{2,3},{3,2},{4,5},{5,4},{6,7},{7,6},{8,9},{9,8},{10,11... | collective-permute-start | bytes 786440 | tf_op jit(solution)/shard_map/ppermute | solution.py:57

commit v4 on v2

--- a/solution.py
+++ b/solution.py
@@ -16,7 +16,6 @@
 TALL = ROWS + 2 * EDGE
 WIDE = 2 * HALF
 MAIN = FIELDS * HERE
-STRIP = 2 * MAIN + 2 * FIELDS
 HI = 256
 LO = 8
 SLOT = 32
@@ -68,7 +67,7 @@
     return ref[level, rows, lanes].astype(jnp.float32)
 
 
-def pack(side, injection, adjoint, lon_wind, lat_wind, mixing, to_partner, edge_mine, edge_other):
+def pack_edges(side, adjoint, lon_wind, lat_wind, mixing, edge_mine, edge_other):
     refs = (adjoint, lon_wind, lat_wind, mixing)
     k = side[0]
     mine = half_at(k)
@@ -82,49 +81,61 @@
             shift = (2 * EDGE * level + EDGE) % HALF
             plane_mine = own_plane(refs, field, level, rows, mine)
             plane_other = own_plane(refs, field, level, rows, other)
-            to_partner[field * HERE + level] = plane_other
             packed_mine = jnp.where(slot == level, pltpu.roll(plane_mine, shift, 1), packed_mine)
             packed_other = jnp.where(slot == level, pltpu.roll(plane_other, shift, 1), packed_other)
-        to_partner[MAIN + field] = packed_mine
         edge_mine[field] = packed_mine
         edge_other[field] = packed_other
-    for tracer in range(TRACERS):
-        for level in range(HERE):
-            row = tracer * HERE + level
-            to_partner[MAIN + FIELDS, row : row + 1, :] = jnp.full((1, HALF), injection[tracer, level], jnp.float32)
-
-
-def strips(side, adjoint, lon_wind, lat_wind, mixing, partner, edge_other, lon_same, lon_cross, first, last, edges):
+
+
+def pack_main(side, injection, adjoint, lon_wind, lat_wind, mixing, edge_mine, edge_other, to_partner, first, last):
     refs = (adjoint, lon_wind, lat_wind, mixing)
     k = side[0]
     mine = half_at(k)
+    other = half_at(1 - k)
+    rows = slice(0, ROWS)
     head = slice(0, EDGE)
     tail = slice(ROWS - EDGE, ROWS)
     for field in range(FIELDS):
         for level in range(HERE):
             at = field * HERE + level
-            if field < TRACERS:
-                first[at] = adjoint[field, level, head, mine]
-                last[at] = adjoint[field, level, tail, mine]
-            else:
-                plane = own_plane(refs, field, level, slice(0, ROWS), mine)
-                first[at] = plane[head]
-                last[at] = plane[tail]
-    first[MAIN : 2 * MAIN] = partner[0:MAIN, head, :]
-    last[MAIN : 2 * MAIN] = partner[0:MAIN, tail, :]
-    lane = lax.broadcasted_iota(jnp.int32, (ROWS, HALF), 1)
-    inner = ((lane // EDGE) % 2) != k
+            to_partner[at] = own_plane(refs, field, level, rows, other)
+            plane = own_plane(refs, field, level, rows, mine)
+            first[at] = plane[head]
+            last[at] = plane[tail]
+        to_partner[MAIN + field] = edge_mine[field]
+        first[MAIN + field] = edge_other[field, head]
+        last[MAIN + field] = edge_other[field, tail]
+    for tracer in range(TRACERS):
+        for level in range(HERE):
+            row = tracer * HERE + level
+            to_partner[MAIN + FIELDS, row : row + 1, :] = jnp.broadcast_to(
+                injection[tracer : tracer + 1, level : level + 1], (1, HALF)
+            )
+
+
+def inner_lanes(side, rows):
+    lane = lax.broadcasted_iota(jnp.int32, (rows, HALF), 1)
+    return ((lane // EDGE) % 2) != side[0]
+
+
+def strips(side, partner, lon_same, lon_cross, own_below, own_above, first, last, edges):
+    head = slice(0, EDGE)
+    tail = slice(ROWS - EDGE, ROWS)
+    inner = inner_lanes(side, ROWS)
+    first[0:MAIN] = partner[0:MAIN, head, :]
+    last[0:MAIN] = partner[0:MAIN, tail, :]
     for field in range(FIELDS):
-        for group, near, far in ((0, edge_other[field], lon_same[field]), (1, partner[MAIN + field], lon_cross[field])):
-            merged = jnp.where(inner, near, far)
-            at = group * FIELDS + field
-            edges[at] = merged
-            first[2 * MAIN + at] = merged[head]
-            last[2 * MAIN + at] = merged[tail]
+        merged = jnp.where(inner, partner[MAIN + field], lon_cross[field])
+        edges[field] = merged
+        first[MAIN + field] = merged[head]
+        last[MAIN + field] = merged[tail]
+        first[MAIN + FIELDS + field] = lon_same[field, head]
+        last[MAIN + FIELDS + field] = lon_same[field, tail]
 
 
 def steps(
-    side, injection, adjoint, lon_wind, lat_wind, mixing, partner, edges, below, above, prior,
+    side, injection, adjoint, lon_wind, lat_wind, mixing, partner, edge_other, lon_same, edges,
+    own_below, own_above, below, above, prior,
     kept, returned, weights,
     field_ref, lon_ref, lat_ref, kab_ref, inv_ref, cp_ref, red_ref, inj_ref,
 ):
@@ -138,32 +149,45 @@
     main = slice(0, HALF)
     wing = slice(HALF, WIDE)
 
+    inner = inner_lanes(side, ROWS)
+    inner_rim = inner_lanes(side, EDGE)
     for group in range(2):
         base = (k if group == 0 else 1 - k) * HERE
-        for level in range(HERE):
-            shift = (HALF - (2 * EDGE * level + EDGE)) % HALF
-            for field in range(FIELDS):
+        under, over = (own_below, own_above) if group == 0 else (below, above)
+        for field in range(FIELDS):
+            rim = MAIN + field
+            if group == 0:
+                far = MAIN + FIELDS + field
+                edge = (
+                    jnp.where(inner_rim, own_below[rim], below[far]),
+                    jnp.where(inner, edge_other[field], lon_same[field]),
+                    jnp.where(inner_rim, own_above[rim], above[far]),
+                )
+            else:
+                edge = (below[rim], edges[field], above[rim])
+            for level in range(HERE):
+                shift = (HALF - (2 * EDGE * level + EDGE)) % HALF
                 at = field * HERE + level
-                plane_at = group * MAIN + at
-                edge_at = group * FIELDS + field
                 where = base + level
                 if field < TRACERS:
                     target = field_ref.at[field, where]
                 else:
                     target = (lon_ref, lat_ref, kab_ref)[field - TRACERS].at[where]
-                target[low, main] = below[plane_at]
-                target[top, main] = above[plane_at]
+                target[low, main] = under[at]
+                target[top, main] = over[at]
                 if group == 0:
                     target[mid, main] = own_plane(refs, field, level, rows, mine)
                 else:
                     target[mid, main] = partner[at]
-                target[low, wing] = pltpu.roll(below[2 * MAIN + edge_at], shift, 1)
-                target[mid, wing] = pltpu.roll(edges[edge_at], shift, 1)
-                target[top, wing] = pltpu.roll(above[2 * MAIN + edge_at], shift, 1)
+                target[low, wing] = pltpu.roll(edge[0], shift, 1)
+                target[mid, wing] = pltpu.roll(edge[1], shift, 1)
+                target[top, wing] = pltpu.roll(edge[2], shift, 1)
     for tracer in range(TRACERS):
         for level in range(HERE):
             row = tracer * HERE + level
-            inj_ref[tracer, pl.ds(k * HERE + level, 1)] = jnp.full((1, 8, HALF), injection[tracer, level], jnp.float32)
+            inj_ref[tracer, pl.ds(k * HERE + level, 1)] = jnp.broadcast_to(
+                injection[tracer : tracer + 1, level : level + 1][None], (1, 8, HALF)
+            )
             inj_ref[tracer, pl.ds((1 - k) * HERE + level, 1)] = jnp.broadcast_to(
                 partner[MAIN + FIELDS, row : row + 1, :][None], (1, 8, HALF)
             )
@@ -287,13 +311,14 @@
     lon_count = lax.axis_size("lon")
     lat_count = lax.axis_size("lat")
     side = lax.axis_index("lev").astype(jnp.int32).reshape(1)
-    own = (adjoint, courant_lon, courant_lat, mixing)
-
-    to_partner, edge_mine, edge_other = call(
-        pack,
-        (near(MAIN + FIELDS + 1, ROWS, HALF), near(FIELDS, ROWS, HALF), near(FIELDS, ROWS, HALF)),
-        (side, injection, *own),
-        2,
+    raw = tuple(
+        pltpu.with_memory_space_constraint(x, pltpu.HBM) for x in (adjoint, courant_lon, courant_lat, mixing)
+    )
+    own = tuple(hold(x) for x in (adjoint, courant_lon, courant_lat, mixing))
+    injection = hold(injection)
+
+    edge_mine, edge_other = call(
+        pack_edges, (near(FIELDS, ROWS, HALF), near(FIELDS, ROWS, HALF)), (side, *raw), 1
     )
     same = []
     cross = []
@@ -301,19 +326,31 @@
         after = (i + 1) % lon_count
         same += [(2 * i, 2 * after), (2 * after + 1, 2 * i + 1)]
         cross += [(2 * i + 1, 2 * after), (2 * after, 2 * i + 1)]
+    north = [(j, j + 1) for j in range(lat_count - 1)]
+    south = [(j + 1, j) for j in range(lat_count - 1)]
+    lon_cross = permute(edge_mine, ("lon", "lev"), cross)
     lon_same = permute(edge_other, ("lon", "lev"), same)
-    lon_cross = permute(edge_mine, ("lon", "lev"), cross)
-
+
+    strip = MAIN + FIELDS
+    to_partner, first, last = call(
+        pack_main,
+        (near(MAIN + FIELDS + 1, ROWS, HALF), near(strip, EDGE, HALF), near(strip, EDGE, HALF)),
+        (side, injection, *own, edge_mine, edge_other),
+        1,
+    )
     partner = permute(to_partner, "lev", [(0, 1), (1, 0)])
-
+    own_below = permute(last, "lat", north)
+    own_above = permute(first, "lat", south)
+
+    strip = MAIN + 2 * FIELDS
     first, last, edges = call(
         strips,
-        (near(STRIP, EDGE, HALF), near(STRIP, EDGE, HALF), near(2 * FIELDS, ROWS, HALF)),
-        (side, *own, partner, edge_other, lon_same, lon_cross),
+        (near(strip, EDGE, HALF), near(strip, EDGE, HALF), near(FIELDS, ROWS, HALF)),
+        (side, partner, lon_same, lon_cross, own_below, own_above),
         1,
     )
-    below = permute(last, "lat", [(j, j + 1) for j in range(lat_count - 1)])
-    above = permute(first, "lat", [(j + 1, j) for j in range(lat_count - 1)])
+    below = permute(last, "lat", north)
+    above = permute(first, "lat", south)
 
     block = (LEVELS, TALL, WIDE)
     kept, returned, weights = call(
@@ -323,8 +360,11 @@
             near(TRACERS, HERE, ROWS, HALF),
             near(STEPS * TRACERS, ROWS, HALF),
         ),
-        (side, injection, *own, partner, edges, below, above, prior_flux),
-        2,
+        (
+            side, injection, *own, partner, edge_other, lon_same, edges,
+            own_below, own_above, below, above, hold(prior_flux),
+        ),
+        1,
         [
             pltpu.VMEM((TRACERS, *block), jnp.float32),
             pltpu.VMEM(block, jnp.float32),

time: 159 us -> 151 us (0.950)
  waiting for transfers between devices: 27.5 us -> 21 us
  local copies, waits for them, and re-layouts: 5.3 us -> 1.33 us
  starting transfers between devices: 55.1 us -> 59 us
  blocking collectives: 38.3 us -> 35.9 us
    ppermute x6 -> x8, waiting for transfers between devices: 27.5 us -> 21 us  [permute(): return hold(lax.ppermute(x, axes, pairs))]
    unnamed x22 -> x14, local copies, waits for them, and re-layouts: 4.63 us -> 0.66 us
    ppermute x6 -> x8, starting transfers between devices: 55.1 us -> 59 us  [permute(): return hold(lax.ppermute(x, axes, pairs))]
    all_to_all x1, blocking collectives: 38.3 us -> 35.9 us  [body(): pieces = lax.all_to_all(sums, ('lon', 'lat', 'lev'), 0, 0, tiled=True)]
    pallas_call x5 -> x6, Pallas kernels: 31.3 us -> 31.5 us  [call(): pl.pallas_call(kernel, out_shape=out_shape, in_specs=specs, out_specs=tup...]
  transfers between devices with their start and end apart: 6 -> 8, of which waited for: 4 -> 4; matrix products, arithmetic and copies ran while one was open for 1% -> 1% of each run, Pallas kernels for 2% -> 2%
where the time goes in v4:
time: 151 us; the launch traced here: 150 us
  starting transfers between devices  59 us (39%)
  blocking collectives  35.9 us (24%)
  Pallas kernels  31.5 us (21%)
  waiting for transfers between devices  21 us (14%)
    ppermute x8, starting transfers between devices, permute(): return hold(lax.ppermute(x, axes, pairs))  59 us
    all_to_all x1, blocking collectives, body(): pieces = lax.all_to_all(sums, ('lon', 'lat', 'lev'), 0, 0, tiled=True)  35.9 us
    pallas_call x6, Pallas kernels, call(): pl.pallas_call(kernel, out_shape=out_shape, in_specs=specs, out_specs=tup...  31.5 us
    ppermute x8, waiting for transfers between devices, permute(): return hold(lax.ppermute(x, axes, pairs))  21 us
  transfers between devices with their start and end apart: 8, of which 4 were waited for; matrix products, arithmetic and copies ran while one was open for 1% of the time, Pallas kernels for 2%

profile of v4, /device:TPU:1, one launch (start us, length us, event | category | flops | bytes accessed | tf_op | source)
XLA Modules:
  0.0 150.1 jit_solution(2942048452577852752)
XLA Ops:
  0.7 1.9 %pack_edges.1 = (f32[7,32,128]{2,1,0:T(8,128)S(1)}, f32[7,32,128]{2,1,0:T(8,128)S(1)}) custom-call(s32[1]{0:T(128)} %bitcast.side, f32[4,8,32,256]{3,2,1,0:T(8,128)} %adjoint.5, bf16[8,32,256]{2,1,0:T(8,128)(2,1)} %lon_wind.5, bf16[8,32,256]{2,1,0:T(8,128)(2,1)} %lat_wind.5, bf16[8,32,256]{2,1,0:T(8,128)(2,1)} %mixing.5), custom_call_target="tpu_custom_call" | custom-call | tf_op jit(solution)/shard_map/pack_edges/pallas_call | solution.py:31
  2.5 0.0 copy-start.6
  2.6 0.6 copy-done.6
  3.2 0.1 pack_main.1
  3.4 11.5 %collective-permute-start = (f32[64,32,128]{2,1,0:T(8,128)S(1)}, f32[64,32,128]{2,1,0:T(8,128)S(1)}, u32[]{:S(2)}, u32[]{:S(2)}) collective-permute-start(f32[64,32,128]{2,1,0:T(8,128)S(1)} %get-tuple-element.15), channel_id=1, source_target_pairs={{0,1},{1,0},{2,3},{3,2},{4,5},{5,4},{6,7},{7,6},{8,9},{9,8},{10,11... | collective-permute-start | bytes 3145736 | tf_op jit(solution)/shard_map/ppermute | solution.py:55
  14.8 3.2 %collective-permute-start.3 = (f32[63,8,128]{2,1,0:T(8,128)S(1)}, f32[63,8,128]{2,1,0:T(8,128)S(1)}, u32[]{:S(2)}, u32[]{:S(2)}) collective-permute-start(f32[63,8,128]{2,1,0:T(8,128)S(1)} %get-tuple-element.16), channel_id=1, source_target_pairs={{0,2},{2,4},{4,6},{6,8},{8,10},{10,12},{12,14},{1,3},{3,5},{5,7},{... | collective-permute-start | bytes 774152 | tf_op jit(solution)/shard_map/ppermute | solution.py:55
  18.1 0.0 copy-start.4
  18.1 1.4 collective-permute-start.4
  19.5 2.9 %collective-permute-start.2 = (f32[7,32,128]{2,1,0:T(8,128)S(1)}, f32[7,32,128]{2,1,0:T(8,128)S(1)}, u32[]{:S(2)}, u32[]{:S(2)}) collective-permute-start(f32[7,32,128]{2,1,0:T(8,128)S(1)} %get-tuple-element.13.edge_mine), channel_id=1, source_target_pairs={{1,16},{16,1},{17,32},{32,17},{33,48},{48,33},{49,64},{64,49},{65,... | collective-permute-start | bytes 344072 | tf_op jit(solution)/shard_map/ppermute | solution.py:55
  22.4 3.3 %collective-permute-start.1 = (f32[7,32,128]{2,1,0:T(8,128)S(1)}, f32[7,32,128]{2,1,0:T(8,128)S(1)}, u32[]{:S(2)}, u32[]{:S(2)}) collective-permute-start(f32[7,32,128]{2,1,0:T(8,128)S(1)} %get-tuple-element.14.edge_other), channel_id=1, source_target_pairs={{0,16},{17,1},{16,32},{33,17},{32,48},{49,33},{48,64},{65,49},{64,... | collective-permute-start | bytes 344072 | tf_op jit(solution)/shard_map/ppermute | solution.py:55
  25.7 14.2 %collective-permute-done.2.lon_cross = f32[7,32,128]{2,1,0:T(8,128)S(1)} collective-permute-done((f32[7,32,128]{2,1,0:T(8,128)S(1)}, f32[7,32,128]{2,1,0:T(8,128)S(1)}, u32[]{:S(2)}, u32[]{:S(2)}) %collective-permute-start.2) | collective-permute-done | bytes 114720 | tf_op jit(solution)/shard_map/ppermute | solution.py:55
  39.9 0.7 collective-permute-done.1.lon_same
  40.6 0.1 strips.1
  40.7 3.2 %collective-permute-start.5 = (f32[70,8,128]{2,1,0:T(8,128)S(1)}, f32[70,8,128]{2,1,0:T(8,128)S(1)}, u32[]{:S(2)}, u32[]{:S(2)}) collective-permute-start(f32[70,8,128]{2,1,0:T(8,128)S(1)} %get-tuple-element.19), channel_id=1, source_target_pairs={{0,2},{2,4},{4,6},{6,8},{8,10},{10,12},{12,14},{1,3},{3,5},{5,7},{... | collective-permute-start | bytes 860168 | tf_op jit(solution)/shard_map/ppermute | solution.py:55
  43.9 1.3 collective-permute-start.6
  45.2 2.2 %collective-permute-done.5.below = f32[70,8,128]{2,1,0:T(8,128)S(1)} collective-permute-done((f32[70,8,128]{2,1,0:T(8,128)S(1)}, f32[70,8,128]{2,1,0:T(8,128)S(1)}, u32[]{:S(2)}, u32[]{:S(2)}) %collective-permute-start.5) | collective-permute-done | bytes 286752 | tf_op jit(solution)/shard_map/ppermute | solution.py:55
  47.4 3.8 %collective-permute-done.6.above = f32[70,8,128]{2,1,0:T(8,128)S(1)} collective-permute-done((f32[70,8,128]{2,1,0:T(8,128)S(1)}, f32[70,8,128]{2,1,0:T(8,128)S(1)}, u32[]{:S(2)}, u32[]{:S(2)}) %collective-permute-start.6) | collective-permute-done | bytes 286752 | tf_op jit(solution)/shard_map/ppermute | solution.py:55
  51.3 26.0 %steps.1 = (f32[4,8,32,128]{3,2,1,0:T(8,128)S(1)}, f32[4,8,32,128]{3,2,1,0:T(8,128)S(1)}, f32[24,32,128]{2,1,0:T(8,128)S(1)}) custom-call(s32[1]{0:T(128)} %bitcast.side, f32[4,8]{1,0:T(4,128)S(1)} %copy-done.6, f32[4,8,32,256]{3,2,1,0:T(8,128)S(1)} %copy-done, bf16[8,32,256]{2,1,0:T(8,128)(2,1)S(1)} %copy-done.1, bf16[8,32,256]{2,1,0:T(8,128)(2,1)S(1)} %copy-done.2, ...), custom_call_target="tpu_custom_call" | custom-call | tf_op jit(solution)/shard_map/steps/pallas_call | solution.py:31
  77.3 32.3 %collective-permute-start.7 = (f32[4,8,32,128]{3,2,1,0:T(8,128)S(1)}, f32[4,8,32,128]{3,2,1,0:T(8,128)S(1)}, u32[]{:S(2)}, u32[]{:S(2)}) collective-permute-start(f32[4,8,32,128]{3,2,1,0:T(8,128)S(1)} %get-tuple-element.22), channel_id=1, source_target_pairs={{0,1},{1,0},{2,3},{3,2},{4,5},{5,4},{6,7},{7,6},{8,9},{9,8},{10,11... | collective-permute-start | bytes 1572872 | tf_op jit(solution)/shard_map/ppermute | solution.py:55
  109.6 2.4 %regions.1 = f32[512,128]{1,0:T(8,128)S(1)} custom-call(s32[1]{0:T(128)} %bitcast.side, f32[24,32,128]{2,1,0:T(8,128)S(1)} %get-tuple-element.23.weights, s32[32,256]{1,0:T(8,128)S(1)} %copy-done.5), custom_call_target="tpu_custom_call" | custom-call | tf_op jit(solution)/shard_map/regions/pallas_call | solution.py:31
  112.0 35.9 %all_to_all.9 = f32[512,1,128]{2,1,0:T(1,128)S(1)} all-to-all(f32[512,1,128]{2,1,0:T(1,128)S(1)} %bitcast.5), channel_id=1, replica_groups=mesh['lon'=32,'lat'=8,'lev'=2] {'lon','lat','lev'}, dimensions={0} | all-to-all | bytes 524288 | tf_op jit(solution)/shard_map/all_to_all | solution.py:389
  147.8 0.6 reduce_sum.9
  148.4 0.7 reshape.13
  149.1 1.0 join.1
  (15 shorter events, 0.0 us)
Async XLA Ops:
  0.6 1.9 %copy-start = (f32[4,8,32,256]{3,2,1,0:T(8,128)S(1)}, f32[4,8,32,256]{3,2,1,0:T(8,128)}, u32[]{:S(2)}) copy-start(f32[4,8,32,256]{3,2,1,0:T(8,128)} %adjoint.5) | copy-start | bytes 3145732
  0.6 1.9 %copy-start.1 = (bf16[8,32,256]{2,1,0:T(8,128)(2,1)S(1)}, bf16[8,32,256]{2,1,0:T(8,128)(2,1)}, u32[]{:S(2)}) copy-start(bf16[8,32,256]{2,1,0:T(8,128)(2,1)} %lon_wind.5) | copy-start | bytes 393220
  0.7 1.9 %copy-start.2 = (bf16[8,32,256]{2,1,0:T(8,128)(2,1)S(1)}, bf16[8,32,256]{2,1,0:T(8,128)(2,1)}, u32[]{:S(2)}) copy-start(bf16[8,32,256]{2,1,0:T(8,128)(2,1)} %lat_wind.5) | copy-start | bytes 393220
  0.7 1.9 %copy-start.3 = (bf16[8,32,256]{2,1,0:T(8,128)(2,1)S(1)}, bf16[8,32,256]{2,1,0:T(8,128)(2,1)}, u32[]{:S(2)}) copy-start(bf16[8,32,256]{2,1,0:T(8,128)(2,1)} %mixing.5) | copy-start | bytes 393220
  2.5 0.7 copy-start.6
  3.4 37.2 %collective-permute-start = (f32[64,32,128]{2,1,0:T(8,128)S(1)}, f32[64,32,128]{2,1,0:T(8,128)S(1)}, u32[]{:S(2)}, u32[]{:S(2)}) collective-permute-start(f32[64,32,128]{2,1,0:T(8,128)S(1)} %get-tuple-element.15), channel_id=1, source_target_pairs={{0,1},{1,0},{2,3},{3,2},{4,5},{5,4},{6,7},{7,6},{8,9},{9,8},{10,11... | collective-permute-start | bytes 3145736 | tf_op jit(solution)/shard_map/ppermute | solution.py:55
  14.8 25.8 %collective-permute-start.3 = (f32[63,8,128]{2,1,0:T(8,128)S(1)}, f32[63,8,128]{2,1,0:T(8,128)S(1)}, u32[]{:S(2)}, u32[]{:S(2)}) collective-permute-start(f32[63,8,128]{2,1,0:T(8,128)S(1)} %get-tuple-element.16), channel_id=1, source_target_pairs={{0,2},{2,4},{4,6},{6,8},{8,10},{10,12},{12,14},{1,3},{3,5},{5,7},{... | collective-permute-start | bytes 774152 | tf_op jit(solution)/shard_map/ppermute | solution.py:55
  18.1 33.2 %copy-start.4 = (bf16[4,32,256]{2,1,0:T(8,128)(2,1)S(1)}, bf16[4,32,256]{2,1,0:T(8,128)(2,1)}, u32[]{:S(2)}) copy-start(bf16[4,32,256]{2,1,0:T(8,128)(2,1)} %prior.1) | copy-start | bytes 196612
  18.1 22.5 %collective-permute-start.4 = (f32[63,8,128]{2,1,0:T(8,128)S(1)}, f32[63,8,128]{2,1,0:T(8,128)S(1)}, u32[]{:S(2)}, u32[]{:S(2)}) collective-permute-start(f32[63,8,128]{2,1,0:T(8,128)S(1)} %get-tuple-element.17), channel_id=1, source_target_pairs={{2,0},{4,2},{6,4},{8,6},{10,8},{12,10},{14,12},{3,1},{5,3},{7,5},{... | collective-permute-start | bytes 774152 | tf_op jit(solution)/shard_map/ppermute | solution.py:55
  19.5 20.4 %collective-permute-start.2 = (f32[7,32,128]{2,1,0:T(8,128)S(1)}, f32[7,32,128]{2,1,0:T(8,128)S(1)}, u32[]{:S(2)}, u32[]{:S(2)}) collective-permute-start(f32[7,32,128]{2,1,0:T(8,128)S(1)} %get-tuple-element.13.edge_mine), channel_id=1, source_target_pairs={{1,16},{16,1},{17,32},{32,17},{33,48},{48,33},{49,64},{64,49},{65,... | collective-permute-start | bytes 344072 | tf_op jit(solution)/shard_map/ppermute | solution.py:55
  22.4 18.2 %collective-permute-start.1 = (f32[7,32,128]{2,1,0:T(8,128)S(1)}, f32[7,32,128]{2,1,0:T(8,128)S(1)}, u32[]{:S(2)}, u32[]{:S(2)}) collective-permute-start(f32[7,32,128]{2,1,0:T(8,128)S(1)} %get-tuple-element.14.edge_other), channel_id=1, source_target_pairs={{0,16},{17,1},{16,32},{33,17},{32,48},{49,33},{48,64},{65,49},{64,... | collective-permute-start | bytes 344072 | tf_op jit(solution)/shard_map/ppermute | solution.py:55
  40.7 6.8 %collective-permute-start.5 = (f32[70,8,128]{2,1,0:T(8,128)S(1)}, f32[70,8,128]{2,1,0:T(8,128)S(1)}, u32[]{:S(2)}, u32[]{:S(2)}) collective-permute-start(f32[70,8,128]{2,1,0:T(8,128)S(1)} %get-tuple-element.19), channel_id=1, source_target_pairs={{0,2},{2,4},{4,6},{6,8},{8,10},{10,12},{12,14},{1,3},{3,5},{5,7},{... | collective-permute-start | bytes 860168 | tf_op jit(solution)/shard_map/ppermute | solution.py:55
  43.9 7.4 %collective-permute-start.6 = (f32[70,8,128]{2,1,0:T(8,128)S(1)}, f32[70,8,128]{2,1,0:T(8,128)S(1)}, u32[]{:S(2)}, u32[]{:S(2)}) collective-permute-start(f32[70,8,128]{2,1,0:T(8,128)S(1)} %get-tuple-element.20), channel_id=1, source_target_pairs={{2,0},{4,2},{6,4},{8,6},{10,8},{12,10},{14,12},{3,1},{5,3},{7,5},{... | collective-permute-start | bytes 860168 | tf_op jit(solution)/shard_map/ppermute | solution.py:55
  51.3 58.3 %copy-start.5 = (s32[32,256]{1,0:T(8,128)S(1)}, s32[32,256]{1,0:T(8,128)}, u32[]{:S(2)}) copy-start(s32[32,256]{1,0:T(8,128)} %ids.1) | copy-start | bytes 98308
  77.3 71.8 %collective-permute-start.7 = (f32[4,8,32,128]{3,2,1,0:T(8,128)S(1)}, f32[4,8,32,128]{3,2,1,0:T(8,128)S(1)}, u32[]{:S(2)}, u32[]{:S(2)}) collective-permute-start(f32[4,8,32,128]{3,2,1,0:T(8,128)S(1)} %get-tuple-element.22), channel_id=1, source_target_pairs={{0,1},{1,0},{2,3},{3,2},{4,5},{5,4},{6,7},{7,6},{8,9},{9,8},{10,11... | collective-permute-start | bytes 1572872 | tf_op jit(solution)/shard_map/ppermute | solution.py:55

commit v5 on v4

--- a/solution.py
+++ b/solution.py
@@ -16,6 +16,8 @@
 TALL = ROWS + 2 * EDGE
 WIDE = 2 * HALF
 MAIN = FIELDS * HERE
+FOLD = 2 * EDGE
+PLANES = MAIN + (FIELDS + 1) // 2 + 1
 HI = 256
 LO = 8
 SLOT = 32
@@ -25,7 +27,7 @@
 MIB = 1024 * 1024
 
 
-def call(kernel, out_shape, operands, scalars, scratch=(), limit=8):
+def call(kernel, out_shape, operands, scalars, scratch=(), limit=8, work=0):
     specs = [SMEM] * scalars + [VMEM] * (len(operands) - scalars)
     many = isinstance(out_shape, (tuple, list))
     return pl.pallas_call(
@@ -36,6 +38,7 @@
         scratch_shapes=list(scratch),
         compiler_params=pltpu.CompilerParams(vmem_limit_bytes=limit * MIB),
         name=kernel.__name__,
+        cost_estimate=pl.CostEstimate(flops=work, bytes_accessed=work, transcendentals=0) if work else None,
     )(*operands)
 
 
@@ -67,74 +70,78 @@
     return ref[level, rows, lanes].astype(jnp.float32)
 
 
-def pack_edges(side, adjoint, lon_wind, lat_wind, mixing, edge_mine, edge_other):
+def pack_edges(side, adjoint, lon_wind, lat_wind, mixing, inner, cross, same, near):
     refs = (adjoint, lon_wind, lat_wind, mixing)
     k = side[0]
     mine = half_at(k)
     other = half_at(1 - k)
-    rows = slice(0, ROWS)
-    slot = lax.broadcasted_iota(jnp.int32, (ROWS, HALF), 1) // (2 * EDGE)
+    slot = lax.broadcasted_iota(jnp.int32, (FOLD, HALF), 1) // EDGE
+    upper = slice(0, FOLD)
+    lower = slice(FOLD, ROWS)
+    west = k == 0
+
+    def packed(planes, begin):
+        out = jnp.zeros((FOLD, HALF), jnp.float32)
+        for level, plane in enumerate(planes):
+            for rows, to in ((upper, level), (lower, HERE + level)):
+                shift = (EDGE * to - begin) % HALF
+                moved = pltpu.roll(plane[rows], shift, 1) if shift else plane[rows]
+                out = jnp.where(slot == to, moved, out)
+        return out
+
     for field in range(FIELDS):
-        packed_mine = jnp.zeros((ROWS, HALF), jnp.float32)
-        packed_other = jnp.zeros((ROWS, HALF), jnp.float32)
-        for level in range(HERE):
-            shift = (2 * EDGE * level + EDGE) % HALF
-            plane_mine = own_plane(refs, field, level, rows, mine)
-            plane_other = own_plane(refs, field, level, rows, other)
-            packed_mine = jnp.where(slot == level, pltpu.roll(plane_mine, shift, 1), packed_mine)
-            packed_other = jnp.where(slot == level, pltpu.roll(plane_other, shift, 1), packed_other)
-        edge_mine[field] = packed_mine
-        edge_other[field] = packed_other
-
-
-def pack_main(side, injection, adjoint, lon_wind, lat_wind, mixing, edge_mine, edge_other, to_partner, first, last):
+        planes = [own_plane(refs, field, level, slice(0, ROWS), mine) for level in range(HERE)]
+        low = packed(planes, 0)
+        high = packed(planes, HALF - EDGE)
+        inner[field] = jnp.where(west, high, low)
+        cross[field] = jnp.where(west, low, high)
+        planes = [own_plane(refs, field, level, slice(0, ROWS), other) for level in range(HERE)]
+        low = packed(planes, 0)
+        high = packed(planes, HALF - EDGE)
+        same[field] = jnp.where(west, high, low)
+        near[field] = jnp.where(west, low, high)
+
+
+def pack_main(side, injection, adjoint, lon_wind, lat_wind, mixing, inner, to_partner):
     refs = (adjoint, lon_wind, lat_wind, mixing)
-    k = side[0]
-    mine = half_at(k)
-    other = half_at(1 - k)
-    rows = slice(0, ROWS)
-    head = slice(0, EDGE)
-    tail = slice(ROWS - EDGE, ROWS)
+    other = half_at(1 - side[0])
     for field in range(FIELDS):
         for level in range(HERE):
-            at = field * HERE + level
-            to_partner[at] = own_plane(refs, field, level, rows, other)
-            plane = own_plane(refs, field, level, rows, mine)
-            first[at] = plane[head]
-            last[at] = plane[tail]
-        to_partner[MAIN + field] = edge_mine[field]
-        first[MAIN + field] = edge_other[field, head]
-        last[MAIN + field] = edge_other[field, tail]
+            to_partner[field * HERE + level] = own_plane(refs, field, level, slice(0, ROWS), other)
+        to_partner[MAIN + field // 2, pl.ds(field % 2 * FOLD, FOLD), :] = inner[field]
     for tracer in range(TRACERS):
         for level in range(HERE):
             row = tracer * HERE + level
-            to_partner[MAIN + FIELDS, row : row + 1, :] = jnp.broadcast_to(
+            to_partner[PLANES - 1, row : row + 1, :] = jnp.broadcast_to(
                 injection[tracer : tracer + 1, level : level + 1], (1, HALF)
             )
 
 
-def inner_lanes(side, rows):
-    lane = lax.broadcasted_iota(jnp.int32, (rows, HALF), 1)
-    return ((lane // EDGE) % 2) != side[0]
-
-
-def strips(side, partner, lon_same, lon_cross, own_below, own_above, first, last, edges):
-    head = slice(0, EDGE)
-    tail = slice(ROWS - EDGE, ROWS)
-    inner = inner_lanes(side, ROWS)
-    first[0:MAIN] = partner[0:MAIN, head, :]
-    last[0:MAIN] = partner[0:MAIN, tail, :]
+def own_strips(side, adjoint, lon_wind, lat_wind, mixing, near, lon_same, lon_cross, first, last):
+    refs = (adjoint, lon_wind, lat_wind, mixing)
+    mine = half_at(side[0])
     for field in range(FIELDS):
-        merged = jnp.where(inner, partner[MAIN + field], lon_cross[field])
-        edges[field] = merged
-        first[MAIN + field] = merged[head]
-        last[MAIN + field] = merged[tail]
-        first[MAIN + FIELDS + field] = lon_same[field, head]
-        last[MAIN + FIELDS + field] = lon_same[field, tail]
+        for level in range(HERE):
+            plane = own_plane(refs, field, level, slice(0, ROWS), mine)
+            first[field * HERE + level] = plane[:EDGE]
+            last[field * HERE + level] = plane[ROWS - EDGE :]
+    for group, rims in enumerate((near, lon_same, lon_cross)):
+        at = slice(MAIN + group * FIELDS, MAIN + (group + 1) * FIELDS)
+        first[at] = rims[:, :EDGE, :]
+        last[at] = rims[:, EDGE:, :]
+
+
+def strips(partner, own_below, own_above, first, last):
+    first[0:MAIN] = partner[0:MAIN, 0:EDGE, :]
+    last[0:MAIN] = partner[0:MAIN, ROWS - EDGE : ROWS, :]
+    for field in range(FIELDS):
+        begin = field % 2 * FOLD
+        first[MAIN + field] = partner[MAIN + field // 2, begin : begin + EDGE, :]
+        last[MAIN + field] = partner[MAIN + field // 2, begin + EDGE : begin + FOLD, :]
 
 
 def steps(
-    side, injection, adjoint, lon_wind, lat_wind, mixing, partner, edge_other, lon_same, edges,
+    side, injection, adjoint, lon_wind, lat_wind, mixing, partner, near, lon_same, lon_cross,
     own_below, own_above, below, above, prior,
     kept, returned, weights,
     field_ref, lon_ref, lat_ref, kab_ref, inv_ref, cp_ref, red_ref, inj_ref,
@@ -149,24 +156,32 @@
     main = slice(0, HALF)
     wing = slice(HALF, WIDE)
 
-    inner = inner_lanes(side, ROWS)
-    inner_rim = inner_lanes(side, EDGE)
+    west = k == 0
+    lane = lax.broadcasted_iota(jnp.int32, (FOLD, HALF), 1) < HALF // 2
+
+    def turned(x, shift):
+        return pltpu.roll(x, shift % HALF, 1) if shift % HALF else x
+
+    def rim(pair, begin):
+        ahead, behind = pair
+        return jnp.where(lane[: ahead.shape[0]], turned(ahead, -begin), turned(behind, -begin - EDGE))
+
+    def ends(inside, outside):
+        return jnp.where(west, inside, outside), jnp.where(west, outside, inside)
+
     for group in range(2):
         base = (k if group == 0 else 1 - k) * HERE
         under, over = (own_below, own_above) if group == 0 else (below, above)
         for field in range(FIELDS):
-            rim = MAIN + field
             if group == 0:
-                far = MAIN + FIELDS + field
-                edge = (
-                    jnp.where(inner_rim, own_below[rim], below[far]),
-                    jnp.where(inner, edge_other[field], lon_same[field]),
-                    jnp.where(inner_rim, own_above[rim], above[far]),
-                )
+                inside = (own_below[MAIN + field], near[field], own_above[MAIN + field])
             else:
-                edge = (below[rim], edges[field], above[rim])
+                begin = field % 2 * FOLD
+                inside = (below[MAIN + field], partner[MAIN + field // 2, begin : begin + FOLD, :], above[MAIN + field])
+            at = MAIN + (1 + group) * FIELDS + field
+            outside = (own_below[at], (lon_same, lon_cross)[group][field], own_above[at])
+            south_rim, middle_rim, north_rim = (ends(*pair) for pair in zip(inside, outside))
             for level in range(HERE):
-                shift = (HALF - (2 * EDGE * level + EDGE)) % HALF
                 at = field * HERE + level
                 where = base + level
                 if field < TRACERS:
@@ -179,9 +194,10 @@
                     target[mid, main] = own_plane(refs, field, level, rows, mine)
                 else:
                     target[mid, main] = partner[at]
-                target[low, wing] = pltpu.roll(edge[0], shift, 1)
-                target[mid, wing] = pltpu.roll(edge[1], shift, 1)
-                target[top, wing] = pltpu.roll(edge[2], shift, 1)
+                target[low, wing] = rim(south_rim, EDGE * (HERE + level))
+                target[EDGE : EDGE + FOLD, wing] = rim(middle_rim, EDGE * level)
+                target[EDGE + FOLD : EDGE + ROWS, wing] = rim(middle_rim, EDGE * (HERE + level))
+                target[top, wing] = rim(north_rim, EDGE * level)
     for tracer in range(TRACERS):
         for level in range(HERE):
             row = tracer * HERE + level
@@ -189,7 +205,7 @@
                 injection[tracer : tracer + 1, level : level + 1][None], (1, 8, HALF)
             )
             inj_ref[tracer, pl.ds((1 - k) * HERE + level, 1)] = jnp.broadcast_to(
-                partner[MAIN + FIELDS, row : row + 1, :][None], (1, 8, HALF)
+                partner[PLANES - 1, row : row + 1, :][None], (1, 8, HALF)
             )
     kab_ref[LEVELS - 1] = jnp.zeros((TALL, WIDE), jnp.float32)
 
@@ -260,7 +276,31 @@
                 field_ref[tracer, level] = centre * cells + lon * along + lat * across
             return 0
 
-        lax.fori_loop(0, LEVELS, advect, 0)
+        def settle(level, _):
+            around = slice(0, TALL)
+            lon = lon_ref[level, mid, main]
+            lat = lat_ref[level, mid, main]
+            for tracer in range(TRACERS):
+                cells = field_ref[tracer, level, mid, :]
+                column = field_ref[tracer, level, around, main]
+                along = jnp.where(
+                    lon > 0.0, pltpu.roll(cells, WIDE - 1, 1)[:, main], pltpu.roll(cells, 1, 1)[:, main]
+                )
+                across = jnp.where(lat > 0.0, pltpu.roll(column, TALL - 1, 0)[mid], pltpu.roll(column, 1, 0)[mid])
+                here = cells[:, main]
+                field_ref[tracer, level, mid, main] = (
+                    (1.0 - jnp.abs(lon) - jnp.abs(lat)) * here + jnp.abs(lon) * along + jnp.abs(lat) * across
+                )
+            return 0
+
+        @pl.when(step < STEPS - 1)
+        def _():
+            lax.fori_loop(0, LEVELS, advect, 0)
+
+        @pl.when(step == STEPS - 1)
+        def _():
+            lax.fori_loop(0, LEVELS, settle, 0)
+
         return 0
 
     lax.fori_loop(0, STEPS, one_step, 0)
@@ -317,8 +357,8 @@
     own = tuple(hold(x) for x in (adjoint, courant_lon, courant_lat, mixing))
     injection = hold(injection)
 
-    edge_mine, edge_other = call(
-        pack_edges, (near(FIELDS, ROWS, HALF), near(FIELDS, ROWS, HALF)), (side, *raw), 1
+    edge_inner, edge_cross, edge_same, edge_near = call(
+        pack_edges, tuple(near(FIELDS, FOLD, HALF) for _ in range(4)), (side, *raw), 1
     )
     same = []
     cross = []
@@ -328,26 +368,29 @@
         cross += [(2 * i + 1, 2 * after), (2 * after, 2 * i + 1)]
     north = [(j, j + 1) for j in range(lat_count - 1)]
     south = [(j + 1, j) for j in range(lat_count - 1)]
-    lon_cross = permute(edge_mine, ("lon", "lev"), cross)
-    lon_same = permute(edge_other, ("lon", "lev"), same)
-
-    strip = MAIN + FIELDS
-    to_partner, first, last = call(
-        pack_main,
-        (near(MAIN + FIELDS + 1, ROWS, HALF), near(strip, EDGE, HALF), near(strip, EDGE, HALF)),
-        (side, injection, *own, edge_mine, edge_other),
+    lon_cross = permute(edge_cross, ("lon", "lev"), cross)
+    lon_same = permute(edge_same, ("lon", "lev"), same)
+
+    to_partner = call(pack_main, near(PLANES, ROWS, HALF), (side, injection, *own, edge_inner), 1, work=100000000)
+    partner = permute(to_partner, "lev", [(0, 1), (1, 0)])
+
+    strip = MAIN + 3 * FIELDS
+    first, last = call(
+        own_strips,
+        (near(strip, EDGE, HALF), near(strip, EDGE, HALF)),
+        (side, *own, edge_near, lon_same, lon_cross),
         1,
-    )
-    partner = permute(to_partner, "lev", [(0, 1), (1, 0)])
+        work=10000000000,
+    )
     own_below = permute(last, "lat", north)
     own_above = permute(first, "lat", south)
 
-    strip = MAIN + 2 * FIELDS
-    first, last, edges = call(
+    strip = MAIN + FIELDS
+    first, last = call(
         strips,
-        (near(strip, EDGE, HALF), near(strip, EDGE, HALF), near(FIELDS, ROWS, HALF)),
-        (side, partner, lon_same, lon_cross, own_below, own_above),
-        1,
+        (near(strip, EDGE, HALF), near(strip, EDGE, HALF)),
+        (partner, own_below, own_above),
+        0,
     )
     below = permute(last, "lat", north)
     above = permute(first, "lat", south)
@@ -361,7 +404,7 @@
             near(STEPS * TRACERS, ROWS, HALF),
         ),
         (
-            side, injection, *own, partner, edge_other, lon_same, edges,
+            side, injection, *own, partner, edge_near, lon_same, lon_cross,
             own_below, own_above, below, above, hold(prior_flux),
         ),
         1,

time: 151 us -> 153 us (1.013)
  waiting for transfers between devices: 21 us -> 46 us
  starting transfers between devices: 59 us -> 37.6 us
    ppermute x8, waiting for transfers between devices: 21 us -> 46 us  [permute(): return hold(lax.ppermute(x, axes, pairs))]
    ppermute x8, starting transfers between devices: 59 us -> 37.6 us  [permute(): return hold(lax.ppermute(x, axes, pairs))]
    pallas_call x6 -> x7, Pallas kernels: 31.5 us -> 31.7 us  [call(): pl.pallas_call(kernel, out_shape=out_shape, in_specs=specs, out_specs=tup...]
  transfers between devices with their start and end apart: 8 -> 8, of which waited for: 4 -> 6; matrix products, arithmetic and copies ran while one was open for 1% -> 1% of each run, Pallas kernels for 2% -> 2%
where the time goes in v5:
time: 153 us
  waiting for transfers between devices  46 us (30%)
  starting transfers between devices  37.6 us (25%)
  blocking collectives  35.5 us (23%)
  Pallas kernels  31.7 us (21%)
    ppermute x8, waiting for transfers between devices, permute(): return hold(lax.ppermute(x, axes, pairs))  46 us
    ppermute x8, starting transfers between devices, permute(): return hold(lax.ppermute(x, axes, pairs))  37.6 us
    all_to_all x1, blocking collectives, body(): pieces = lax.all_to_all(sums, ('lon', 'lat', 'lev'), 0, 0, tiled=True)  35.5 us
    pallas_call x7, Pallas kernels, call(): pl.pallas_call(kernel, out_shape=out_shape, in_specs=specs, out_specs=tup...  31.7 us
  transfers between devices with their start and end apart: 8, of which 6 were waited for; matrix products, arithmetic and copies ran while one was open for 1% of the time, Pallas kernels for 2%

profile of v5, /device:TPU:1, one launch (start us, length us, event | category | flops | bytes accessed | tf_op | source)
XLA Modules:
  0.0 152.9 jit_solution(13198026858907978820)
XLA Ops:
  0.7 2.2 %pack_edges.1 = (f32[7,16,128]{2,1,0:T(8,128)S(1)}, f32[7,16,128]{2,1,0:T(8,128)S(1)}, f32[7,16,128]{2,1,0:T(8,128)S(1)}, f32[7,16,128]{2,1,0:T(8,128)S(1)}) custom-call(s32[1]{0:T(128)} %bitcast.side, f32[4,8,32,256]{3,2,1,0:T(8,128)} %adjoint.7, bf16[8,32,256]{2,1,0:T(8,128)(2,1)} %lon_wind.7, bf16[8,32,256]{2,1,0:T(8,128)(2,1)} %lat_wind.7, ...), custom_call_target="tpu_custom_call" | custom-call | tf_op jit(solution)/shard_map/pack_edges/pallas_call | solution.py:33
  2.9 0.0 copy-start.6
  2.9 5.4 %collective-permute-start.1 = (f32[7,16,128]{2,1,0:T(8,128)S(1)}, f32[7,16,128]{2,1,0:T(8,128)S(1)}, u32[]{:S(2)}, u32[]{:S(2)}) collective-permute-start(f32[7,16,128]{2,1,0:T(8,128)S(1)} %get-tuple-element.15), channel_id=1, source_target_pairs={{0,16},{17,1},{16,32},{33,17},{32,48},{49,33},{48,64},{65,49},{64,... | collective-permute-start | bytes 172040 | tf_op jit(solution)/shard_map/ppermute | solution.py:58
  8.3 13.5 %collective-permute-start.2 = (f32[7,16,128]{2,1,0:T(8,128)S(1)}, f32[7,16,128]{2,1,0:T(8,128)S(1)}, u32[]{:S(2)}, u32[]{:S(2)}) collective-permute-start(f32[7,16,128]{2,1,0:T(8,128)S(1)} %get-tuple-element.16), channel_id=1, source_target_pairs={{1,16},{16,1},{17,32},{32,17},{33,48},{48,33},{49,64},{64,49},{65,... | collective-permute-start | bytes 172040 | tf_op jit(solution)/shard_map/ppermute | solution.py:58
  21.8 0.1 pack_main.1
  21.9 1.9 %collective-permute-start = (f32[61,32,128]{2,1,0:T(8,128)S(1)}, f32[61,32,128]{2,1,0:T(8,128)S(1)}, u32[]{:S(2)}, u32[]{:S(2)}) collective-permute-start(f32[61,32,128]{2,1,0:T(8,128)S(1)} %pack_main.1), channel_id=1, source_target_pairs={{0,1},{1,0},{2,3},{3,2},{4,5},{5,4},{6,7},{7,6},{8,9},{9,8},{10,11... | collective-permute-start | bytes 2998280 | tf_op jit(solution)/shard_map/ppermute | solution.py:58
  23.9 4.5 %collective-permute-done.2.lon_cross = f32[7,16,128]{2,1,0:T(8,128)S(1)} collective-permute-done((f32[7,16,128]{2,1,0:T(8,128)S(1)}, f32[7,16,128]{2,1,0:T(8,128)S(1)}, u32[]{:S(2)}, u32[]{:S(2)}) %collective-permute-start.2) | collective-permute-done | bytes 57376 | tf_op jit(solution)/shard_map/ppermute | solution.py:58
  28.4 3.2 %collective-permute-start.3 = (f32[77,8,128]{2,1,0:T(8,128)S(1)}, f32[77,8,128]{2,1,0:T(8,128)S(1)}, u32[]{:S(2)}, u32[]{:S(2)}) collective-permute-start(f32[77,8,128]{2,1,0:T(8,128)S(1)} %get-tuple-element.17), channel_id=1, source_target_pairs={{0,2},{2,4},{4,6},{6,8},{8,10},{10,12},{12,14},{1,3},{3,5},{5,7},{... | collective-permute-start | bytes 946184 | tf_op jit(solution)/shard_map/ppermute | solution.py:58
  31.6 1.4 collective-permute-start.4
  33.1 2.4 %collective-permute-done.3.own_below = f32[77,8,128]{2,1,0:T(8,128)S(1)} collective-permute-done((f32[77,8,128]{2,1,0:T(8,128)S(1)}, f32[77,8,128]{2,1,0:T(8,128)S(1)}, u32[]{:S(2)}, u32[]{:S(2)}) %collective-permute-start.3) | collective-permute-done | bytes 315424 | tf_op jit(solution)/shard_map/ppermute | solution.py:58
  35.5 4.3 %collective-permute-done.4.own_above = f32[77,8,128]{2,1,0:T(8,128)S(1)} collective-permute-done((f32[77,8,128]{2,1,0:T(8,128)S(1)}, f32[77,8,128]{2,1,0:T(8,128)S(1)}, u32[]{:S(2)}, u32[]{:S(2)}) %collective-permute-start.4) | collective-permute-done | bytes 315424 | tf_op jit(solution)/shard_map/ppermute | solution.py:58
  39.7 28.8 %collective-permute-done.partner = f32[61,32,128]{2,1,0:T(8,128)S(1)} collective-permute-done((f32[61,32,128]{2,1,0:T(8,128)S(1)}, f32[61,32,128]{2,1,0:T(8,128)S(1)}, u32[]{:S(2)}, u32[]{:S(2)}) %collective-permute-start) | collective-permute-done | bytes 999456 | tf_op jit(solution)/shard_map/ppermute | solution.py:58
  68.5 3.2 %collective-permute-start.5 = (f32[63,8,128]{2,1,0:T(8,128)S(1)}, f32[63,8,128]{2,1,0:T(8,128)S(1)}, u32[]{:S(2)}, u32[]{:S(2)}) collective-permute-start(f32[63,8,128]{2,1,0:T(8,128)S(1)} %get-tuple-element.19), channel_id=1, source_target_pairs={{0,2},{2,4},{4,6},{6,8},{8,10},{10,12},{12,14},{1,3},{3,5},{5,7},{... | collective-permute-start | bytes 774152 | tf_op jit(solution)/shard_map/ppermute | solution.py:58
  71.8 0.0 copy-start.5
  71.8 1.3 collective-permute-start.6
  73.1 1.9 %collective-permute-done.5.below = f32[63,8,128]{2,1,0:T(8,128)S(1)} collective-permute-done((f32[63,8,128]{2,1,0:T(8,128)S(1)}, f32[63,8,128]{2,1,0:T(8,128)S(1)}, u32[]{:S(2)}, u32[]{:S(2)}) %collective-permute-start.5) | collective-permute-done | bytes 258080 | tf_op jit(solution)/shard_map/ppermute | solution.py:58
  75.0 4.2 %collective-permute-done.6.above = f32[63,8,128]{2,1,0:T(8,128)S(1)} collective-permute-done((f32[63,8,128]{2,1,0:T(8,128)S(1)}, f32[63,8,128]{2,1,0:T(8,128)S(1)}, u32[]{:S(2)}, u32[]{:S(2)}) %collective-permute-start.6) | collective-permute-done | bytes 258080 | tf_op jit(solution)/shard_map/ppermute | solution.py:58
  79.2 25.9 %steps.1 = (f32[4,8,32,128]{3,2,1,0:T(8,128)S(1)}, f32[4,8,32,128]{3,2,1,0:T(8,128)S(1)}, f32[24,32,128]{2,1,0:T(8,128)S(1)}) custom-call(s32[1]{0:T(128)} %bitcast.side, f32[4,8]{1,0:T(4,128)S(1)} %copy-done.6, f32[4,8,32,256]{3,2,1,0:T(8,128)S(1)} %copy-done, bf16[8,32,256]{2,1,0:T(8,128)(2,1)S(1)} %copy-done.1, bf16[8,32,256]{2,1,0:T(8,128)(2,1)S(1)} %copy-done.2, ...), custom_call_target="tpu_custom_call" | custom-call | tf_op jit(solution)/shard_map/steps/pallas_call | solution.py:33
  105.1 7.7 %collective-permute-start.7 = (f32[4,8,32,128]{3,2,1,0:T(8,128)S(1)}, f32[4,8,32,128]{3,2,1,0:T(8,128)S(1)}, u32[]{:S(2)}, u32[]{:S(2)}) collective-permute-start(f32[4,8,32,128]{3,2,1,0:T(8,128)S(1)} %get-tuple-element.22), channel_id=1, source_target_pairs={{0,1},{1,0},{2,3},{3,2},{4,5},{5,4},{6,7},{7,6},{8,9},{9,8},{10,11... | collective-permute-start | bytes 1572872 | tf_op jit(solution)/shard_map/ppermute | solution.py:58
  112.8 2.4 %regions.1 = f32[512,128]{1,0:T(8,128)S(1)} custom-call(s32[1]{0:T(128)} %bitcast.side, f32[24,32,128]{2,1,0:T(8,128)S(1)} %get-tuple-element.23.weights, s32[32,256]{1,0:T(8,128)S(1)} %copy-done.5), custom_call_target="tpu_custom_call" | custom-call | tf_op jit(solution)/shard_map/regions/pallas_call | solution.py:33
  115.2 35.5 %all_to_all.9 = f32[512,1,128]{2,1,0:T(1,128)S(1)} all-to-all(f32[512,1,128]{2,1,0:T(1,128)S(1)} %bitcast.5), channel_id=1, replica_groups=mesh['lon'=32,'lat'=8,'lev'=2] {'lon','lat','lev'}, dimensions={0} | all-to-all | bytes 524288 | tf_op jit(solution)/shard_map/all_to_all | solution.py:432
  150.7 0.6 reduce_sum.9
  151.2 0.7 reshape.13
  151.9 1.0 join.1
  (16 shorter events, 0.1 us)
Async XLA Ops:
  0.6 21.1 %copy-start = (f32[4,8,32,256]{3,2,1,0:T(8,128)S(1)}, f32[4,8,32,256]{3,2,1,0:T(8,128)}, u32[]{:S(2)}) copy-start(f32[4,8,32,256]{3,2,1,0:T(8,128)} %adjoint.7) | copy-start | bytes 3145732
  0.6 21.1 %copy-start.1 = (bf16[8,32,256]{2,1,0:T(8,128)(2,1)S(1)}, bf16[8,32,256]{2,1,0:T(8,128)(2,1)}, u32[]{:S(2)}) copy-start(bf16[8,32,256]{2,1,0:T(8,128)(2,1)} %lon_wind.7) | copy-start | bytes 393220
  0.7 21.1 %copy-start.2 = (bf16[8,32,256]{2,1,0:T(8,128)(2,1)S(1)}, bf16[8,32,256]{2,1,0:T(8,128)(2,1)}, u32[]{:S(2)}) copy-start(bf16[8,32,256]{2,1,0:T(8,128)(2,1)} %lat_wind.7) | copy-start | bytes 393220
  0.7 21.1 %copy-start.3 = (bf16[8,32,256]{2,1,0:T(8,128)(2,1)S(1)}, bf16[8,32,256]{2,1,0:T(8,128)(2,1)}, u32[]{:S(2)}) copy-start(bf16[8,32,256]{2,1,0:T(8,128)(2,1)} %mixing.7) | copy-start | bytes 393220
  2.9 18.9 %copy-start.6 = (f32[4,8]{1,0:T(4,128)S(1)}, f32[4,8]{1,0:T(4,128)}, u32[]{:S(2)}) copy-start(f32[4,8]{1,0:T(4,128)} %injection.3) | copy-start | bytes 388
  2.9 21.0 %collective-permute-start.1 = (f32[7,16,128]{2,1,0:T(8,128)S(1)}, f32[7,16,128]{2,1,0:T(8,128)S(1)}, u32[]{:S(2)}, u32[]{:S(2)}) collective-permute-start(f32[7,16,128]{2,1,0:T(8,128)S(1)} %get-tuple-element.15), channel_id=1, source_target_pairs={{0,16},{17,1},{16,32},{33,17},{32,48},{49,33},{48,64},{65,49},{64,... | collective-permute-start | bytes 172040 | tf_op jit(solution)/shard_map/ppermute | solution.py:58
  8.3 20.0 %collective-permute-start.2 = (f32[7,16,128]{2,1,0:T(8,128)S(1)}, f32[7,16,128]{2,1,0:T(8,128)S(1)}, u32[]{:S(2)}, u32[]{:S(2)}) collective-permute-start(f32[7,16,128]{2,1,0:T(8,128)S(1)} %get-tuple-element.16), channel_id=1, source_target_pairs={{1,16},{16,1},{17,32},{32,17},{33,48},{48,33},{49,64},{64,49},{65,... | collective-permute-start | bytes 172040 | tf_op jit(solution)/shard_map/ppermute | solution.py:58
  21.9 46.6 %collective-permute-start = (f32[61,32,128]{2,1,0:T(8,128)S(1)}, f32[61,32,128]{2,1,0:T(8,128)S(1)}, u32[]{:S(2)}, u32[]{:S(2)}) collective-permute-start(f32[61,32,128]{2,1,0:T(8,128)S(1)} %pack_main.1), channel_id=1, source_target_pairs={{0,1},{1,0},{2,3},{3,2},{4,5},{5,4},{6,7},{7,6},{8,9},{9,8},{10,11... | collective-permute-start | bytes 2998280 | tf_op jit(solution)/shard_map/ppermute | solution.py:58
  28.4 7.1 %collective-permute-start.3 = (f32[77,8,128]{2,1,0:T(8,128)S(1)}, f32[77,8,128]{2,1,0:T(8,128)S(1)}, u32[]{:S(2)}, u32[]{:S(2)}) collective-permute-start(f32[77,8,128]{2,1,0:T(8,128)S(1)} %get-tuple-element.17), channel_id=1, source_target_pairs={{0,2},{2,4},{4,6},{6,8},{8,10},{10,12},{12,14},{1,3},{3,5},{5,7},{... | collective-permute-start | bytes 946184 | tf_op jit(solution)/shard_map/ppermute | solution.py:58
  31.6 47.6 %copy-start.4 = (bf16[4,32,256]{2,1,0:T(8,128)(2,1)S(1)}, bf16[4,32,256]{2,1,0:T(8,128)(2,1)}, u32[]{:S(2)}) copy-start(bf16[4,32,256]{2,1,0:T(8,128)(2,1)} %prior.1) | copy-start | bytes 196612
  31.6 8.1 %collective-permute-start.4 = (f32[77,8,128]{2,1,0:T(8,128)S(1)}, f32[77,8,128]{2,1,0:T(8,128)S(1)}, u32[]{:S(2)}, u32[]{:S(2)}) collective-permute-start(f32[77,8,128]{2,1,0:T(8,128)S(1)} %get-tuple-element.18), channel_id=1, source_target_pairs={{2,0},{4,2},{6,4},{8,6},{10,8},{12,10},{14,12},{3,1},{5,3},{7,5},{... | collective-permute-start | bytes 946184 | tf_op jit(solution)/shard_map/ppermute | solution.py:58
  68.5 6.5 %collective-permute-start.5 = (f32[63,8,128]{2,1,0:T(8,128)S(1)}, f32[63,8,128]{2,1,0:T(8,128)S(1)}, u32[]{:S(2)}, u32[]{:S(2)}) collective-permute-start(f32[63,8,128]{2,1,0:T(8,128)S(1)} %get-tuple-element.19), channel_id=1, source_target_pairs={{0,2},{2,4},{4,6},{6,8},{8,10},{10,12},{12,14},{1,3},{3,5},{5,7},{... | collective-permute-start | bytes 774152 | tf_op jit(solution)/shard_map/ppermute | solution.py:58
  71.8 41.0 %copy-start.5 = (s32[32,256]{1,0:T(8,128)S(1)}, s32[32,256]{1,0:T(8,128)}, u32[]{:S(2)}) copy-start(s32[32,256]{1,0:T(8,128)} %ids.1) | copy-start | bytes 98308
  71.8 7.4 %collective-permute-start.6 = (f32[63,8,128]{2,1,0:T(8,128)S(1)}, f32[63,8,128]{2,1,0:T(8,128)S(1)}, u32[]{:S(2)}, u32[]{:S(2)}) collective-permute-start(f32[63,8,128]{2,1,0:T(8,128)S(1)} %get-tuple-element.20), channel_id=1, source_target_pairs={{2,0},{4,2},{6,4},{8,6},{10,8},{12,10},{14,12},{3,1},{5,3},{7,5},{... | collective-permute-start | bytes 774152 | tf_op jit(solution)/shard_map/ppermute | solution.py:58
  105.1 46.8 %collective-permute-start.7 = (f32[4,8,32,128]{3,2,1,0:T(8,128)S(1)}, f32[4,8,32,128]{3,2,1,0:T(8,128)S(1)}, u32[]{:S(2)}, u32[]{:S(2)}) collective-permute-start(f32[4,8,32,128]{3,2,1,0:T(8,128)S(1)} %get-tuple-element.22), channel_id=1, source_target_pairs={{0,1},{1,0},{2,3},{3,2},{4,5},{5,4},{6,7},{7,6},{8,9},{9,8},{10,11... | collective-permute-start | bytes 1572872 | tf_op jit(solution)/shard_map/ppermute | solution.py:58

commit v6 on v5

--- a/solution.py
+++ b/solution.py
@@ -27,7 +27,7 @@
 MIB = 1024 * 1024
 
 
-def call(kernel, out_shape, operands, scalars, scratch=(), limit=8, work=0):
+def call(kernel, out_shape, operands, scalars, scratch=(), limit=8):
     specs = [SMEM] * scalars + [VMEM] * (len(operands) - scalars)
     many = isinstance(out_shape, (tuple, list))
     return pl.pallas_call(
@@ -38,7 +38,6 @@
         scratch_shapes=list(scratch),
         compiler_params=pltpu.CompilerParams(vmem_limit_bytes=limit * MIB),
         name=kernel.__name__,
-        cost_estimate=pl.CostEstimate(flops=work, bytes_accessed=work, transcendentals=0) if work else None,
     )(*operands)
 
 
@@ -102,13 +101,20 @@
         near[field] = jnp.where(west, low, high)
 
 
-def pack_main(side, injection, adjoint, lon_wind, lat_wind, mixing, inner, to_partner):
+def pack_main(side, injection, adjoint, lon_wind, lat_wind, mixing, inner, near, to_partner, first, last):
     refs = (adjoint, lon_wind, lat_wind, mixing)
+    mine = half_at(side[0])
     other = half_at(1 - side[0])
     for field in range(FIELDS):
         for level in range(HERE):
-            to_partner[field * HERE + level] = own_plane(refs, field, level, slice(0, ROWS), other)
+            at = field * HERE + level
+            to_partner[at] = own_plane(refs, field, level, slice(0, ROWS), other)
+            plane = own_plane(refs, field, level, slice(0, ROWS), mine)
+            first[at] = plane[:EDGE]
+            last[at] = plane[ROWS - EDGE :]
         to_partner[MAIN + field // 2, pl.ds(field % 2 * FOLD, FOLD), :] = inner[field]
+        first[MAIN + field] = near[field, :EDGE]
+        last[MAIN + field] = near[field, EDGE:]
     for tracer in range(TRACERS):
         for level in range(HERE):
             row = tracer * HERE + level
@@ -117,27 +123,17 @@
             )
 
 
-def own_strips(side, adjoint, lon_wind, lat_wind, mixing, near, lon_same, lon_cross, first, last):
-    refs = (adjoint, lon_wind, lat_wind, mixing)
-    mine = half_at(side[0])
-    for field in range(FIELDS):
-        for level in range(HERE):
-            plane = own_plane(refs, field, level, slice(0, ROWS), mine)
-            first[field * HERE + level] = plane[:EDGE]
-            last[field * HERE + level] = plane[ROWS - EDGE :]
-    for group, rims in enumerate((near, lon_same, lon_cross)):
-        at = slice(MAIN + group * FIELDS, MAIN + (group + 1) * FIELDS)
-        first[at] = rims[:, :EDGE, :]
-        last[at] = rims[:, EDGE:, :]
-
-
-def strips(partner, own_below, own_above, first, last):
+def strips(partner, lon_same, lon_cross, own_below, own_above, first, last):
     first[0:MAIN] = partner[0:MAIN, 0:EDGE, :]
     last[0:MAIN] = partner[0:MAIN, ROWS - EDGE : ROWS, :]
     for field in range(FIELDS):
         begin = field % 2 * FOLD
         first[MAIN + field] = partner[MAIN + field // 2, begin : begin + EDGE, :]
         last[MAIN + field] = partner[MAIN + field // 2, begin + EDGE : begin + FOLD, :]
+    for group, rims in enumerate((lon_same, lon_cross)):
+        at = slice(MAIN + (1 + group) * FIELDS, MAIN + (2 + group) * FIELDS)
+        first[at] = rims[:, :EDGE, :]
+        last[at] = rims[:, EDGE:, :]
 
 
 def steps(
@@ -179,7 +175,7 @@
                 begin = field % 2 * FOLD
                 inside = (below[MAIN + field], partner[MAIN + field // 2, begin : begin + FOLD, :], above[MAIN + field])
             at = MAIN + (1 + group) * FIELDS + field
-            outside = (own_below[at], (lon_same, lon_cross)[group][field], own_above[at])
+            outside = (below[at], (lon_same, lon_cross)[group][field], above[at])
             south_rim, middle_rim, north_rim = (ends(*pair) for pair in zip(inside, outside))
             for level in range(HERE):
                 at = field * HERE + level
@@ -371,25 +367,22 @@
     lon_cross = permute(edge_cross, ("lon", "lev"), cross)
     lon_same = permute(edge_same, ("lon", "lev"), same)
 
-    to_partner = call(pack_main, near(PLANES, ROWS, HALF), (side, injection, *own, edge_inner), 1, work=100000000)
+    strip = MAIN + FIELDS
+    to_partner, first, last = call(
+        pack_main,
+        (near(PLANES, ROWS, HALF), near(strip, EDGE, HALF), near(strip, EDGE, HALF)),
+        (side, injection, *own, edge_inner, edge_near),
+        1,
+    )
     partner = permute(to_partner, "lev", [(0, 1), (1, 0)])
-
-    strip = MAIN + 3 * FIELDS
-    first, last = call(
-        own_strips,
-        (near(strip, EDGE, HALF), near(strip, EDGE, HALF)),
-        (side, *own, edge_near, lon_same, lon_cross),
-        1,
-        work=10000000000,
-    )
     own_below = permute(last, "lat", north)
     own_above = permute(first, "lat", south)
 
-    strip = MAIN + FIELDS
+    strip = MAIN + 3 * FIELDS
     first, last = call(
         strips,
         (near(strip, EDGE, HALF), near(strip, EDGE, HALF)),
-        (partner, own_below, own_above),
+        (partner, lon_same, lon_cross, own_below, own_above),
         0,
     )
     below = permute(last, "lat", north)

time: 153 us -> 145 us (0.948)
  waiting for transfers between devices: 46 us -> 16.5 us
  starting transfers between devices: 37.6 us -> 62 us
  blocking collectives: 35.5 us -> 31.8 us
    ppermute x8, waiting for transfers between devices: 46 us -> 16.5 us  [permute(): return hold(lax.ppermute(x, axes, pairs))]
    ppermute x8, starting transfers between devices: 37.6 us -> 62 us  [permute(): return hold(lax.ppermute(x, axes, pairs))]
    all_to_all x1, blocking collectives: 35.5 us -> 31.8 us  [body(): pieces = lax.all_to_all(sums, ('lon', 'lat', 'lev'), 0, 0, tiled=True)]
    pallas_call x7 -> x6, Pallas kernels: 31.7 us -> 31.7 us  [call(): pl.pallas_call(kernel, out_shape=out_shape, in_specs=specs, out_specs=tup...]
  transfers between devices with their start and end apart: 8 -> 8, of which waited for: 6 -> 4; matrix products, arithmetic and copies ran while one was open for 1% -> 1% of each run, Pallas kernels for 2% -> 2%
where the time goes in v6:
time: 145 us
  starting transfers between devices  62 us (43%)
  blocking collectives  31.8 us (22%)
  Pallas kernels  31.7 us (22%)
  waiting for transfers between devices  16.5 us (11%)
    ppermute x8, starting transfers between devices, permute(): return hold(lax.ppermute(x, axes, pairs))  62 us
    all_to_all x1, blocking collectives, body(): pieces = lax.all_to_all(sums, ('lon', 'lat', 'lev'), 0, 0, tiled=True)  31.8 us
    pallas_call x6, Pallas kernels, call(): pl.pallas_call(kernel, out_shape=out_shape, in_specs=specs, out_specs=tup...  31.7 us
    ppermute x8, waiting for transfers between devices, permute(): return hold(lax.ppermute(x, axes, pairs))  16.5 us
  transfers between devices with their start and end apart: 8, of which 4 were waited for; matrix products, arithmetic and copies ran while one was open for 1% of the time, Pallas kernels for 2%

profile of v6, /device:TPU:1, one launch (start us, length us, event | category | flops | bytes accessed | tf_op | source)
XLA Modules:
  0.0 144.7 jit_solution(10598827524175947698)
XLA Ops:
  0.7 2.2 %pack_edges.1 = (f32[7,16,128]{2,1,0:T(8,128)S(1)}, f32[7,16,128]{2,1,0:T(8,128)S(1)}, f32[7,16,128]{2,1,0:T(8,128)S(1)}, f32[7,16,128]{2,1,0:T(8,128)S(1)}) custom-call(s32[1]{0:T(128)} %bitcast.side, f32[4,8,32,256]{3,2,1,0:T(8,128)} %adjoint.5, bf16[8,32,256]{2,1,0:T(8,128)(2,1)} %lon_wind.5, bf16[8,32,256]{2,1,0:T(8,128)(2,1)} %lat_wind.5, ...), custom_call_target="tpu_custom_call" | custom-call | tf_op jit(solution)/shard_map/pack_edges/pallas_call | solution.py:33
  2.9 0.0 copy-start.6
  2.9 0.6 copy-done.6
  3.6 0.1 pack_main.1
  3.7 11.5 %collective-permute-start = (f32[61,32,128]{2,1,0:T(8,128)S(1)}, f32[61,32,128]{2,1,0:T(8,128)S(1)}, u32[]{:S(2)}, u32[]{:S(2)}) collective-permute-start(f32[61,32,128]{2,1,0:T(8,128)S(1)} %get-tuple-element.16), channel_id=1, source_target_pairs={{0,1},{1,0},{2,3},{3,2},{4,5},{5,4},{6,7},{7,6},{8,9},{9,8},{10,11... | collective-permute-start | bytes 2998280 | tf_op jit(solution)/shard_map/ppermute | solution.py:57
  15.2 3.2 %collective-permute-start.3 = (f32[63,8,128]{2,1,0:T(8,128)S(1)}, f32[63,8,128]{2,1,0:T(8,128)S(1)}, u32[]{:S(2)}, u32[]{:S(2)}) collective-permute-start(f32[63,8,128]{2,1,0:T(8,128)S(1)} %get-tuple-element.19), channel_id=1, source_target_pairs={{0,2},{2,4},{4,6},{6,8},{8,10},{10,12},{12,14},{1,3},{3,5},{5,7},{... | collective-permute-start | bytes 774152 | tf_op jit(solution)/shard_map/ppermute | solution.py:57
  18.4 1.3 collective-permute-start.4
  19.7 4.2 %collective-permute-start.1 = (f32[7,16,128]{2,1,0:T(8,128)S(1)}, f32[7,16,128]{2,1,0:T(8,128)S(1)}, u32[]{:S(2)}, u32[]{:S(2)}) collective-permute-start(f32[7,16,128]{2,1,0:T(8,128)S(1)} %get-tuple-element.17), channel_id=1, source_target_pairs={{0,16},{17,1},{16,32},{33,17},{32,48},{49,33},{48,64},{65,49},{64,... | collective-permute-start | bytes 172040 | tf_op jit(solution)/shard_map/ppermute | solution.py:57
  23.9 0.0 copy-start.4
  23.9 5.2 %collective-permute-start.2 = (f32[7,16,128]{2,1,0:T(8,128)S(1)}, f32[7,16,128]{2,1,0:T(8,128)S(1)}, u32[]{:S(2)}, u32[]{:S(2)}) collective-permute-start(f32[7,16,128]{2,1,0:T(8,128)S(1)} %get-tuple-element.18), channel_id=1, source_target_pairs={{1,16},{16,1},{17,32},{32,17},{33,48},{48,33},{49,64},{64,49},{65,... | collective-permute-start | bytes 172040 | tf_op jit(solution)/shard_map/ppermute | solution.py:57
  29.2 8.6 %collective-permute-done.1.lon_same = f32[7,16,128]{2,1,0:T(8,128)S(1)} collective-permute-done((f32[7,16,128]{2,1,0:T(8,128)S(1)}, f32[7,16,128]{2,1,0:T(8,128)S(1)}, u32[]{:S(2)}, u32[]{:S(2)}) %collective-permute-start.1) | collective-permute-done | bytes 57376 | tf_op jit(solution)/shard_map/ppermute | solution.py:57
  37.7 1.5 %collective-permute-done.2.lon_cross = f32[7,16,128]{2,1,0:T(8,128)S(1)} collective-permute-done((f32[7,16,128]{2,1,0:T(8,128)S(1)}, f32[7,16,128]{2,1,0:T(8,128)S(1)}, u32[]{:S(2)}, u32[]{:S(2)}) %collective-permute-start.2) | collective-permute-done | bytes 57376 | tf_op jit(solution)/shard_map/ppermute | solution.py:57
  39.3 3.2 %collective-permute-start.5 = (f32[77,8,128]{2,1,0:T(8,128)S(1)}, f32[77,8,128]{2,1,0:T(8,128)S(1)}, u32[]{:S(2)}, u32[]{:S(2)}) collective-permute-start(f32[77,8,128]{2,1,0:T(8,128)S(1)} %get-tuple-element.21), channel_id=1, source_target_pairs={{0,2},{2,4},{4,6},{6,8},{8,10},{10,12},{12,14},{1,3},{3,5},{5,7},{... | collective-permute-start | bytes 946184 | tf_op jit(solution)/shard_map/ppermute | solution.py:57
  42.6 0.0 copy-start.5
  42.6 1.3 collective-permute-start.6
  43.9 2.5 %collective-permute-done.5.below = f32[77,8,128]{2,1,0:T(8,128)S(1)} collective-permute-done((f32[77,8,128]{2,1,0:T(8,128)S(1)}, f32[77,8,128]{2,1,0:T(8,128)S(1)}, u32[]{:S(2)}, u32[]{:S(2)}) %collective-permute-start.5) | collective-permute-done | bytes 315424 | tf_op jit(solution)/shard_map/ppermute | solution.py:57
  46.4 3.8 %collective-permute-done.6.above = f32[77,8,128]{2,1,0:T(8,128)S(1)} collective-permute-done((f32[77,8,128]{2,1,0:T(8,128)S(1)}, f32[77,8,128]{2,1,0:T(8,128)S(1)}, u32[]{:S(2)}, u32[]{:S(2)}) %collective-permute-start.6) | collective-permute-done | bytes 315424 | tf_op jit(solution)/shard_map/ppermute | solution.py:57
  50.3 25.9 %steps.1 = (f32[4,8,32,128]{3,2,1,0:T(8,128)S(1)}, f32[4,8,32,128]{3,2,1,0:T(8,128)S(1)}, f32[24,32,128]{2,1,0:T(8,128)S(1)}) custom-call(s32[1]{0:T(128)} %bitcast.side, f32[4,8]{1,0:T(4,128)S(1)} %copy-done.6, f32[4,8,32,256]{3,2,1,0:T(8,128)S(1)} %copy-done, bf16[8,32,256]{2,1,0:T(8,128)(2,1)S(1)} %copy-done.1, bf16[8,32,256]{2,1,0:T(8,128)(2,1)S(1)} %copy-done.2, ...), custom_call_target="tpu_custom_call" | custom-call | tf_op jit(solution)/shard_map/steps/pallas_call | solution.py:33
  76.2 32.1 %collective-permute-start.7 = (f32[4,8,32,128]{3,2,1,0:T(8,128)S(1)}, f32[4,8,32,128]{3,2,1,0:T(8,128)S(1)}, u32[]{:S(2)}, u32[]{:S(2)}) collective-permute-start(f32[4,8,32,128]{3,2,1,0:T(8,128)S(1)} %get-tuple-element.24), channel_id=1, source_target_pairs={{0,1},{1,0},{2,3},{3,2},{4,5},{5,4},{6,7},{7,6},{8,9},{9,8},{10,11... | collective-permute-start | bytes 1572872 | tf_op jit(solution)/shard_map/ppermute | solution.py:57
  108.3 2.4 %regions.1 = f32[512,128]{1,0:T(8,128)S(1)} custom-call(s32[1]{0:T(128)} %bitcast.side, f32[24,32,128]{2,1,0:T(8,128)S(1)} %get-tuple-element.25.weights, s32[32,256]{1,0:T(8,128)S(1)} %copy-done.5), custom_call_target="tpu_custom_call" | custom-call | tf_op jit(solution)/shard_map/regions/pallas_call | solution.py:33
  110.7 31.8 %all_to_all.9 = f32[512,1,128]{2,1,0:T(1,128)S(1)} all-to-all(f32[512,1,128]{2,1,0:T(1,128)S(1)} %bitcast.5), channel_id=1, replica_groups=mesh['lon'=32,'lat'=8,'lev'=2] {'lon','lat','lev'}, dimensions={0} | all-to-all | bytes 524288 | tf_op jit(solution)/shard_map/all_to_all | solution.py:425
  142.5 0.6 reduce_sum.9
  143.0 0.7 reshape.13
  143.7 1.0 join.1
  (15 shorter events, 0.1 us)
Async XLA Ops:
  0.6 2.3 %copy-start = (f32[4,8,32,256]{3,2,1,0:T(8,128)S(1)}, f32[4,8,32,256]{3,2,1,0:T(8,128)}, u32[]{:S(2)}) copy-start(f32[4,8,32,256]{3,2,1,0:T(8,128)} %adjoint.5) | copy-start | bytes 3145732
  0.6 2.3 %copy-start.1 = (bf16[8,32,256]{2,1,0:T(8,128)(2,1)S(1)}, bf16[8,32,256]{2,1,0:T(8,128)(2,1)}, u32[]{:S(2)}) copy-start(bf16[8,32,256]{2,1,0:T(8,128)(2,1)} %lon_wind.5) | copy-start | bytes 393220
  0.7 2.3 %copy-start.2 = (bf16[8,32,256]{2,1,0:T(8,128)(2,1)S(1)}, bf16[8,32,256]{2,1,0:T(8,128)(2,1)}, u32[]{:S(2)}) copy-start(bf16[8,32,256]{2,1,0:T(8,128)(2,1)} %lat_wind.5) | copy-start | bytes 393220
  0.7 2.3 %copy-start.3 = (bf16[8,32,256]{2,1,0:T(8,128)(2,1)S(1)}, bf16[8,32,256]{2,1,0:T(8,128)(2,1)}, u32[]{:S(2)}) copy-start(bf16[8,32,256]{2,1,0:T(8,128)(2,1)} %mixing.5) | copy-start | bytes 393220
  2.9 0.7 copy-start.6
  3.7 35.6 %collective-permute-start = (f32[61,32,128]{2,1,0:T(8,128)S(1)}, f32[61,32,128]{2,1,0:T(8,128)S(1)}, u32[]{:S(2)}, u32[]{:S(2)}) collective-permute-start(f32[61,32,128]{2,1,0:T(8,128)S(1)} %get-tuple-element.16), channel_id=1, source_target_pairs={{0,1},{1,0},{2,3},{3,2},{4,5},{5,4},{6,7},{7,6},{8,9},{9,8},{10,11... | collective-permute-start | bytes 2998280 | tf_op jit(solution)/shard_map/ppermute | solution.py:57
  15.2 24.1 %collective-permute-start.3 = (f32[63,8,128]{2,1,0:T(8,128)S(1)}, f32[63,8,128]{2,1,0:T(8,128)S(1)}, u32[]{:S(2)}, u32[]{:S(2)}) collective-permute-start(f32[63,8,128]{2,1,0:T(8,128)S(1)} %get-tuple-element.19), channel_id=1, source_target_pairs={{0,2},{2,4},{4,6},{6,8},{8,10},{10,12},{12,14},{1,3},{3,5},{5,7},{... | collective-permute-start | bytes 774152 | tf_op jit(solution)/shard_map/ppermute | solution.py:57
  18.4 20.9 %collective-permute-start.4 = (f32[63,8,128]{2,1,0:T(8,128)S(1)}, f32[63,8,128]{2,1,0:T(8,128)S(1)}, u32[]{:S(2)}, u32[]{:S(2)}) collective-permute-start(f32[63,8,128]{2,1,0:T(8,128)S(1)} %get-tuple-element.20), channel_id=1, source_target_pairs={{2,0},{4,2},{6,4},{8,6},{10,8},{12,10},{14,12},{3,1},{5,3},{7,5},{... | collective-permute-start | bytes 774152 | tf_op jit(solution)/shard_map/ppermute | solution.py:57
  19.7 18.0 %collective-permute-start.1 = (f32[7,16,128]{2,1,0:T(8,128)S(1)}, f32[7,16,128]{2,1,0:T(8,128)S(1)}, u32[]{:S(2)}, u32[]{:S(2)}) collective-permute-start(f32[7,16,128]{2,1,0:T(8,128)S(1)} %get-tuple-element.17), channel_id=1, source_target_pairs={{0,16},{17,1},{16,32},{33,17},{32,48},{49,33},{48,64},{65,49},{64,... | collective-permute-start | bytes 172040 | tf_op jit(solution)/shard_map/ppermute | solution.py:57
  23.9 26.4 %copy-start.4 = (bf16[4,32,256]{2,1,0:T(8,128)(2,1)S(1)}, bf16[4,32,256]{2,1,0:T(8,128)(2,1)}, u32[]{:S(2)}) copy-start(bf16[4,32,256]{2,1,0:T(8,128)(2,1)} %prior.1) | copy-start | bytes 196612
  23.9 15.3 %collective-permute-start.2 = (f32[7,16,128]{2,1,0:T(8,128)S(1)}, f32[7,16,128]{2,1,0:T(8,128)S(1)}, u32[]{:S(2)}, u32[]{:S(2)}) collective-permute-start(f32[7,16,128]{2,1,0:T(8,128)S(1)} %get-tuple-element.18), channel_id=1, source_target_pairs={{1,16},{16,1},{17,32},{32,17},{33,48},{48,33},{49,64},{64,49},{65,... | collective-permute-start | bytes 172040 | tf_op jit(solution)/shard_map/ppermute | solution.py:57
  39.3 7.1 %collective-permute-start.5 = (f32[77,8,128]{2,1,0:T(8,128)S(1)}, f32[77,8,128]{2,1,0:T(8,128)S(1)}, u32[]{:S(2)}, u32[]{:S(2)}) collective-permute-start(f32[77,8,128]{2,1,0:T(8,128)S(1)} %get-tuple-element.21), channel_id=1, source_target_pairs={{0,2},{2,4},{4,6},{6,8},{8,10},{10,12},{12,14},{1,3},{3,5},{5,7},{... | collective-permute-start | bytes 946184 | tf_op jit(solution)/shard_map/ppermute | solution.py:57
  42.6 65.7 %copy-start.5 = (s32[32,256]{1,0:T(8,128)S(1)}, s32[32,256]{1,0:T(8,128)}, u32[]{:S(2)}) copy-start(s32[32,256]{1,0:T(8,128)} %ids.1) | copy-start | bytes 98308
  42.6 7.7 %collective-permute-start.6 = (f32[77,8,128]{2,1,0:T(8,128)S(1)}, f32[77,8,128]{2,1,0:T(8,128)S(1)}, u32[]{:S(2)}, u32[]{:S(2)}) collective-permute-start(f32[77,8,128]{2,1,0:T(8,128)S(1)} %get-tuple-element.22), channel_id=1, source_target_pairs={{2,0},{4,2},{6,4},{8,6},{10,8},{12,10},{14,12},{3,1},{5,3},{7,5},{... | collective-permute-start | bytes 946184 | tf_op jit(solution)/shard_map/ppermute | solution.py:57
  76.2 67.5 %collective-permute-start.7 = (f32[4,8,32,128]{3,2,1,0:T(8,128)S(1)}, f32[4,8,32,128]{3,2,1,0:T(8,128)S(1)}, u32[]{:S(2)}, u32[]{:S(2)}) collective-permute-start(f32[4,8,32,128]{3,2,1,0:T(8,128)S(1)} %get-tuple-element.24), channel_id=1, source_target_pairs={{0,1},{1,0},{2,3},{3,2},{4,5},{5,4},{6,7},{7,6},{8,9},{9,8},{10,11... | collective-permute-start | bytes 1572872 | tf_op jit(solution)/shard_map/ppermute | solution.py:57

commit v7 on v6

--- a/solution.py
+++ b/solution.py
@@ -27,7 +27,7 @@
 MIB = 1024 * 1024
 
 
-def call(kernel, out_shape, operands, scalars, scratch=(), limit=8):
+def call(kernel, out_shape, operands, scalars, scratch=(), limit=8, alias=None):
     specs = [SMEM] * scalars + [VMEM] * (len(operands) - scalars)
     many = isinstance(out_shape, (tuple, list))
     return pl.pallas_call(
@@ -38,6 +38,7 @@
         scratch_shapes=list(scratch),
         compiler_params=pltpu.CompilerParams(vmem_limit_bytes=limit * MIB),
         name=kernel.__name__,
+        input_output_aliases=alias or {},
     )(*operands)
 
 
@@ -123,6 +124,13 @@
             )
 
 
+def pack(
+    side, injection, adjoint, lon_wind, lat_wind, mixing, inner, cross, same, near, to_partner, first, last
+):
+    pack_edges(side, adjoint, lon_wind, lat_wind, mixing, inner, cross, same, near)
+    pack_main(side, injection, adjoint, lon_wind, lat_wind, mixing, inner, near, to_partner, first, last)
+
+
 def strips(partner, lon_same, lon_cross, own_below, own_above, first, last):
     first[0:MAIN] = partner[0:MAIN, 0:EDGE, :]
     last[0:MAIN] = partner[0:MAIN, ROWS - EDGE : ROWS, :]
@@ -136,64 +144,85 @@
         last[at] = rims[:, EDGE:, :]
 
 
-def steps(
+def turned(x, shift):
+    return pltpu.roll(x, shift % HALF, 1) if shift % HALF else x
+
+
+def rim(pair, begin):
+    ahead, behind = pair
+    lane = lax.broadcasted_iota(jnp.int32, ahead.shape, 1) < HALF // 2
+    return jnp.where(lane, turned(ahead, -begin), turned(behind, -begin - EDGE))
+
+
+def ends(k, inside, outside):
+    return jnp.where(k == 0, inside, outside), jnp.where(k == 0, outside, inside)
+
+
+MAIN_LANES = slice(0, HALF)
+WING_LANES = slice(HALF, WIDE)
+
+
+def eliminate_tile(tile, kab_ref, inv_ref, cp_ref):
+    at = pl.ds(pl.multiple_of(tile * 8, 8), 8)
+    carried = jnp.zeros((8, WIDE), jnp.float32)
+    kbelow = jnp.zeros((8, WIDE), jnp.float32)
+    for level in range(LEVELS):
+        kabove = kab_ref[level, at, :]
+        inverse = 1.0 / (1.0 + kabove + kbelow * (1.0 + carried))
+        carried = -kabove * inverse
+        inv_ref[level, at, :] = inverse
+        cp_ref[level, at, :] = carried
+        kbelow = kabove
+
+
+def solve_tile(tile, field_ref, kab_ref, inv_ref, cp_ref, red_ref):
+    at = pl.ds(pl.multiple_of(tile * 8, 8), 8)
+    carried = [None] * TRACERS
+    for level in range(LEVELS):
+        inverse = inv_ref[level, at, :]
+        if level:
+            kbelow = kab_ref[level - 1, at, :]
+        for tracer in range(TRACERS):
+            rhs = field_ref[tracer, level, at, :]
+            if level:
+                rhs = rhs + kbelow * carried[tracer]
+            carried[tracer] = rhs * inverse
+            red_ref[tracer, level] = carried[tracer]
+    for tracer in range(TRACERS):
+        field_ref[tracer, LEVELS - 1, at, :] = carried[tracer]
+    for level in reversed(range(LEVELS - 1)):
+        cprime = cp_ref[level, at, :]
+        for tracer in range(TRACERS):
+            carried[tracer] = red_ref[tracer, level] - cprime * carried[tracer]
+            field_ref[tracer, level, at, :] = carried[tracer]
+
+
+def prepare(
     side, injection, adjoint, lon_wind, lat_wind, mixing, partner, near, lon_same, lon_cross,
-    own_below, own_above, below, above, prior,
-    kept, returned, weights,
-    field_ref, lon_ref, lat_ref, kab_ref, inv_ref, cp_ref, red_ref, inj_ref,
+    field_ref, lon_ref, lat_ref, kab_ref, inv_ref, cp_ref, inj_ref, red_ref,
 ):
     refs = (adjoint, lon_wind, lat_wind, mixing)
     k = side[0]
     mine = half_at(k)
-    rows = slice(0, ROWS)
-    low = slice(0, EDGE)
-    mid = slice(EDGE, EDGE + ROWS)
-    top = slice(EDGE + ROWS, TALL)
-    main = slice(0, HALF)
-    wing = slice(HALF, WIDE)
-
-    west = k == 0
-    lane = lax.broadcasted_iota(jnp.int32, (FOLD, HALF), 1) < HALF // 2
-
-    def turned(x, shift):
-        return pltpu.roll(x, shift % HALF, 1) if shift % HALF else x
-
-    def rim(pair, begin):
-        ahead, behind = pair
-        return jnp.where(lane[: ahead.shape[0]], turned(ahead, -begin), turned(behind, -begin - EDGE))
-
-    def ends(inside, outside):
-        return jnp.where(west, inside, outside), jnp.where(west, outside, inside)
-
     for group in range(2):
         base = (k if group == 0 else 1 - k) * HERE
-        under, over = (own_below, own_above) if group == 0 else (below, above)
         for field in range(FIELDS):
-            if group == 0:
-                inside = (own_below[MAIN + field], near[field], own_above[MAIN + field])
-            else:
-                begin = field % 2 * FOLD
-                inside = (below[MAIN + field], partner[MAIN + field // 2, begin : begin + FOLD, :], above[MAIN + field])
-            at = MAIN + (1 + group) * FIELDS + field
-            outside = (below[at], (lon_same, lon_cross)[group][field], above[at])
-            south_rim, middle_rim, north_rim = (ends(*pair) for pair in zip(inside, outside))
+            begin = field % 2 * FOLD
+            inside = near[field] if group == 0 else partner[MAIN + field // 2, begin : begin + FOLD, :]
+            pair = ends(k, inside, (lon_same, lon_cross)[group][field])
             for level in range(HERE):
-                at = field * HERE + level
                 where = base + level
                 if field < TRACERS:
                     target = field_ref.at[field, where]
                 else:
                     target = (lon_ref, lat_ref, kab_ref)[field - TRACERS].at[where]
-                target[low, main] = under[at]
-                target[top, main] = over[at]
                 if group == 0:
-                    target[mid, main] = own_plane(refs, field, level, rows, mine)
+                    plane = own_plane(refs, field, level, slice(0, ROWS), mine)
                 else:
-                    target[mid, main] = partner[at]
-                target[low, wing] = rim(south_rim, EDGE * (HERE + level))
-                target[EDGE : EDGE + FOLD, wing] = rim(middle_rim, EDGE * level)
-                target[EDGE + FOLD : EDGE + ROWS, wing] = rim(middle_rim, EDGE * (HERE + level))
-                target[top, wing] = rim(north_rim, EDGE * level)
+                    plane = partner[field * HERE + level]
+                target[EDGE : EDGE + ROWS, MAIN_LANES] = plane
+                target[EDGE : EDGE + FOLD, WING_LANES] = rim(pair, EDGE * level)
+                target[EDGE + FOLD : EDGE + ROWS, WING_LANES] = rim(pair, EDGE * (HERE + level))
     for tracer in range(TRACERS):
         for level in range(HERE):
             row = tracer * HERE + level
@@ -205,45 +234,62 @@
             )
     kab_ref[LEVELS - 1] = jnp.zeros((TALL, WIDE), jnp.float32)
 
-    def pivots(tile, _):
-        at = pl.ds(pl.multiple_of(tile * 8, 8), 8)
-        carried = jnp.zeros((8, WIDE), jnp.float32)
-        kbelow = jnp.zeros((8, WIDE), jnp.float32)
-        for level in range(LEVELS):
-            kabove = kab_ref[level, at, :]
-            inverse = 1.0 / (1.0 + kabove + kbelow * (1.0 + carried))
-            carried = -kabove * inverse
-            inv_ref[level, at, :] = inverse
-            cp_ref[level, at, :] = carried
-            kbelow = kabove
+    def inner(tile, _):
+        eliminate_tile(tile, kab_ref, inv_ref, cp_ref)
+        solve_tile(tile, field_ref, kab_ref, inv_ref, cp_ref, red_ref)
         return 0
 
-    lax.fori_loop(0, TALL // 8, pivots, 0)
+    lax.fori_loop(1, 1 + ROWS // 8, inner, 0)
+
+
+def steps(
+    side, own_below, own_above, below, above, prior, inj_ref,
+    field_in, lon_in, lat_in, kab_in, inv_in, cp_in,
+    kept, returned, weights,
+    field_ref, lon_ref, lat_ref, kab_ref, inv_ref, cp_ref, red_ref,
+):
+    k = side[0]
+    mine = half_at(k)
+    mid = slice(EDGE, EDGE + ROWS)
+    low = slice(0, EDGE)
+    top = slice(EDGE + ROWS, TALL)
+    main = MAIN_LANES
+    wing = WING_LANES
+    for group in range(2):
+        base = (k if group == 0 else 1 - k) * HERE
+        under, over = (own_below, own_above) if group == 0 else (below, above)
+        for field in range(FIELDS):
+            near_at = MAIN + field
+            far_at = MAIN + (1 + group) * FIELDS + field
+            south_rim = ends(k, under[near_at], below[far_at])
+            north_rim = ends(k, over[near_at], above[far_at])
+            for level in range(HERE):
+                at = field * HERE + level
+                where = base + level
+                if field < TRACERS:
+                    target = field_ref.at[field, where]
+                else:
+                    target = (lon_ref, lat_ref, kab_ref)[field - TRACERS].at[where]
+                target[low, main] = under[at]
+                target[top, main] = over[at]
+                target[low, wing] = rim(south_rim, EDGE * (HERE + level))
+                target[top, wing] = rim(north_rim, EDGE * level)
+    kab_ref[LEVELS - 1] = jnp.zeros((TALL, WIDE), jnp.float32)
+    last_tile = TALL // 8 - 1
+
+    def outer(i, _):
+        eliminate_tile(i * last_tile, kab_ref, inv_ref, cp_ref)
+        return 0
+
+    lax.fori_loop(0, 2, outer, 0)
 
     def one_step(step, _):
-        def solve(tile, _):
-            at = pl.ds(pl.multiple_of(tile * 8, 8), 8)
-            carried = [jnp.zeros((8, WIDE), jnp.float32) for _ in range(TRACERS)]
-            for level in range(LEVELS):
-                inverse = inv_ref[level, at, :]
-                if level:
-                    kbelow = kab_ref[level - 1, at, :]
-                for tracer in range(TRACERS):
-                    rhs = field_ref[tracer, level, at, :]
-                    if level:
-                        rhs = rhs + kbelow * carried[tracer]
-                    carried[tracer] = rhs * inverse
-                    red_ref[tracer, level] = carried[tracer]
-            for tracer in range(TRACERS):
-                field_ref[tracer, LEVELS - 1, at, :] = carried[tracer]
-            for level in reversed(range(LEVELS - 1)):
-                cprime = cp_ref[level, at, :]
-                for tracer in range(TRACERS):
-                    carried[tracer] = red_ref[tracer, level] - cprime * carried[tracer]
-                    field_ref[tracer, level, at, :] = carried[tracer]
+        def solve(i, _):
+            tile = jnp.where(step == 0, i * last_tile, i)
+            solve_tile(tile, field_ref, kab_ref, inv_ref, cp_ref, red_ref)
             return 0
 
-        lax.fori_loop(0, TALL // 8, solve, 0)
+        lax.fori_loop(0, jnp.where(step == 0, 2, TALL // 8), solve, 0)
 
         def weigh(tile, _):
             at = pl.ds(pl.multiple_of(tile * 8 + EDGE, 8), 8)
@@ -353,8 +399,17 @@
     own = tuple(hold(x) for x in (adjoint, courant_lon, courant_lat, mixing))
     injection = hold(injection)
 
-    edge_inner, edge_cross, edge_same, edge_near = call(
-        pack_edges, tuple(near(FIELDS, FOLD, HALF) for _ in range(4)), (side, *raw), 1
+    strip = MAIN + FIELDS
+    _, edge_cross, edge_same, edge_near, to_partner, first, last = call(
+        pack,
+        (
+            *(near(FIELDS, FOLD, HALF) for _ in range(4)),
+            near(PLANES, ROWS, HALF),
+            near(strip, EDGE, HALF),
+            near(strip, EDGE, HALF),
+        ),
+        (side, injection, *raw),
+        1,
     )
     same = []
     cross = []
@@ -367,13 +422,6 @@
     lon_cross = permute(edge_cross, ("lon", "lev"), cross)
     lon_same = permute(edge_same, ("lon", "lev"), same)
 
-    strip = MAIN + FIELDS
-    to_partner, first, last = call(
-        pack_main,
-        (near(PLANES, ROWS, HALF), near(strip, EDGE, HALF), near(strip, EDGE, HALF)),
-        (side, injection, *own, edge_inner, edge_near),
-        1,
-    )
     partner = permute(to_partner, "lev", [(0, 1), (1, 0)])
     own_below = permute(last, "lat", north)
     own_above = permute(first, "lat", south)
@@ -389,30 +437,29 @@
     above = permute(first, "lat", south)
 
     block = (LEVELS, TALL, WIDE)
+    tile = pltpu.VMEM((TRACERS, LEVELS, 8, WIDE), jnp.float32)
+    arrays = (near(TRACERS, *block), *(near(*block) for _ in range(5)))
+    *state, inj = call(
+        prepare,
+        (*arrays, near(TRACERS, LEVELS, 8, HALF)),
+        (side, injection, *own, partner, edge_near, lon_same, lon_cross),
+        1,
+        [tile],
+    )
     kept, returned, weights = call(
         steps,
         (
             near(TRACERS, HERE, ROWS, HALF),
             near(TRACERS, HERE, ROWS, HALF),
             near(STEPS * TRACERS, ROWS, HALF),
+            *arrays,
         ),
-        (
-            side, injection, *own, partner, edge_near, lon_same, lon_cross,
-            own_below, own_above, below, above, hold(prior_flux),
-        ),
+        (side, own_below, own_above, below, above, hold(prior_flux), hold(inj), *(hold(x) for x in state)),
         1,
-        [
-            pltpu.VMEM((TRACERS, *block), jnp.float32),
-            pltpu.VMEM(block, jnp.float32),
-            pltpu.VMEM(block, jnp.float32),
-            pltpu.VMEM(block, jnp.float32),
-            pltpu.VMEM(block, jnp.float32),
-            pltpu.VMEM(block, jnp.float32),
-            pltpu.VMEM((TRACERS, LEVELS, 8, WIDE), jnp.float32),
-            pltpu.VMEM((TRACERS, LEVELS, 8, HALF), jnp.float32),
-        ],
-        24,
-    )
+        [tile],
+        8,
+        {7 + i: 3 + i for i in range(6)},
+    )[:3]
     received = permute(returned, "lev", [(0, 1), (1, 0)])
     sums = call(
         regions,

time: 145 us -> 143 us (0.986)
  waiting for transfers between devices: 16.5 us -> 14.7 us
    ppermute x8, waiting for transfers between devices: 16.5 us -> 14.7 us  [permute(): return hold(lax.ppermute(x, axes, pairs))]
  transfers between devices with their start and end apart: 8 -> 8, of which waited for: 4 -> 4; matrix products, arithmetic and copies ran while one was open for 1% -> 1% of each run, Pallas kernels for 2% -> 3%
where the time goes in v7:
time: 143 us; the launch traced here: 142 us
  starting transfers between devices  61.9 us (43%)
  blocking collectives  31.8 us (22%)
  Pallas kernels  31.2 us (22%)
  waiting for transfers between devices  14.7 us (10%)
  local copies, waits for them, and re-layouts  1.47 us (1%)
    ppermute x8, starting transfers between devices, permute(): return hold(lax.ppermute(x, axes, pairs))  61.9 us
    all_to_all x1, blocking collectives, body(): pieces = lax.all_to_all(sums, ('lon', 'lat', 'lev'), 0, 0, tiled=True)  31.8 us
    pallas_call x6, Pallas kernels, call(): pl.pallas_call(kernel, out_shape=out_shape, in_specs=specs, out_specs=tup...  31.2 us
    ppermute x8, waiting for transfers between devices, permute(): return hold(lax.ppermute(x, axes, pairs))  14.7 us
  transfers between devices with their start and end apart: 8, of which 4 were waited for; matrix products, arithmetic and copies ran while one was open for 1% of the time, Pallas kernels for 3%

profile of v7, /device:TPU:1, one launch (start us, length us, event | category | flops | bytes accessed | tf_op | source)
XLA Modules:
  0.0 142.4 jit_solution(13072389249909642243)
XLA Ops:
  0.7 0.8 copy-done.6
  1.5 2.8 %pack.1 = (f32[7,16,128]{2,1,0:T(8,128)}, f32[7,16,128]{2,1,0:T(8,128)S(1)}, f32[7,16,128]{2,1,0:T(8,128)S(1)}, f32[7,16,128]{2,1,0:T(8,128)S(1)}, f32[61,32,128...) custom-call(s32[1]{0:T(128)} %bitcast.side, f32[4,8]{1,0:T(4,128)S(1)} %copy-done.6, ...), custom_call_target="tpu_custom_call" | custom-call | tf_op jit(solution)/shard_map/pack/pallas_call | solution.py:33
  4.2 11.5 %collective-permute-start.2 = (f32[61,32,128]{2,1,0:T(8,128)S(1)}, f32[61,32,128]{2,1,0:T(8,128)S(1)}, u32[]{:S(2)}, u32[]{:S(2)}) collective-permute-start(f32[61,32,128]{2,1,0:T(8,128)S(1)} %get-tuple-element.22), channel_id=1, source_target_pairs={{0,1},{1,0},{2,3},{3,2},{4,5},{5,4},{6,7},{7,6},{8,9},{9,8},{10,11... | collective-permute-start | bytes 2998280 | tf_op jit(solution)/shard_map/ppermute | solution.py:58
  15.7 3.2 %collective-permute-start = (f32[63,8,128]{2,1,0:T(8,128)S(1)}, f32[63,8,128]{2,1,0:T(8,128)S(1)}, u32[]{:S(2)}, u32[]{:S(2)}) collective-permute-start(f32[63,8,128]{2,1,0:T(8,128)S(1)} %get-tuple-element.20), channel_id=1, source_target_pairs={{0,2},{2,4},{4,6},{6,8},{8,10},{10,12},{12,14},{1,3},{3,5},{5,7},{... | collective-permute-start | bytes 774152 | tf_op jit(solution)/shard_map/ppermute | solution.py:58
  18.9 1.3 collective-permute-start.1
  20.2 4.2 %collective-permute-start.3 = (f32[7,16,128]{2,1,0:T(8,128)S(1)}, f32[7,16,128]{2,1,0:T(8,128)S(1)}, u32[]{:S(2)}, u32[]{:S(2)}) collective-permute-start(f32[7,16,128]{2,1,0:T(8,128)S(1)} %get-tuple-element.23), channel_id=1, source_target_pairs={{0,16},{17,1},{16,32},{33,17},{32,48},{49,33},{48,64},{65,49},{64,... | collective-permute-start | bytes 172040 | tf_op jit(solution)/shard_map/ppermute | solution.py:58
  24.5 5.1 %collective-permute-start.4 = (f32[7,16,128]{2,1,0:T(8,128)S(1)}, f32[7,16,128]{2,1,0:T(8,128)S(1)}, u32[]{:S(2)}, u32[]{:S(2)}) collective-permute-start(f32[7,16,128]{2,1,0:T(8,128)S(1)} %get-tuple-element.24), channel_id=1, source_target_pairs={{1,16},{16,1},{17,32},{32,17},{33,48},{48,33},{49,64},{64,49},{65,... | collective-permute-start | bytes 172040 | tf_op jit(solution)/shard_map/ppermute | solution.py:58
  29.6 8.7 %collective-permute-done.3.lon_same = f32[7,16,128]{2,1,0:T(8,128)S(1)} collective-permute-done((f32[7,16,128]{2,1,0:T(8,128)S(1)}, f32[7,16,128]{2,1,0:T(8,128)S(1)}, u32[]{:S(2)}, u32[]{:S(2)}) %collective-permute-start.3) | collective-permute-done | bytes 57376 | tf_op jit(solution)/shard_map/ppermute | solution.py:58
  38.3 1.5 %collective-permute-done.4.lon_cross = f32[7,16,128]{2,1,0:T(8,128)S(1)} collective-permute-done((f32[7,16,128]{2,1,0:T(8,128)S(1)}, f32[7,16,128]{2,1,0:T(8,128)S(1)}, u32[]{:S(2)}, u32[]{:S(2)}) %collective-permute-start.4) | collective-permute-done | bytes 57376 | tf_op jit(solution)/shard_map/ppermute | solution.py:58
  39.8 0.0 collective-permute-done.own_below
  39.8 0.0 collective-permute-done.1.own_above
  39.8 0.0 collective-permute-done.2.partner
  39.9 3.2 %collective-permute-start.5 = (f32[77,8,128]{2,1,0:T(8,128)S(1)}, f32[77,8,128]{2,1,0:T(8,128)S(1)}, u32[]{:S(2)}, u32[]{:S(2)}) collective-permute-start(f32[77,8,128]{2,1,0:T(8,128)S(1)} %get-tuple-element.25), channel_id=1, source_target_pairs={{0,2},{2,4},{4,6},{6,8},{8,10},{10,12},{12,14},{1,3},{3,5},{5,7},{... | collective-permute-start | bytes 946184 | tf_op jit(solution)/shard_map/ppermute | solution.py:58
  43.1 1.3 collective-permute-start.6
  44.4 1.9 %prepare.1 = (f32[4,16,48,256]{3,2,1,0:T(8,128)S(1)}, f32[16,48,256]{2,1,0:T(8,128)S(1)}, f32[16,48,256]{2,1,0:T(8,128)S(1)}, f32[16,48,256]{2,1,0:T(8,128)S(1)}...) custom-call(s32[1]{0:T(128)} %bitcast.side, f32[4,8]{1,0:T(4,128)S(1)} %copy-done.6, ...), custom_call_target="tpu_custom_call" | custom-call | tf_op jit(solution)/shard_map/prepare/pallas_call | solution.py:33
  46.4 0.6 collective-permute-done.5.below
  47.0 3.8 %collective-permute-done.6.above = f32[77,8,128]{2,1,0:T(8,128)S(1)} collective-permute-done((f32[77,8,128]{2,1,0:T(8,128)S(1)}, f32[77,8,128]{2,1,0:T(8,128)S(1)}, u32[]{:S(2)}, u32[]{:S(2)}) %collective-permute-start.6) | collective-permute-done | bytes 315424 | tf_op jit(solution)/shard_map/ppermute | solution.py:58
  50.8 23.0 %steps.1 = (f32[4,8,32,128]{3,2,1,0:T(8,128)S(1)}, f32[4,8,32,128]{3,2,1,0:T(8,128)S(1)}, f32[24,32,128]{2,1,0:T(8,128)S(1)}, f32[4,16,48,256]{3,2,1,0:T(8,128)S...) custom-call(s32[1]{0:T(128)} %bitcast.side, ...), custom_call_target="tpu_custom_call", output_to_operand_aliasing={{3}: (7, {}), {4}: (8, {}), {5}: (9, {}), {6}: (10, {}), {7... | custom-call | tf_op jit(solution)/shard_map/steps/pallas_call | solution.py:33
  73.8 32.1 %collective-permute-start.7 = (f32[4,8,32,128]{3,2,1,0:T(8,128)S(1)}, f32[4,8,32,128]{3,2,1,0:T(8,128)S(1)}, u32[]{:S(2)}, u32[]{:S(2)}) collective-permute-start(f32[4,8,32,128]{3,2,1,0:T(8,128)S(1)} %get-tuple-element.36), channel_id=1, source_target_pairs={{0,1},{1,0},{2,3},{3,2},{4,5},{5,4},{6,7},{7,6},{8,9},{9,8},{10,11... | collective-permute-start | bytes 1572872 | tf_op jit(solution)/shard_map/ppermute | solution.py:58
  105.9 2.4 %regions.1 = f32[512,128]{1,0:T(8,128)S(1)} custom-call(s32[1]{0:T(128)} %bitcast.side, f32[24,32,128]{2,1,0:T(8,128)S(1)} %get-tuple-element.37.weights, s32[32,256]{1,0:T(8,128)S(1)} %copy-done.5), custom_call_target="tpu_custom_call" | custom-call | tf_op jit(solution)/shard_map/regions/pallas_call | solution.py:33
  108.3 31.8 %all_to_all.9 = f32[512,1,128]{2,1,0:T(1,128)S(1)} all-to-all(f32[512,1,128]{2,1,0:T(1,128)S(1)} %bitcast.5), channel_id=1, replica_groups=mesh['lon'=32,'lat'=8,'lev'=2] {'lon','lat','lev'}, dimensions={0} | all-to-all | bytes 524288 | tf_op jit(solution)/shard_map/all_to_all | solution.py:472
  140.2 0.6 reduce_sum.9
  140.7 0.7 reshape.13
  141.4 1.0 join.1
  (15 shorter events, 0.1 us)
Async XLA Ops:
  0.6 43.8 %copy-start.3 = (bf16[8,32,256]{2,1,0:T(8,128)(2,1)S(1)}, bf16[8,32,256]{2,1,0:T(8,128)(2,1)}, u32[]{:S(2)}) copy-start(bf16[8,32,256]{2,1,0:T(8,128)(2,1)} %mixing.3) | copy-start | bytes 393220
  0.6 43.8 %copy-start.2 = (bf16[8,32,256]{2,1,0:T(8,128)(2,1)S(1)}, bf16[8,32,256]{2,1,0:T(8,128)(2,1)}, u32[]{:S(2)}) copy-start(bf16[8,32,256]{2,1,0:T(8,128)(2,1)} %lat_wind.3) | copy-start | bytes 393220
  0.7 43.8 %copy-start.1 = (bf16[8,32,256]{2,1,0:T(8,128)(2,1)S(1)}, bf16[8,32,256]{2,1,0:T(8,128)(2,1)}, u32[]{:S(2)}) copy-start(bf16[8,32,256]{2,1,0:T(8,128)(2,1)} %lon_wind.3) | copy-start | bytes 393220
  0.7 43.8 %copy-start = (f32[4,8,32,256]{3,2,1,0:T(8,128)S(1)}, f32[4,8,32,256]{3,2,1,0:T(8,128)}, u32[]{:S(2)}) copy-start(f32[4,8,32,256]{3,2,1,0:T(8,128)} %adjoint.3) | copy-start | bytes 3145732
  0.7 50.1 %copy-start.4 = (bf16[4,32,256]{2,1,0:T(8,128)(2,1)S(1)}, bf16[4,32,256]{2,1,0:T(8,128)(2,1)}, u32[]{:S(2)}) copy-start(bf16[4,32,256]{2,1,0:T(8,128)(2,1)} %prior.1) | copy-start | bytes 196612
  0.7 0.8 copy-start.6
  4.2 35.6 %collective-permute-start.2 = (f32[61,32,128]{2,1,0:T(8,128)S(1)}, f32[61,32,128]{2,1,0:T(8,128)S(1)}, u32[]{:S(2)}, u32[]{:S(2)}) collective-permute-start(f32[61,32,128]{2,1,0:T(8,128)S(1)} %get-tuple-element.22), channel_id=1, source_target_pairs={{0,1},{1,0},{2,3},{3,2},{4,5},{5,4},{6,7},{7,6},{8,9},{9,8},{10,11... | collective-permute-start | bytes 2998280 | tf_op jit(solution)/shard_map/ppermute | solution.py:58
  15.7 24.1 %collective-permute-start = (f32[63,8,128]{2,1,0:T(8,128)S(1)}, f32[63,8,128]{2,1,0:T(8,128)S(1)}, u32[]{:S(2)}, u32[]{:S(2)}) collective-permute-start(f32[63,8,128]{2,1,0:T(8,128)S(1)} %get-tuple-element.20), channel_id=1, source_target_pairs={{0,2},{2,4},{4,6},{6,8},{8,10},{10,12},{12,14},{1,3},{3,5},{5,7},{... | collective-permute-start | bytes 774152 | tf_op jit(solution)/shard_map/ppermute | solution.py:58
  18.9 20.9 %collective-permute-start.1 = (f32[63,8,128]{2,1,0:T(8,128)S(1)}, f32[63,8,128]{2,1,0:T(8,128)S(1)}, u32[]{:S(2)}, u32[]{:S(2)}) collective-permute-start(f32[63,8,128]{2,1,0:T(8,128)S(1)} %get-tuple-element.21), channel_id=1, source_target_pairs={{2,0},{4,2},{6,4},{8,6},{10,8},{12,10},{14,12},{3,1},{5,3},{7,5},{... | collective-permute-start | bytes 774152 | tf_op jit(solution)/shard_map/ppermute | solution.py:58
  20.2 18.0 %collective-permute-start.3 = (f32[7,16,128]{2,1,0:T(8,128)S(1)}, f32[7,16,128]{2,1,0:T(8,128)S(1)}, u32[]{:S(2)}, u32[]{:S(2)}) collective-permute-start(f32[7,16,128]{2,1,0:T(8,128)S(1)} %get-tuple-element.23), channel_id=1, source_target_pairs={{0,16},{17,1},{16,32},{33,17},{32,48},{49,33},{48,64},{65,49},{64,... | collective-permute-start | bytes 172040 | tf_op jit(solution)/shard_map/ppermute | solution.py:58
  24.5 15.4 %collective-permute-start.4 = (f32[7,16,128]{2,1,0:T(8,128)S(1)}, f32[7,16,128]{2,1,0:T(8,128)S(1)}, u32[]{:S(2)}, u32[]{:S(2)}) collective-permute-start(f32[7,16,128]{2,1,0:T(8,128)S(1)} %get-tuple-element.24), channel_id=1, source_target_pairs={{1,16},{16,1},{17,32},{32,17},{33,48},{48,33},{49,64},{64,49},{65,... | collective-permute-start | bytes 172040 | tf_op jit(solution)/shard_map/ppermute | solution.py:58
  39.9 7.1 %collective-permute-start.5 = (f32[77,8,128]{2,1,0:T(8,128)S(1)}, f32[77,8,128]{2,1,0:T(8,128)S(1)}, u32[]{:S(2)}, u32[]{:S(2)}) collective-permute-start(f32[77,8,128]{2,1,0:T(8,128)S(1)} %get-tuple-element.25), channel_id=1, source_target_pairs={{0,2},{2,4},{4,6},{6,8},{8,10},{10,12},{12,14},{1,3},{3,5},{5,7},{... | collective-permute-start | bytes 946184 | tf_op jit(solution)/shard_map/ppermute | solution.py:58
  43.1 7.7 %collective-permute-start.6 = (f32[77,8,128]{2,1,0:T(8,128)S(1)}, f32[77,8,128]{2,1,0:T(8,128)S(1)}, u32[]{:S(2)}, u32[]{:S(2)}) collective-permute-start(f32[77,8,128]{2,1,0:T(8,128)S(1)} %get-tuple-element.26), channel_id=1, source_target_pairs={{2,0},{4,2},{6,4},{8,6},{10,8},{12,10},{14,12},{3,1},{5,3},{7,5},{... | collective-permute-start | bytes 946184 | tf_op jit(solution)/shard_map/ppermute | solution.py:58
  50.8 55.1 %copy-start.5 = (s32[32,256]{1,0:T(8,128)S(1)}, s32[32,256]{1,0:T(8,128)}, u32[]{:S(2)}) copy-start(s32[32,256]{1,0:T(8,128)} %ids.1) | copy-start | bytes 98308
  73.8 67.6 %collective-permute-start.7 = (f32[4,8,32,128]{3,2,1,0:T(8,128)S(1)}, f32[4,8,32,128]{3,2,1,0:T(8,128)S(1)}, u32[]{:S(2)}, u32[]{:S(2)}) collective-permute-start(f32[4,8,32,128]{3,2,1,0:T(8,128)S(1)} %get-tuple-element.36), channel_id=1, source_target_pairs={{0,1},{1,0},{2,3},{3,2},{4,5},{5,4},{6,7},{7,6},{8,9},{9,8},{10,11... | collective-permute-start | bytes 1572872 | tf_op jit(solution)/shard_map/ppermute | solution.py:58

commit v8 on v7

--- a/solution.py
+++ b/solution.py
@@ -175,7 +175,7 @@
         kbelow = kabove
 
 
-def solve_tile(tile, field_ref, kab_ref, inv_ref, cp_ref, red_ref):
+def solve_tile(tile, field_ref, solved_ref, kab_ref, inv_ref, cp_ref, red_ref):
     at = pl.ds(pl.multiple_of(tile * 8, 8), 8)
     carried = [None] * TRACERS
     for level in range(LEVELS):
@@ -189,17 +189,69 @@
             carried[tracer] = rhs * inverse
             red_ref[tracer, level] = carried[tracer]
     for tracer in range(TRACERS):
-        field_ref[tracer, LEVELS - 1, at, :] = carried[tracer]
+        solved_ref[tracer, LEVELS - 1, at, :] = carried[tracer]
     for level in reversed(range(LEVELS - 1)):
         cprime = cp_ref[level, at, :]
         for tracer in range(TRACERS):
             carried[tracer] = red_ref[tracer, level] - cprime * carried[tracer]
-            field_ref[tracer, level, at, :] = carried[tracer]
+            solved_ref[tracer, level, at, :] = carried[tracer]
+
+
+TILES = TALL // 8
+UNROLL = 4
+
+
+def rows_of(tile):
+    return pl.ds(pl.multiple_of(tile * 8, 8), 8)
+
+
+def advect_tile(level, tile, field_ref, solved_ref, lon_ref, lat_ref, wings):
+    at = rows_of(tile)
+    before = rows_of(jnp.where(tile == 0, TILES - 1, tile - 1))
+    after = rows_of(jnp.where(tile == TILES - 1, 0, tile + 1))
+    sides = (MAIN_LANES, WING_LANES)
+    count = 2 if wings else 1
+    row = lax.broadcasted_iota(jnp.int32, (8, HALF), 0)
+    lane = lax.broadcasted_iota(jnp.int32, (8, HALF), 1)
+    rates = []
+    for side in sides[:count]:
+        lon = lon_ref[level, at, side]
+        lat = lat_ref[level, at, side]
+        rates.append((lon > 0.0, lat > 0.0, jnp.abs(lon), jnp.abs(lat)))
+    for tracer in range(TRACERS):
+        cells = [solved_ref[tracer, level, at, side] for side in sides]
+        for i, side in enumerate(sides[:count]):
+            east, north, lon, lat = rates[i]
+            here = cells[i]
+            beside = cells[1 - i]
+            along = jnp.where(
+                east,
+                pltpu.roll(jnp.where(lane == 0, beside, here), HALF - 1, 1),
+                pltpu.roll(jnp.where(lane == HALF - 1, beside, here), 1, 1),
+            )
+            across = jnp.where(
+                north,
+                pltpu.roll(jnp.where(row == 0, solved_ref[tracer, level, after, side], here), 7, 0),
+                pltpu.roll(jnp.where(row == 7, solved_ref[tracer, level, before, side], here), 1, 0),
+            )
+            field_ref[tracer, level, at, side] = here + lon * (along - here) + lat * (across - here)
+
+
+def advect_tiles(count, tile_of, field_ref, solved_ref, lon_ref, lat_ref, wings=True):
+    blocks = LEVELS // UNROLL
+
+    def some(i, _):
+        tile = tile_of(i // blocks)
+        for level in range(UNROLL):
+            advect_tile(i % blocks * UNROLL + level, tile, field_ref, solved_ref, lon_ref, lat_ref, wings)
+        return 0
+
+    lax.fori_loop(0, count * blocks, some, 0)
 
 
 def prepare(
     side, injection, adjoint, lon_wind, lat_wind, mixing, partner, near, lon_same, lon_cross,
-    field_ref, lon_ref, lat_ref, kab_ref, inv_ref, cp_ref, inj_ref, red_ref,
+    field_ref, solved_ref, lon_ref, lat_ref, kab_ref, inv_ref, cp_ref, inj_ref, red_ref,
 ):
     refs = (adjoint, lon_wind, lat_wind, mixing)
     k = side[0]
@@ -236,17 +288,18 @@
 
     def inner(tile, _):
         eliminate_tile(tile, kab_ref, inv_ref, cp_ref)
-        solve_tile(tile, field_ref, kab_ref, inv_ref, cp_ref, red_ref)
+        solve_tile(tile, field_ref, solved_ref, kab_ref, inv_ref, cp_ref, red_ref)
         return 0
 
     lax.fori_loop(1, 1 + ROWS // 8, inner, 0)
+    advect_tiles(2, lambda i: i + 2, field_ref, solved_ref, lon_ref, lat_ref)
 
 
 def steps(
     side, own_below, own_above, below, above, prior, inj_ref,
-    field_in, lon_in, lat_in, kab_in, inv_in, cp_in,
+    field_in, solved_in, lon_in, lat_in, kab_in, inv_in, cp_in,
     kept, returned, weights,
-    field_ref, lon_ref, lat_ref, kab_ref, inv_ref, cp_ref, red_ref,
+    field_ref, solved_ref, lon_ref, lat_ref, kab_ref, inv_ref, cp_ref, red_ref,
 ):
     k = side[0]
     mine = half_at(k)
@@ -286,7 +339,7 @@
     def one_step(step, _):
         def solve(i, _):
             tile = jnp.where(step == 0, i * last_tile, i)
-            solve_tile(tile, field_ref, kab_ref, inv_ref, cp_ref, red_ref)
+            solve_tile(tile, field_ref, solved_ref, kab_ref, inv_ref, cp_ref, red_ref)
             return 0
 
         lax.fori_loop(0, jnp.where(step == 0, 2, TALL // 8), solve, 0)
@@ -297,51 +350,23 @@
             for tracer in range(TRACERS):
                 total = jnp.zeros((8, HALF), jnp.float32)
                 for level in range(LEVELS):
-                    total = total + inj_ref[tracer, level] * field_ref[tracer, level, at, main]
+                    total = total + inj_ref[tracer, level] * solved_ref[tracer, level, at, main]
                 weights[step * TRACERS + tracer, to, :] = total
             return 0
 
         lax.fori_loop(0, ROWS // 8, weigh, 0)
 
-        def advect(level, _):
-            lon = lon_ref[level]
-            lat = lat_ref[level]
-            east = lon > 0.0
-            north = lat > 0.0
-            lon = jnp.abs(lon)
-            lat = jnp.abs(lat)
-            centre = 1.0 - lon - lat
-            for tracer in range(TRACERS):
-                cells = field_ref[tracer, level]
-                along = jnp.where(east, pltpu.roll(cells, WIDE - 1, 1), pltpu.roll(cells, 1, 1))
-                across = jnp.where(north, pltpu.roll(cells, TALL - 1, 0), pltpu.roll(cells, 1, 0))
-                field_ref[tracer, level] = centre * cells + lon * along + lat * across
-            return 0
-
-        def settle(level, _):
-            around = slice(0, TALL)
-            lon = lon_ref[level, mid, main]
-            lat = lat_ref[level, mid, main]
-            for tracer in range(TRACERS):
-                cells = field_ref[tracer, level, mid, :]
-                column = field_ref[tracer, level, around, main]
-                along = jnp.where(
-                    lon > 0.0, pltpu.roll(cells, WIDE - 1, 1)[:, main], pltpu.roll(cells, 1, 1)[:, main]
-                )
-                across = jnp.where(lat > 0.0, pltpu.roll(column, TALL - 1, 0)[mid], pltpu.roll(column, 1, 0)[mid])
-                here = cells[:, main]
-                field_ref[tracer, level, mid, main] = (
-                    (1.0 - jnp.abs(lon) - jnp.abs(lat)) * here + jnp.abs(lon) * along + jnp.abs(lat) * across
-                )
-            return 0
-
         @pl.when(step < STEPS - 1)
         def _():
-            lax.fori_loop(0, LEVELS, advect, 0)
+            advect_tiles(
+                jnp.where(step == 0, TILES - 2, TILES),
+                lambda i: jnp.where((step == 0) & (i >= 2), i + 2, i),
+                field_ref, solved_ref, lon_ref, lat_ref,
+            )
 
         @pl.when(step == STEPS - 1)
         def _():
-            lax.fori_loop(0, LEVELS, settle, 0)
+            advect_tiles(ROWS // 8, lambda i: i + 1, field_ref, solved_ref, lon_ref, lat_ref, False)
 
         return 0
 
@@ -438,7 +463,7 @@
 
     block = (LEVELS, TALL, WIDE)
     tile = pltpu.VMEM((TRACERS, LEVELS, 8, WIDE), jnp.float32)
-    arrays = (near(TRACERS, *block), *(near(*block) for _ in range(5)))
+    arrays = (near(TRACERS, *block), near(TRACERS, *block), *(near(*block) for _ in range(5)))
     *state, inj = call(
         prepare,
         (*arrays, near(TRACERS, LEVELS, 8, HALF)),
@@ -458,7 +483,7 @@
         1,
         [tile],
         8,
-        {7 + i: 3 + i for i in range(6)},
+        {7 + i: 3 + i for i in range(7)},
     )[:3]
     received = permute(returned, "lev", [(0, 1), (1, 0)])
     sums = call(

time: 143 us -> 144 us (level)
  Pallas kernels: 31.2 us -> 33.6 us
    pallas_call x6, Pallas kernels: 31.2 us -> 33.6 us  [call(): pl.pallas_call(kernel, out_shape=out_shape, in_specs=specs, out_specs=tup...]
  transfers between devices with their start and end apart: 8 -> 8, of which waited for: 4 -> 3; matrix products, arithmetic and copies ran while one was open for 1% -> 1% of each run, Pallas kernels for 3% -> 4%
where the time goes in v8:
time: 144 us
  starting transfers between devices  61.9 us (43%)
  Pallas kernels  33.6 us (23%)
  blocking collectives  31.8 us (22%)
  waiting for transfers between devices  13.6 us (9%)
  local copies, waits for them, and re-layouts  1.47 us (1%)
    ppermute x8, starting transfers between devices, permute(): return hold(lax.ppermute(x, axes, pairs))  61.9 us
    pallas_call x6, Pallas kernels, call(): pl.pallas_call(kernel, out_shape=out_shape, in_specs=specs, out_specs=tup...  33.6 us
    all_to_all x1, blocking collectives, body(): pieces = lax.all_to_all(sums, ('lon', 'lat', 'lev'), 0, 0, tiled=True)  31.8 us
    ppermute x8, waiting for transfers between devices, permute(): return hold(lax.ppermute(x, axes, pairs))  13.6 us
  transfers between devices with their start and end apart: 8, of which 3 were waited for; matrix products, arithmetic and copies ran while one was open for 1% of the time, Pallas kernels for 4%

profile of v8, /device:TPU:1, one launch (start us, length us, event | category | flops | bytes accessed | tf_op | source)
XLA Modules:
  0.0 143.8 jit_solution(10528904989442918797)
XLA Ops:
  0.7 0.8 copy-done.6
  1.5 2.8 %pack.1 = (f32[7,16,128]{2,1,0:T(8,128)}, f32[7,16,128]{2,1,0:T(8,128)S(1)}, f32[7,16,128]{2,1,0:T(8,128)S(1)}, f32[7,16,128]{2,1,0:T(8,128)S(1)}, f32[61,32,128...) custom-call(s32[1]{0:T(128)} %bitcast.side, f32[4,8]{1,0:T(4,128)S(1)} %copy-done.6, ...), custom_call_target="tpu_custom_call" | custom-call | tf_op jit(solution)/shard_map/pack/pallas_call | solution.py:33
  4.2 11.5 %collective-permute-start.2 = (f32[61,32,128]{2,1,0:T(8,128)S(1)}, f32[61,32,128]{2,1,0:T(8,128)S(1)}, u32[]{:S(2)}, u32[]{:S(2)}) collective-permute-start(f32[61,32,128]{2,1,0:T(8,128)S(1)} %get-tuple-element.23), channel_id=1, source_target_pairs={{0,1},{1,0},{2,3},{3,2},{4,5},{5,4},{6,7},{7,6},{8,9},{9,8},{10,11... | collective-permute-start | bytes 2998280 | tf_op jit(solution)/shard_map/ppermute | solution.py:58
  15.7 3.2 %collective-permute-start = (f32[63,8,128]{2,1,0:T(8,128)S(1)}, f32[63,8,128]{2,1,0:T(8,128)S(1)}, u32[]{:S(2)}, u32[]{:S(2)}) collective-permute-start(f32[63,8,128]{2,1,0:T(8,128)S(1)} %get-tuple-element.21), channel_id=1, source_target_pairs={{0,2},{2,4},{4,6},{6,8},{8,10},{10,12},{12,14},{1,3},{3,5},{5,7},{... | collective-permute-start | bytes 774152 | tf_op jit(solution)/shard_map/ppermute | solution.py:58
  18.9 1.3 collective-permute-start.1
  20.2 4.2 %collective-permute-start.3 = (f32[7,16,128]{2,1,0:T(8,128)S(1)}, f32[7,16,128]{2,1,0:T(8,128)S(1)}, u32[]{:S(2)}, u32[]{:S(2)}) collective-permute-start(f32[7,16,128]{2,1,0:T(8,128)S(1)} %get-tuple-element.24), channel_id=1, source_target_pairs={{0,16},{17,1},{16,32},{33,17},{32,48},{49,33},{48,64},{65,49},{64,... | collective-permute-start | bytes 172040 | tf_op jit(solution)/shard_map/ppermute | solution.py:58
  24.5 5.1 %collective-permute-start.4 = (f32[7,16,128]{2,1,0:T(8,128)S(1)}, f32[7,16,128]{2,1,0:T(8,128)S(1)}, u32[]{:S(2)}, u32[]{:S(2)}) collective-permute-start(f32[7,16,128]{2,1,0:T(8,128)S(1)} %get-tuple-element.25), channel_id=1, source_target_pairs={{1,16},{16,1},{17,32},{32,17},{33,48},{48,33},{49,64},{64,49},{65,... | collective-permute-start | bytes 172040 | tf_op jit(solution)/shard_map/ppermute | solution.py:58
  29.6 8.7 %collective-permute-done.3.lon_same = f32[7,16,128]{2,1,0:T(8,128)S(1)} collective-permute-done((f32[7,16,128]{2,1,0:T(8,128)S(1)}, f32[7,16,128]{2,1,0:T(8,128)S(1)}, u32[]{:S(2)}, u32[]{:S(2)}) %collective-permute-start.3) | collective-permute-done | bytes 57376 | tf_op jit(solution)/shard_map/ppermute | solution.py:58
  38.3 1.5 %collective-permute-done.4.lon_cross = f32[7,16,128]{2,1,0:T(8,128)S(1)} collective-permute-done((f32[7,16,128]{2,1,0:T(8,128)S(1)}, f32[7,16,128]{2,1,0:T(8,128)S(1)}, u32[]{:S(2)}, u32[]{:S(2)}) %collective-permute-start.4) | collective-permute-done | bytes 57376 | tf_op jit(solution)/shard_map/ppermute | solution.py:58
  39.8 0.0 collective-permute-done.own_below
  39.8 0.0 collective-permute-done.1.own_above
  39.8 0.0 collective-permute-done.2.partner
  39.9 3.2 %collective-permute-start.5 = (f32[77,8,128]{2,1,0:T(8,128)S(1)}, f32[77,8,128]{2,1,0:T(8,128)S(1)}, u32[]{:S(2)}, u32[]{:S(2)}) collective-permute-start(f32[77,8,128]{2,1,0:T(8,128)S(1)} %get-tuple-element.26), channel_id=1, source_target_pairs={{0,2},{2,4},{4,6},{6,8},{8,10},{10,12},{12,14},{1,3},{3,5},{5,7},{... | collective-permute-start | bytes 946184 | tf_op jit(solution)/shard_map/ppermute | solution.py:58
  43.1 1.3 collective-permute-start.6
  44.4 3.0 %prepare.1 = (f32[4,16,48,256]{3,2,1,0:T(8,128)S(1)}, f32[4,16,48,256]{3,2,1,0:T(8,128)S(1)}, f32[16,48,256]{2,1,0:T(8,128)S(1)}, f32[16,48,256]{2,1,0:T(8,128)S...) custom-call(s32[1]{0:T(128)} %bitcast.side, ...), custom_call_target="tpu_custom_call" | custom-call | tf_op jit(solution)/shard_map/prepare/pallas_call | solution.py:33
  47.5 0.0 collective-permute-done.5.below
  47.5 3.3 %collective-permute-done.6.above = f32[77,8,128]{2,1,0:T(8,128)S(1)} collective-permute-done((f32[77,8,128]{2,1,0:T(8,128)S(1)}, f32[77,8,128]{2,1,0:T(8,128)S(1)}, u32[]{:S(2)}, u32[]{:S(2)}) %collective-permute-start.6) | collective-permute-done | bytes 315424 | tf_op jit(solution)/shard_map/ppermute | solution.py:58
  50.8 24.4 %steps.1 = (f32[4,8,32,128]{3,2,1,0:T(8,128)S(1)}, f32[4,8,32,128]{3,2,1,0:T(8,128)S(1)}, f32[24,32,128]{2,1,0:T(8,128)S(1)}, f32[4,16,48,256]{3,2,1,0:T(8,128)S...) custom-call(s32[1]{0:T(128)} %bitcast.side, ...), custom_call_target="tpu_custom_call", output_to_operand_aliasing={{3}: (7, {}), {4}: (8, {}), {5}: (9, {}), {6}: (10, {}), {7... | custom-call | tf_op jit(solution)/shard_map/steps/pallas_call | solution.py:33
  75.2 32.1 %collective-permute-start.7 = (f32[4,8,32,128]{3,2,1,0:T(8,128)S(1)}, f32[4,8,32,128]{3,2,1,0:T(8,128)S(1)}, u32[]{:S(2)}, u32[]{:S(2)}) collective-permute-start(f32[4,8,32,128]{3,2,1,0:T(8,128)S(1)} %get-tuple-element.38), channel_id=1, source_target_pairs={{0,1},{1,0},{2,3},{3,2},{4,5},{5,4},{6,7},{7,6},{8,9},{9,8},{10,11... | collective-permute-start | bytes 1572872 | tf_op jit(solution)/shard_map/ppermute | solution.py:58
  107.3 2.4 %regions.1 = f32[512,128]{1,0:T(8,128)S(1)} custom-call(s32[1]{0:T(128)} %bitcast.side, f32[24,32,128]{2,1,0:T(8,128)S(1)} %get-tuple-element.39.weights, s32[32,256]{1,0:T(8,128)S(1)} %copy-done.5), custom_call_target="tpu_custom_call" | custom-call | tf_op jit(solution)/shard_map/regions/pallas_call | solution.py:33
  109.7 31.8 %all_to_all.9 = f32[512,1,128]{2,1,0:T(1,128)S(1)} all-to-all(f32[512,1,128]{2,1,0:T(1,128)S(1)} %bitcast.5), channel_id=1, replica_groups=mesh['lon'=32,'lat'=8,'lev'=2] {'lon','lat','lev'}, dimensions={0} | all-to-all | bytes 524288 | tf_op jit(solution)/shard_map/all_to_all | solution.py:497
  141.5 0.6 reduce_sum.9
  142.0 0.7 reshape.13
  142.7 1.0 join.1
  (15 shorter events, 0.1 us)
Async XLA Ops:
  0.6 43.8 %copy-start.3 = (bf16[8,32,256]{2,1,0:T(8,128)(2,1)S(1)}, bf16[8,32,256]{2,1,0:T(8,128)(2,1)}, u32[]{:S(2)}) copy-start(bf16[8,32,256]{2,1,0:T(8,128)(2,1)} %mixing.3) | copy-start | bytes 393220
  0.6 43.8 %copy-start.2 = (bf16[8,32,256]{2,1,0:T(8,128)(2,1)S(1)}, bf16[8,32,256]{2,1,0:T(8,128)(2,1)}, u32[]{:S(2)}) copy-start(bf16[8,32,256]{2,1,0:T(8,128)(2,1)} %lat_wind.3) | copy-start | bytes 393220
  0.7 43.8 %copy-start.1 = (bf16[8,32,256]{2,1,0:T(8,128)(2,1)S(1)}, bf16[8,32,256]{2,1,0:T(8,128)(2,1)}, u32[]{:S(2)}) copy-start(bf16[8,32,256]{2,1,0:T(8,128)(2,1)} %lon_wind.3) | copy-start | bytes 393220
  0.7 43.8 %copy-start = (f32[4,8,32,256]{3,2,1,0:T(8,128)S(1)}, f32[4,8,32,256]{3,2,1,0:T(8,128)}, u32[]{:S(2)}) copy-start(f32[4,8,32,256]{3,2,1,0:T(8,128)} %adjoint.3) | copy-start | bytes 3145732
  0.7 50.1 %copy-start.4 = (bf16[4,32,256]{2,1,0:T(8,128)(2,1)S(1)}, bf16[4,32,256]{2,1,0:T(8,128)(2,1)}, u32[]{:S(2)}) copy-start(bf16[4,32,256]{2,1,0:T(8,128)(2,1)} %prior.1) | copy-start | bytes 196612
  0.7 0.8 copy-start.6
  4.2 35.6 %collective-permute-start.2 = (f32[61,32,128]{2,1,0:T(8,128)S(1)}, f32[61,32,128]{2,1,0:T(8,128)S(1)}, u32[]{:S(2)}, u32[]{:S(2)}) collective-permute-start(f32[61,32,128]{2,1,0:T(8,128)S(1)} %get-tuple-element.23), channel_id=1, source_target_pairs={{0,1},{1,0},{2,3},{3,2},{4,5},{5,4},{6,7},{7,6},{8,9},{9,8},{10,11... | collective-permute-start | bytes 2998280 | tf_op jit(solution)/shard_map/ppermute | solution.py:58
  15.7 24.1 %collective-permute-start = (f32[63,8,128]{2,1,0:T(8,128)S(1)}, f32[63,8,128]{2,1,0:T(8,128)S(1)}, u32[]{:S(2)}, u32[]{:S(2)}) collective-permute-start(f32[63,8,128]{2,1,0:T(8,128)S(1)} %get-tuple-element.21), channel_id=1, source_target_pairs={{0,2},{2,4},{4,6},{6,8},{8,10},{10,12},{12,14},{1,3},{3,5},{5,7},{... | collective-permute-start | bytes 774152 | tf_op jit(solution)/shard_map/ppermute | solution.py:58
  18.9 20.9 %collective-permute-start.1 = (f32[63,8,128]{2,1,0:T(8,128)S(1)}, f32[63,8,128]{2,1,0:T(8,128)S(1)}, u32[]{:S(2)}, u32[]{:S(2)}) collective-permute-start(f32[63,8,128]{2,1,0:T(8,128)S(1)} %get-tuple-element.22), channel_id=1, source_target_pairs={{2,0},{4,2},{6,4},{8,6},{10,8},{12,10},{14,12},{3,1},{5,3},{7,5},{... | collective-permute-start | bytes 774152 | tf_op jit(solution)/shard_map/ppermute | solution.py:58
  20.2 18.0 %collective-permute-start.3 = (f32[7,16,128]{2,1,0:T(8,128)S(1)}, f32[7,16,128]{2,1,0:T(8,128)S(1)}, u32[]{:S(2)}, u32[]{:S(2)}) collective-permute-start(f32[7,16,128]{2,1,0:T(8,128)S(1)} %get-tuple-element.24), channel_id=1, source_target_pairs={{0,16},{17,1},{16,32},{33,17},{32,48},{49,33},{48,64},{65,49},{64,... | collective-permute-start | bytes 172040 | tf_op jit(solution)/shard_map/ppermute | solution.py:58
  24.5 15.4 %collective-permute-start.4 = (f32[7,16,128]{2,1,0:T(8,128)S(1)}, f32[7,16,128]{2,1,0:T(8,128)S(1)}, u32[]{:S(2)}, u32[]{:S(2)}) collective-permute-start(f32[7,16,128]{2,1,0:T(8,128)S(1)} %get-tuple-element.25), channel_id=1, source_target_pairs={{1,16},{16,1},{17,32},{32,17},{33,48},{48,33},{49,64},{64,49},{65,... | collective-permute-start | bytes 172040 | tf_op jit(solution)/shard_map/ppermute | solution.py:58
  39.9 7.6 %collective-permute-start.5 = (f32[77,8,128]{2,1,0:T(8,128)S(1)}, f32[77,8,128]{2,1,0:T(8,128)S(1)}, u32[]{:S(2)}, u32[]{:S(2)}) collective-permute-start(f32[77,8,128]{2,1,0:T(8,128)S(1)} %get-tuple-element.26), channel_id=1, source_target_pairs={{0,2},{2,4},{4,6},{6,8},{8,10},{10,12},{12,14},{1,3},{3,5},{5,7},{... | collective-permute-start | bytes 946184 | tf_op jit(solution)/shard_map/ppermute | solution.py:58
  43.1 7.7 %collective-permute-start.6 = (f32[77,8,128]{2,1,0:T(8,128)S(1)}, f32[77,8,128]{2,1,0:T(8,128)S(1)}, u32[]{:S(2)}, u32[]{:S(2)}) collective-permute-start(f32[77,8,128]{2,1,0:T(8,128)S(1)} %get-tuple-element.27), channel_id=1, source_target_pairs={{2,0},{4,2},{6,4},{8,6},{10,8},{12,10},{14,12},{3,1},{5,3},{7,5},{... | collective-permute-start | bytes 946184 | tf_op jit(solution)/shard_map/ppermute | solution.py:58
  50.8 56.5 %copy-start.5 = (s32[32,256]{1,0:T(8,128)S(1)}, s32[32,256]{1,0:T(8,128)}, u32[]{:S(2)}) copy-start(s32[32,256]{1,0:T(8,128)} %ids.1) | copy-start | bytes 98308
  75.2 67.5 %collective-permute-start.7 = (f32[4,8,32,128]{3,2,1,0:T(8,128)S(1)}, f32[4,8,32,128]{3,2,1,0:T(8,128)S(1)}, u32[]{:S(2)}, u32[]{:S(2)}) collective-permute-start(f32[4,8,32,128]{3,2,1,0:T(8,128)S(1)} %get-tuple-element.38), channel_id=1, source_target_pairs={{0,1},{1,0},{2,3},{3,2},{4,5},{5,4},{6,7},{7,6},{8,9},{9,8},{10,11... | collective-permute-start | bytes 1572872 | tf_op jit(solution)/shard_map/ppermute | solution.py:58

commit v9 on v8

--- a/solution.py
+++ b/solution.py
@@ -198,55 +198,49 @@
 
 
 TILES = TALL // 8
-UNROLL = 4
 
 
 def rows_of(tile):
-    return pl.ds(pl.multiple_of(tile * 8, 8), 8)
-
-
-def advect_tile(level, tile, field_ref, solved_ref, lon_ref, lat_ref, wings):
-    at = rows_of(tile)
-    before = rows_of(jnp.where(tile == 0, TILES - 1, tile - 1))
-    after = rows_of(jnp.where(tile == TILES - 1, 0, tile + 1))
+    return slice(tile % TILES * 8, tile % TILES * 8 + 8)
+
+
+def advect_tiles(tiles, field_ref, solved_ref, lon_ref, lat_ref, wings=True):
     sides = (MAIN_LANES, WING_LANES)
     count = 2 if wings else 1
     row = lax.broadcasted_iota(jnp.int32, (8, HALF), 0)
     lane = lax.broadcasted_iota(jnp.int32, (8, HALF), 1)
-    rates = []
-    for side in sides[:count]:
-        lon = lon_ref[level, at, side]
-        lat = lat_ref[level, at, side]
-        rates.append((lon > 0.0, lat > 0.0, jnp.abs(lon), jnp.abs(lat)))
-    for tracer in range(TRACERS):
-        cells = [solved_ref[tracer, level, at, side] for side in sides]
-        for i, side in enumerate(sides[:count]):
-            east, north, lon, lat = rates[i]
-            here = cells[i]
-            beside = cells[1 - i]
-            along = jnp.where(
-                east,
-                pltpu.roll(jnp.where(lane == 0, beside, here), HALF - 1, 1),
-                pltpu.roll(jnp.where(lane == HALF - 1, beside, here), 1, 1),
-            )
-            across = jnp.where(
-                north,
-                pltpu.roll(jnp.where(row == 0, solved_ref[tracer, level, after, side], here), 7, 0),
-                pltpu.roll(jnp.where(row == 7, solved_ref[tracer, level, before, side], here), 1, 0),
-            )
-            field_ref[tracer, level, at, side] = here + lon * (along - here) + lat * (across - here)
-
-
-def advect_tiles(count, tile_of, field_ref, solved_ref, lon_ref, lat_ref, wings=True):
-    blocks = LEVELS // UNROLL
-
-    def some(i, _):
-        tile = tile_of(i // blocks)
-        for level in range(UNROLL):
-            advect_tile(i % blocks * UNROLL + level, tile, field_ref, solved_ref, lon_ref, lat_ref, wings)
+
+    def one_level(level, _):
+        for tile in tiles:
+            at = rows_of(tile)
+            rates = []
+            for side in sides[:count]:
+                lon = lon_ref[level, at, side]
+                lat = lat_ref[level, at, side]
+                rates.append((lon > 0.0, lat > 0.0, jnp.abs(lon), jnp.abs(lat)))
+            for tracer in range(TRACERS):
+                cells = [solved_ref[tracer, level, at, side] for side in sides]
+                ahead = [pltpu.roll(c, HALF - 1, 1) for c in cells]
+                behind = [pltpu.roll(c, 1, 1) for c in cells]
+                for i, side in enumerate(sides[:count]):
+                    east, north, lon, lat = rates[i]
+                    here = cells[i]
+                    along = jnp.where(
+                        east,
+                        jnp.where(lane == HALF - 1, ahead[1 - i], ahead[i]),
+                        jnp.where(lane == 0, behind[1 - i], behind[i]),
+                    )
+                    after = solved_ref[tracer, level, rows_of(tile + 1), side]
+                    before = solved_ref[tracer, level, rows_of(tile - 1), side]
+                    across = jnp.where(
+                        north,
+                        jnp.where(row == 7, pltpu.roll(after, 7, 0), pltpu.roll(here, 7, 0)),
+                        jnp.where(row == 0, pltpu.roll(before, 1, 0), pltpu.roll(here, 1, 0)),
+                    )
+                    field_ref[tracer, level, at, side] = here + lon * (along - here) + lat * (across - here)
         return 0
 
-    lax.fori_loop(0, count * blocks, some, 0)
+    lax.fori_loop(0, LEVELS, one_level, 0)
 
 
 def prepare(
@@ -292,7 +286,7 @@
         return 0
 
     lax.fori_loop(1, 1 + ROWS // 8, inner, 0)
-    advect_tiles(2, lambda i: i + 2, field_ref, solved_ref, lon_ref, lat_ref)
+    advect_tiles((2, 3), field_ref, solved_ref, lon_ref, lat_ref)
 
 
 def steps(
@@ -356,17 +350,19 @@
 
         lax.fori_loop(0, ROWS // 8, weigh, 0)
 
-        @pl.when(step < STEPS - 1)
+        buffers = (field_ref, solved_ref, lon_ref, lat_ref)
+
+        @pl.when(step == 0)
         def _():
-            advect_tiles(
-                jnp.where(step == 0, TILES - 2, TILES),
-                lambda i: jnp.where((step == 0) & (i >= 2), i + 2, i),
-                field_ref, solved_ref, lon_ref, lat_ref,
-            )
+            advect_tiles((0, 1, 4, 5), *buffers)
+
+        @pl.when((step > 0) & (step < STEPS - 1))
+        def _():
+            advect_tiles(range(TILES), *buffers)
 
         @pl.when(step == STEPS - 1)
         def _():
-            advect_tiles(ROWS // 8, lambda i: i + 1, field_ref, solved_ref, lon_ref, lat_ref, False)
+            advect_tiles(range(1, 1 + ROWS // 8), *buffers, wings=False)
 
         return 0
 

time: 144 us -> 142 us (0.986)
  Pallas kernels: 33.6 us -> 32.1 us
    pallas_call x6, Pallas kernels: 33.6 us -> 32.1 us  [call(): pl.pallas_call(kernel, out_shape=out_shape, in_specs=specs, out_specs=tup...]
where the time goes in v9:
time: 142 us
  starting transfers between devices  61.9 us (44%)
  Pallas kernels  32.1 us (23%)
  blocking collectives  31.8 us (22%)
  waiting for transfers between devices  13 us (9%)
  local copies, waits for them, and re-layouts  1.47 us (1%)
    ppermute x8, starting transfers between devices, permute(): return hold(lax.ppermute(x, axes, pairs))  61.9 us
    pallas_call x6, Pallas kernels, call(): pl.pallas_call(kernel, out_shape=out_shape, in_specs=specs, out_specs=tup...  32.1 us
    all_to_all x1, blocking collectives, body(): pieces = lax.all_to_all(sums, ('lon', 'lat', 'lev'), 0, 0, tiled=True)  31.8 us
    ppermute x8, waiting for transfers between devices, permute(): return hold(lax.ppermute(x, axes, pairs))  13 us
  transfers between devices with their start and end apart: 8, of which 3 were waited for; matrix products, arithmetic and copies ran while one was open for 1% of the time, Pallas kernels for 4%

profile of v9, /device:TPU:1, one launch (start us, length us, event | category | flops | bytes accessed | tf_op | source)
XLA Modules:
  0.0 141.6 jit_solution(17156633861052863859)
XLA Ops:
  0.7 0.8 copy-done.6
  1.5 2.8 %pack.1 = (f32[7,16,128]{2,1,0:T(8,128)}, f32[7,16,128]{2,1,0:T(8,128)S(1)}, f32[7,16,128]{2,1,0:T(8,128)S(1)}, f32[7,16,128]{2,1,0:T(8,128)S(1)}, f32[61,32,128...) custom-call(s32[1]{0:T(128)} %bitcast.side, f32[4,8]{1,0:T(4,128)S(1)} %copy-done.6, ...), custom_call_target="tpu_custom_call" | custom-call | tf_op jit(solution)/shard_map/pack/pallas_call | solution.py:33
  4.2 11.5 %collective-permute-start.2 = (f32[61,32,128]{2,1,0:T(8,128)S(1)}, f32[61,32,128]{2,1,0:T(8,128)S(1)}, u32[]{:S(2)}, u32[]{:S(2)}) collective-permute-start(f32[61,32,128]{2,1,0:T(8,128)S(1)} %get-tuple-element.23), channel_id=1, source_target_pairs={{0,1},{1,0},{2,3},{3,2},{4,5},{5,4},{6,7},{7,6},{8,9},{9,8},{10,11... | collective-permute-start | bytes 2998280 | tf_op jit(solution)/shard_map/ppermute | solution.py:58
  15.7 3.2 %collective-permute-start = (f32[63,8,128]{2,1,0:T(8,128)S(1)}, f32[63,8,128]{2,1,0:T(8,128)S(1)}, u32[]{:S(2)}, u32[]{:S(2)}) collective-permute-start(f32[63,8,128]{2,1,0:T(8,128)S(1)} %get-tuple-element.21), channel_id=1, source_target_pairs={{0,2},{2,4},{4,6},{6,8},{8,10},{10,12},{12,14},{1,3},{3,5},{5,7},{... | collective-permute-start | bytes 774152 | tf_op jit(solution)/shard_map/ppermute | solution.py:58
  18.9 1.3 collective-permute-start.1
  20.2 4.2 %collective-permute-start.3 = (f32[7,16,128]{2,1,0:T(8,128)S(1)}, f32[7,16,128]{2,1,0:T(8,128)S(1)}, u32[]{:S(2)}, u32[]{:S(2)}) collective-permute-start(f32[7,16,128]{2,1,0:T(8,128)S(1)} %get-tuple-element.24), channel_id=1, source_target_pairs={{0,16},{17,1},{16,32},{33,17},{32,48},{49,33},{48,64},{65,49},{64,... | collective-permute-start | bytes 172040 | tf_op jit(solution)/shard_map/ppermute | solution.py:58
  24.5 5.1 %collective-permute-start.4 = (f32[7,16,128]{2,1,0:T(8,128)S(1)}, f32[7,16,128]{2,1,0:T(8,128)S(1)}, u32[]{:S(2)}, u32[]{:S(2)}) collective-permute-start(f32[7,16,128]{2,1,0:T(8,128)S(1)} %get-tuple-element.25), channel_id=1, source_target_pairs={{1,16},{16,1},{17,32},{32,17},{33,48},{48,33},{49,64},{64,49},{65,... | collective-permute-start | bytes 172040 | tf_op jit(solution)/shard_map/ppermute | solution.py:58
  29.6 8.7 %collective-permute-done.3.lon_same = f32[7,16,128]{2,1,0:T(8,128)S(1)} collective-permute-done((f32[7,16,128]{2,1,0:T(8,128)S(1)}, f32[7,16,128]{2,1,0:T(8,128)S(1)}, u32[]{:S(2)}, u32[]{:S(2)}) %collective-permute-start.3) | collective-permute-done | bytes 57376 | tf_op jit(solution)/shard_map/ppermute | solution.py:58
  38.3 1.5 %collective-permute-done.4.lon_cross = f32[7,16,128]{2,1,0:T(8,128)S(1)} collective-permute-done((f32[7,16,128]{2,1,0:T(8,128)S(1)}, f32[7,16,128]{2,1,0:T(8,128)S(1)}, u32[]{:S(2)}, u32[]{:S(2)}) %collective-permute-start.4) | collective-permute-done | bytes 57376 | tf_op jit(solution)/shard_map/ppermute | solution.py:58
  39.8 0.0 collective-permute-done.own_below
  39.8 0.0 collective-permute-done.1.own_above
  39.8 0.0 collective-permute-done.2.partner
  39.9 3.2 %collective-permute-start.5 = (f32[77,8,128]{2,1,0:T(8,128)S(1)}, f32[77,8,128]{2,1,0:T(8,128)S(1)}, u32[]{:S(2)}, u32[]{:S(2)}) collective-permute-start(f32[77,8,128]{2,1,0:T(8,128)S(1)} %get-tuple-element.26), channel_id=1, source_target_pairs={{0,2},{2,4},{4,6},{6,8},{8,10},{10,12},{12,14},{1,3},{3,5},{5,7},{... | collective-permute-start | bytes 946184 | tf_op jit(solution)/shard_map/ppermute | solution.py:58
  43.1 1.3 collective-permute-start.6
  44.4 3.6 %prepare.1 = (f32[4,16,48,256]{3,2,1,0:T(8,128)S(1)}, f32[4,16,48,256]{3,2,1,0:T(8,128)S(1)}, f32[16,48,256]{2,1,0:T(8,128)S(1)}, f32[16,48,256]{2,1,0:T(8,128)S...) custom-call(s32[1]{0:T(128)} %bitcast.side, ...), custom_call_target="tpu_custom_call" | custom-call | tf_op jit(solution)/shard_map/prepare/pallas_call | solution.py:33
  48.0 0.0 collective-permute-done.5.below
  48.1 2.7 %collective-permute-done.6.above = f32[77,8,128]{2,1,0:T(8,128)S(1)} collective-permute-done((f32[77,8,128]{2,1,0:T(8,128)S(1)}, f32[77,8,128]{2,1,0:T(8,128)S(1)}, u32[]{:S(2)}, u32[]{:S(2)}) %collective-permute-start.6) | collective-permute-done | bytes 315424 | tf_op jit(solution)/shard_map/ppermute | solution.py:58
  50.8 22.2 %steps.1 = (f32[4,8,32,128]{3,2,1,0:T(8,128)S(1)}, f32[4,8,32,128]{3,2,1,0:T(8,128)S(1)}, f32[24,32,128]{2,1,0:T(8,128)S(1)}, f32[4,16,48,256]{3,2,1,0:T(8,128)S...) custom-call(s32[1]{0:T(128)} %bitcast.side, ...), custom_call_target="tpu_custom_call", output_to_operand_aliasing={{3}: (7, {}), {4}: (8, {}), {5}: (9, {}), {6}: (10, {}), {7... | custom-call | tf_op jit(solution)/shard_map/steps/pallas_call | solution.py:33
  73.0 32.1 %collective-permute-start.7 = (f32[4,8,32,128]{3,2,1,0:T(8,128)S(1)}, f32[4,8,32,128]{3,2,1,0:T(8,128)S(1)}, u32[]{:S(2)}, u32[]{:S(2)}) collective-permute-start(f32[4,8,32,128]{3,2,1,0:T(8,128)S(1)} %get-tuple-element.38), channel_id=1, source_target_pairs={{0,1},{1,0},{2,3},{3,2},{4,5},{5,4},{6,7},{7,6},{8,9},{9,8},{10,11... | collective-permute-start | bytes 1572872 | tf_op jit(solution)/shard_map/ppermute | solution.py:58
  105.2 2.4 %regions.1 = f32[512,128]{1,0:T(8,128)S(1)} custom-call(s32[1]{0:T(128)} %bitcast.side, f32[24,32,128]{2,1,0:T(8,128)S(1)} %get-tuple-element.39.weights, s32[32,256]{1,0:T(8,128)S(1)} %copy-done.5), custom_call_target="tpu_custom_call" | custom-call | tf_op jit(solution)/shard_map/regions/pallas_call | solution.py:33
  107.6 31.8 %all_to_all.9 = f32[512,1,128]{2,1,0:T(1,128)S(1)} all-to-all(f32[512,1,128]{2,1,0:T(1,128)S(1)} %bitcast.5), channel_id=1, replica_groups=mesh['lon'=32,'lat'=8,'lev'=2] {'lon','lat','lev'}, dimensions={0} | all-to-all | bytes 524288 | tf_op jit(solution)/shard_map/all_to_all | solution.py:493
  139.4 0.6 reduce_sum.9
  139.9 0.7 reshape.13
  140.6 1.0 join.1
  (15 shorter events, 0.1 us)
Async XLA Ops:
  0.6 43.8 %copy-start.3 = (bf16[8,32,256]{2,1,0:T(8,128)(2,1)S(1)}, bf16[8,32,256]{2,1,0:T(8,128)(2,1)}, u32[]{:S(2)}) copy-start(bf16[8,32,256]{2,1,0:T(8,128)(2,1)} %mixing.3) | copy-start | bytes 393220
  0.6 43.8 %copy-start.2 = (bf16[8,32,256]{2,1,0:T(8,128)(2,1)S(1)}, bf16[8,32,256]{2,1,0:T(8,128)(2,1)}, u32[]{:S(2)}) copy-start(bf16[8,32,256]{2,1,0:T(8,128)(2,1)} %lat_wind.3) | copy-start | bytes 393220
  0.7 43.8 %copy-start.1 = (bf16[8,32,256]{2,1,0:T(8,128)(2,1)S(1)}, bf16[8,32,256]{2,1,0:T(8,128)(2,1)}, u32[]{:S(2)}) copy-start(bf16[8,32,256]{2,1,0:T(8,128)(2,1)} %lon_wind.3) | copy-start | bytes 393220
  0.7 43.8 %copy-start = (f32[4,8,32,256]{3,2,1,0:T(8,128)S(1)}, f32[4,8,32,256]{3,2,1,0:T(8,128)}, u32[]{:S(2)}) copy-start(f32[4,8,32,256]{3,2,1,0:T(8,128)} %adjoint.3) | copy-start | bytes 3145732
  0.7 50.1 %copy-start.4 = (bf16[4,32,256]{2,1,0:T(8,128)(2,1)S(1)}, bf16[4,32,256]{2,1,0:T(8,128)(2,1)}, u32[]{:S(2)}) copy-start(bf16[4,32,256]{2,1,0:T(8,128)(2,1)} %prior.1) | copy-start | bytes 196612
  0.7 0.8 copy-start.6
  4.2 35.6 %collective-permute-start.2 = (f32[61,32,128]{2,1,0:T(8,128)S(1)}, f32[61,32,128]{2,1,0:T(8,128)S(1)}, u32[]{:S(2)}, u32[]{:S(2)}) collective-permute-start(f32[61,32,128]{2,1,0:T(8,128)S(1)} %get-tuple-element.23), channel_id=1, source_target_pairs={{0,1},{1,0},{2,3},{3,2},{4,5},{5,4},{6,7},{7,6},{8,9},{9,8},{10,11... | collective-permute-start | bytes 2998280 | tf_op jit(solution)/shard_map/ppermute | solution.py:58
  15.7 24.1 %collective-permute-start = (f32[63,8,128]{2,1,0:T(8,128)S(1)}, f32[63,8,128]{2,1,0:T(8,128)S(1)}, u32[]{:S(2)}, u32[]{:S(2)}) collective-permute-start(f32[63,8,128]{2,1,0:T(8,128)S(1)} %get-tuple-element.21), channel_id=1, source_target_pairs={{0,2},{2,4},{4,6},{6,8},{8,10},{10,12},{12,14},{1,3},{3,5},{5,7},{... | collective-permute-start | bytes 774152 | tf_op jit(solution)/shard_map/ppermute | solution.py:58
  18.9 20.9 %collective-permute-start.1 = (f32[63,8,128]{2,1,0:T(8,128)S(1)}, f32[63,8,128]{2,1,0:T(8,128)S(1)}, u32[]{:S(2)}, u32[]{:S(2)}) collective-permute-start(f32[63,8,128]{2,1,0:T(8,128)S(1)} %get-tuple-element.22), channel_id=1, source_target_pairs={{2,0},{4,2},{6,4},{8,6},{10,8},{12,10},{14,12},{3,1},{5,3},{7,5},{... | collective-permute-start | bytes 774152 | tf_op jit(solution)/shard_map/ppermute | solution.py:58
  20.2 18.0 %collective-permute-start.3 = (f32[7,16,128]{2,1,0:T(8,128)S(1)}, f32[7,16,128]{2,1,0:T(8,128)S(1)}, u32[]{:S(2)}, u32[]{:S(2)}) collective-permute-start(f32[7,16,128]{2,1,0:T(8,128)S(1)} %get-tuple-element.24), channel_id=1, source_target_pairs={{0,16},{17,1},{16,32},{33,17},{32,48},{49,33},{48,64},{65,49},{64,... | collective-permute-start | bytes 172040 | tf_op jit(solution)/shard_map/ppermute | solution.py:58
  24.5 15.4 %collective-permute-start.4 = (f32[7,16,128]{2,1,0:T(8,128)S(1)}, f32[7,16,128]{2,1,0:T(8,128)S(1)}, u32[]{:S(2)}, u32[]{:S(2)}) collective-permute-start(f32[7,16,128]{2,1,0:T(8,128)S(1)} %get-tuple-element.25), channel_id=1, source_target_pairs={{1,16},{16,1},{17,32},{32,17},{33,48},{48,33},{49,64},{64,49},{65,... | collective-permute-start | bytes 172040 | tf_op jit(solution)/shard_map/ppermute | solution.py:58
  39.9 8.2 %collective-permute-start.5 = (f32[77,8,128]{2,1,0:T(8,128)S(1)}, f32[77,8,128]{2,1,0:T(8,128)S(1)}, u32[]{:S(2)}, u32[]{:S(2)}) collective-permute-start(f32[77,8,128]{2,1,0:T(8,128)S(1)} %get-tuple-element.26), channel_id=1, source_target_pairs={{0,2},{2,4},{4,6},{6,8},{8,10},{10,12},{12,14},{1,3},{3,5},{5,7},{... | collective-permute-start | bytes 946184 | tf_op jit(solution)/shard_map/ppermute | solution.py:58
  43.1 7.7 %collective-permute-start.6 = (f32[77,8,128]{2,1,0:T(8,128)S(1)}, f32[77,8,128]{2,1,0:T(8,128)S(1)}, u32[]{:S(2)}, u32[]{:S(2)}) collective-permute-start(f32[77,8,128]{2,1,0:T(8,128)S(1)} %get-tuple-element.27), channel_id=1, source_target_pairs={{2,0},{4,2},{6,4},{8,6},{10,8},{12,10},{14,12},{3,1},{5,3},{7,5},{... | collective-permute-start | bytes 946184 | tf_op jit(solution)/shard_map/ppermute | solution.py:58
  50.8 54.4 %copy-start.5 = (s32[32,256]{1,0:T(8,128)S(1)}, s32[32,256]{1,0:T(8,128)}, u32[]{:S(2)}) copy-start(s32[32,256]{1,0:T(8,128)} %ids.1) | copy-start | bytes 98308
  73.0 67.6 %collective-permute-start.7 = (f32[4,8,32,128]{3,2,1,0:T(8,128)S(1)}, f32[4,8,32,128]{3,2,1,0:T(8,128)S(1)}, u32[]{:S(2)}, u32[]{:S(2)}) collective-permute-start(f32[4,8,32,128]{3,2,1,0:T(8,128)S(1)} %get-tuple-element.38), channel_id=1, source_target_pairs={{0,1},{1,0},{2,3},{3,2},{4,5},{5,4},{6,7},{7,6},{8,9},{9,8},{10,11... | collective-permute-start | bytes 1572872 | tf_op jit(solution)/shard_map/ppermute | solution.py:58

commit v10 on v9

--- a/solution.py
+++ b/solution.py
@@ -418,6 +418,7 @@
         pltpu.with_memory_space_constraint(x, pltpu.HBM) for x in (adjoint, courant_lon, courant_lat, mixing)
     )
     own = tuple(hold(x) for x in (adjoint, courant_lon, courant_lat, mixing))
+    far_injection = pltpu.with_memory_space_constraint(injection, pltpu.HBM)
     injection = hold(injection)
 
     strip = MAIN + FIELDS
@@ -429,7 +430,7 @@
             near(strip, EDGE, HALF),
             near(strip, EDGE, HALF),
         ),
-        (side, injection, *raw),
+        (side, far_injection, *raw),
         1,
     )
     same = []

time: 142 us -> 141 us (level)
  no operation moved by 1% of the time
where the time goes in v10:
time: 141 us
  starting transfers between devices  61.9 us (44%)
  Pallas kernels  32.2 us (23%)
  blocking collectives  31.8 us (23%)
  waiting for transfers between devices  12.3 us (9%)
    ppermute x8, starting transfers between devices, permute(): return hold(lax.ppermute(x, axes, pairs))  61.9 us
    pallas_call x6, Pallas kernels, call(): pl.pallas_call(kernel, out_shape=out_shape, in_specs=specs, out_specs=tup...  32.2 us
    all_to_all x1, blocking collectives, body(): pieces = lax.all_to_all(sums, ('lon', 'lat', 'lev'), 0, 0, tiled=True)  31.8 us
    ppermute x8, waiting for transfers between devices, permute(): return hold(lax.ppermute(x, axes, pairs))  12.3 us
  transfers between devices with their start and end apart: 8, of which 3 were waited for; matrix products, arithmetic and copies ran while one was open for 1% of the time, Pallas kernels for 4%

profile of v10, /device:TPU:1, one launch (start us, length us, event | category | flops | bytes accessed | tf_op | source)
XLA Modules:
  0.0 140.9 jit_solution(623765977532480852)
XLA Ops:
  0.7 2.9 %pack.1 = (f32[7,16,128]{2,1,0:T(8,128)}, f32[7,16,128]{2,1,0:T(8,128)S(1)}, f32[7,16,128]{2,1,0:T(8,128)S(1)}, f32[7,16,128]{2,1,0:T(8,128)S(1)}, f32[61,32,128...) custom-call(s32[1]{0:T(128)} %bitcast.side, f32[4,8]{1,0:T(4,128)} %injection.3, ...), custom_call_target="tpu_custom_call" | custom-call | tf_op jit(solution)/shard_map/pack/pallas_call | solution.py:33
  3.5 11.5 %collective-permute-start.2 = (f32[61,32,128]{2,1,0:T(8,128)S(1)}, f32[61,32,128]{2,1,0:T(8,128)S(1)}, u32[]{:S(2)}, u32[]{:S(2)}) collective-permute-start(f32[61,32,128]{2,1,0:T(8,128)S(1)} %get-tuple-element.23), channel_id=1, source_target_pairs={{0,1},{1,0},{2,3},{3,2},{4,5},{5,4},{6,7},{7,6},{8,9},{9,8},{10,11... | collective-permute-start | bytes 2998280 | tf_op jit(solution)/shard_map/ppermute | solution.py:58
  15.0 3.2 %collective-permute-start = (f32[63,8,128]{2,1,0:T(8,128)S(1)}, f32[63,8,128]{2,1,0:T(8,128)S(1)}, u32[]{:S(2)}, u32[]{:S(2)}) collective-permute-start(f32[63,8,128]{2,1,0:T(8,128)S(1)} %get-tuple-element.21), channel_id=1, source_target_pairs={{0,2},{2,4},{4,6},{6,8},{8,10},{10,12},{12,14},{1,3},{3,5},{5,7},{... | collective-permute-start | bytes 774152 | tf_op jit(solution)/shard_map/ppermute | solution.py:58
  18.2 1.3 collective-permute-start.1
  19.5 4.2 %collective-permute-start.3 = (f32[7,16,128]{2,1,0:T(8,128)S(1)}, f32[7,16,128]{2,1,0:T(8,128)S(1)}, u32[]{:S(2)}, u32[]{:S(2)}) collective-permute-start(f32[7,16,128]{2,1,0:T(8,128)S(1)} %get-tuple-element.24), channel_id=1, source_target_pairs={{0,16},{17,1},{16,32},{33,17},{32,48},{49,33},{48,64},{65,49},{64,... | collective-permute-start | bytes 172040 | tf_op jit(solution)/shard_map/ppermute | solution.py:58
  23.8 5.1 %collective-permute-start.4 = (f32[7,16,128]{2,1,0:T(8,128)S(1)}, f32[7,16,128]{2,1,0:T(8,128)S(1)}, u32[]{:S(2)}, u32[]{:S(2)}) collective-permute-start(f32[7,16,128]{2,1,0:T(8,128)S(1)} %get-tuple-element.25), channel_id=1, source_target_pairs={{1,16},{16,1},{17,32},{32,17},{33,48},{48,33},{49,64},{64,49},{65,... | collective-permute-start | bytes 172040 | tf_op jit(solution)/shard_map/ppermute | solution.py:58
  28.9 8.7 %collective-permute-done.3.lon_same = f32[7,16,128]{2,1,0:T(8,128)S(1)} collective-permute-done((f32[7,16,128]{2,1,0:T(8,128)S(1)}, f32[7,16,128]{2,1,0:T(8,128)S(1)}, u32[]{:S(2)}, u32[]{:S(2)}) %collective-permute-start.3) | collective-permute-done | bytes 57376 | tf_op jit(solution)/shard_map/ppermute | solution.py:58
  37.6 1.5 %collective-permute-done.4.lon_cross = f32[7,16,128]{2,1,0:T(8,128)S(1)} collective-permute-done((f32[7,16,128]{2,1,0:T(8,128)S(1)}, f32[7,16,128]{2,1,0:T(8,128)S(1)}, u32[]{:S(2)}, u32[]{:S(2)}) %collective-permute-start.4) | collective-permute-done | bytes 57376 | tf_op jit(solution)/shard_map/ppermute | solution.py:58
  39.1 0.0 collective-permute-done.own_below
  39.2 3.2 %collective-permute-start.5 = (f32[77,8,128]{2,1,0:T(8,128)S(1)}, f32[77,8,128]{2,1,0:T(8,128)S(1)}, u32[]{:S(2)}, u32[]{:S(2)}) collective-permute-start(f32[77,8,128]{2,1,0:T(8,128)S(1)} %get-tuple-element.26), channel_id=1, source_target_pairs={{0,2},{2,4},{4,6},{6,8},{8,10},{10,12},{12,14},{1,3},{3,5},{5,7},{... | collective-permute-start | bytes 946184 | tf_op jit(solution)/shard_map/ppermute | solution.py:58
  42.4 1.3 collective-permute-start.6
  43.8 0.0 copy-start.6
  43.8 0.7 copy-done.6
  44.4 3.6 %prepare.1 = (f32[4,16,48,256]{3,2,1,0:T(8,128)S(1)}, f32[4,16,48,256]{3,2,1,0:T(8,128)S(1)}, f32[16,48,256]{2,1,0:T(8,128)S(1)}, f32[16,48,256]{2,1,0:T(8,128)S...) custom-call(s32[1]{0:T(128)} %bitcast.side, ...), custom_call_target="tpu_custom_call" | custom-call | tf_op jit(solution)/shard_map/prepare/pallas_call | solution.py:33
  48.0 0.0 collective-permute-done.5.below
  48.0 2.1 %collective-permute-done.6.above = f32[77,8,128]{2,1,0:T(8,128)S(1)} collective-permute-done((f32[77,8,128]{2,1,0:T(8,128)S(1)}, f32[77,8,128]{2,1,0:T(8,128)S(1)}, u32[]{:S(2)}, u32[]{:S(2)}) %collective-permute-start.6) | collective-permute-done | bytes 315424 | tf_op jit(solution)/shard_map/ppermute | solution.py:58
  50.1 22.2 %steps.1 = (f32[4,8,32,128]{3,2,1,0:T(8,128)S(1)}, f32[4,8,32,128]{3,2,1,0:T(8,128)S(1)}, f32[24,32,128]{2,1,0:T(8,128)S(1)}, f32[4,16,48,256]{3,2,1,0:T(8,128)S...) custom-call(s32[1]{0:T(128)} %bitcast.side, ...), custom_call_target="tpu_custom_call", output_to_operand_aliasing={{3}: (7, {}), {4}: (8, {}), {5}: (9, {}), {6}: (10, {}), {7... | custom-call | tf_op jit(solution)/shard_map/steps/pallas_call | solution.py:33
  72.4 32.1 %collective-permute-start.7 = (f32[4,8,32,128]{3,2,1,0:T(8,128)S(1)}, f32[4,8,32,128]{3,2,1,0:T(8,128)S(1)}, u32[]{:S(2)}, u32[]{:S(2)}) collective-permute-start(f32[4,8,32,128]{3,2,1,0:T(8,128)S(1)} %get-tuple-element.38), channel_id=1, source_target_pairs={{0,1},{1,0},{2,3},{3,2},{4,5},{5,4},{6,7},{7,6},{8,9},{9,8},{10,11... | collective-permute-start | bytes 1572872 | tf_op jit(solution)/shard_map/ppermute | solution.py:58
  104.5 2.4 %regions.1 = f32[512,128]{1,0:T(8,128)S(1)} custom-call(s32[1]{0:T(128)} %bitcast.side, f32[24,32,128]{2,1,0:T(8,128)S(1)} %get-tuple-element.39.weights, s32[32,256]{1,0:T(8,128)S(1)} %copy-done.5), custom_call_target="tpu_custom_call" | custom-call | tf_op jit(solution)/shard_map/regions/pallas_call | solution.py:33
  106.9 31.8 %all_to_all.9 = f32[512,1,128]{2,1,0:T(1,128)S(1)} all-to-all(f32[512,1,128]{2,1,0:T(1,128)S(1)} %bitcast.5), channel_id=1, replica_groups=mesh['lon'=32,'lat'=8,'lev'=2] {'lon','lat','lev'}, dimensions={0} | all-to-all | bytes 524288 | tf_op jit(solution)/shard_map/all_to_all | solution.py:494
  138.7 0.6 reduce_sum.9
  139.2 0.7 reshape.13
  139.9 0.0 collective-permute-done.7.received
  139.9 1.0 join.1
  (15 shorter events, 0.1 us)
Async XLA Ops:
  0.6 43.1 %copy-start.3 = (bf16[8,32,256]{2,1,0:T(8,128)(2,1)S(1)}, bf16[8,32,256]{2,1,0:T(8,128)(2,1)}, u32[]{:S(2)}) copy-start(bf16[8,32,256]{2,1,0:T(8,128)(2,1)} %mixing.3) | copy-start | bytes 393220
  0.6 43.1 %copy-start.2 = (bf16[8,32,256]{2,1,0:T(8,128)(2,1)S(1)}, bf16[8,32,256]{2,1,0:T(8,128)(2,1)}, u32[]{:S(2)}) copy-start(bf16[8,32,256]{2,1,0:T(8,128)(2,1)} %lat_wind.3) | copy-start | bytes 393220
  0.7 43.1 %copy-start.1 = (bf16[8,32,256]{2,1,0:T(8,128)(2,1)S(1)}, bf16[8,32,256]{2,1,0:T(8,128)(2,1)}, u32[]{:S(2)}) copy-start(bf16[8,32,256]{2,1,0:T(8,128)(2,1)} %lon_wind.3) | copy-start | bytes 393220
  0.7 43.1 %copy-start = (f32[4,8,32,256]{3,2,1,0:T(8,128)S(1)}, f32[4,8,32,256]{3,2,1,0:T(8,128)}, u32[]{:S(2)}) copy-start(f32[4,8,32,256]{3,2,1,0:T(8,128)} %adjoint.3) | copy-start | bytes 3145732
  0.7 49.4 %copy-start.4 = (bf16[4,32,256]{2,1,0:T(8,128)(2,1)S(1)}, bf16[4,32,256]{2,1,0:T(8,128)(2,1)}, u32[]{:S(2)}) copy-start(bf16[4,32,256]{2,1,0:T(8,128)(2,1)} %prior.1) | copy-start | bytes 196612
  3.5 35.6 %collective-permute-start.2 = (f32[61,32,128]{2,1,0:T(8,128)S(1)}, f32[61,32,128]{2,1,0:T(8,128)S(1)}, u32[]{:S(2)}, u32[]{:S(2)}) collective-permute-start(f32[61,32,128]{2,1,0:T(8,128)S(1)} %get-tuple-element.23), channel_id=1, source_target_pairs={{0,1},{1,0},{2,3},{3,2},{4,5},{5,4},{6,7},{7,6},{8,9},{9,8},{10,11... | collective-permute-start | bytes 2998280 | tf_op jit(solution)/shard_map/ppermute | solution.py:58
  15.0 24.1 %collective-permute-start = (f32[63,8,128]{2,1,0:T(8,128)S(1)}, f32[63,8,128]{2,1,0:T(8,128)S(1)}, u32[]{:S(2)}, u32[]{:S(2)}) collective-permute-start(f32[63,8,128]{2,1,0:T(8,128)S(1)} %get-tuple-element.21), channel_id=1, source_target_pairs={{0,2},{2,4},{4,6},{6,8},{8,10},{10,12},{12,14},{1,3},{3,5},{5,7},{... | collective-permute-start | bytes 774152 | tf_op jit(solution)/shard_map/ppermute | solution.py:58
  18.2 20.9 %collective-permute-start.1 = (f32[63,8,128]{2,1,0:T(8,128)S(1)}, f32[63,8,128]{2,1,0:T(8,128)S(1)}, u32[]{:S(2)}, u32[]{:S(2)}) collective-permute-start(f32[63,8,128]{2,1,0:T(8,128)S(1)} %get-tuple-element.22), channel_id=1, source_target_pairs={{2,0},{4,2},{6,4},{8,6},{10,8},{12,10},{14,12},{3,1},{5,3},{7,5},{... | collective-permute-start | bytes 774152 | tf_op jit(solution)/shard_map/ppermute | solution.py:58
  19.5 18.0 %collective-permute-start.3 = (f32[7,16,128]{2,1,0:T(8,128)S(1)}, f32[7,16,128]{2,1,0:T(8,128)S(1)}, u32[]{:S(2)}, u32[]{:S(2)}) collective-permute-start(f32[7,16,128]{2,1,0:T(8,128)S(1)} %get-tuple-element.24), channel_id=1, source_target_pairs={{0,16},{17,1},{16,32},{33,17},{32,48},{49,33},{48,64},{65,49},{64,... | collective-permute-start | bytes 172040 | tf_op jit(solution)/shard_map/ppermute | solution.py:58
  23.8 15.4 %collective-permute-start.4 = (f32[7,16,128]{2,1,0:T(8,128)S(1)}, f32[7,16,128]{2,1,0:T(8,128)S(1)}, u32[]{:S(2)}, u32[]{:S(2)}) collective-permute-start(f32[7,16,128]{2,1,0:T(8,128)S(1)} %get-tuple-element.25), channel_id=1, source_target_pairs={{1,16},{16,1},{17,32},{32,17},{33,48},{48,33},{49,64},{64,49},{65,... | collective-permute-start | bytes 172040 | tf_op jit(solution)/shard_map/ppermute | solution.py:58
  39.2 8.8 %collective-permute-start.5 = (f32[77,8,128]{2,1,0:T(8,128)S(1)}, f32[77,8,128]{2,1,0:T(8,128)S(1)}, u32[]{:S(2)}, u32[]{:S(2)}) collective-permute-start(f32[77,8,128]{2,1,0:T(8,128)S(1)} %get-tuple-element.26), channel_id=1, source_target_pairs={{0,2},{2,4},{4,6},{6,8},{8,10},{10,12},{12,14},{1,3},{3,5},{5,7},{... | collective-permute-start | bytes 946184 | tf_op jit(solution)/shard_map/ppermute | solution.py:58
  42.4 7.7 %collective-permute-start.6 = (f32[77,8,128]{2,1,0:T(8,128)S(1)}, f32[77,8,128]{2,1,0:T(8,128)S(1)}, u32[]{:S(2)}, u32[]{:S(2)}) collective-permute-start(f32[77,8,128]{2,1,0:T(8,128)S(1)} %get-tuple-element.27), channel_id=1, source_target_pairs={{2,0},{4,2},{6,4},{8,6},{10,8},{12,10},{14,12},{3,1},{5,3},{7,5},{... | collective-permute-start | bytes 946184 | tf_op jit(solution)/shard_map/ppermute | solution.py:58
  43.8 0.7 copy-start.6
  50.1 54.4 %copy-start.5 = (s32[32,256]{1,0:T(8,128)S(1)}, s32[32,256]{1,0:T(8,128)}, u32[]{:S(2)}) copy-start(s32[32,256]{1,0:T(8,128)} %ids.1) | copy-start | bytes 98308
  72.4 67.6 %collective-permute-start.7 = (f32[4,8,32,128]{3,2,1,0:T(8,128)S(1)}, f32[4,8,32,128]{3,2,1,0:T(8,128)S(1)}, u32[]{:S(2)}, u32[]{:S(2)}) collective-permute-start(f32[4,8,32,128]{3,2,1,0:T(8,128)S(1)} %get-tuple-element.38), channel_id=1, source_target_pairs={{0,1},{1,0},{2,3},{3,2},{4,5},{5,4},{6,7},{7,6},{8,9},{9,8},{10,11... | collective-permute-start | bytes 1572872 | tf_op jit(solution)/shard_map/ppermute | solution.py:58
